TPU v7x, 512 devices: a whole 4x8x8 slice. The times are simulated.
512 devices in a mesh: expert: 32 (over y, z_lo, core), tensor: 16 (over x, z_hi).
Axes of the slice: x: 4, y: 8, z: 8 (z_hi: 4, z_lo: 2; z = z_hi * 2 + z_lo), core: 2. Of those that a mesh axis runs over, the one named last changes fastest.
Arguments:
- tokens: bfloat16 [4096, 6144], P('expert', 'tensor'), may hold values from -6 to 6
- expert_ids: int32 [4096, 2], P('expert'), may hold values from 0 to 7, all different within a row; in each aligned block of 128 rows (0 to 127, 128 to 255, ...) at most 48 rows name the same one
- gate_fixed: int32 [4096, 2], P('expert'), may hold values from 4096 to 65535
- w_gate: bfloat16 [32, 1024, 6144], P('expert', None, 'tensor'), may hold values from -0.078125 to 0.078125
- w_up: bfloat16 [32, 1024, 6144], P('expert', None, 'tensor'), may hold values from -0.078125 to 0.078125
- w_down: bfloat16 [32, 1024, 6144], P('expert', None, 'tensor'), may hold values from -0.0625 to 0.0625
Outputs:
- mixed: bfloat16 [4096, 6144], P('expert', 'tensor')
Inputs may be any that keep to these rules, and one draw needn't show every extreme that they name: `expert_ids`: each row names 2 different experts. Among the 128 rows of one sequence shard (aligned blocks), no expert is named by more than 48 rows, a bound that some block reaches.
All inputs are finite; a program needn't handle non-finite values.
Results may differ from a plain program's by a relative error of at most 0.0064.
Values may be sent and summed in bfloat16 or wider, within the bound.
No kernel may reach another device: no remote copies, remote signals or barrier semaphores. Data moves between devices by JAX's collectives and lax.ppermute only.
A program may use at most 64 MiB of HBM per device.

v0:
```python
import jax
import jax.numpy as jnp
from jax import lax
from jax.sharding import PartitionSpec as P

EXPERTS = 4
CAP = 48


def on_device(tokens, expert_ids, gate_fixed, w_gate, w_up, w_down):
    width_part = tokens.shape[1]
    quarters = lax.axis_size("expert") // EXPERTS
    groups = lax.axis_size("tensor")
    expert_iota = jnp.arange(EXPERTS, dtype=jnp.int32)
    matched = expert_ids[:, :, None] == expert_iota
    routed = jnp.sum(matched.astype(jnp.int32), axis=1)
    weights = (
        jnp.sum(jnp.where(matched, gate_fixed[:, :, None], 0), axis=1).astype(jnp.float32) / 65536.0
    )
    position = jnp.cumsum(routed, axis=0) - routed
    slot_iota = jnp.arange(CAP, dtype=jnp.int32)
    placed = (position[:, :, None] == slot_iota) & (routed[:, :, None] > 0)
    outgoing = jnp.einsum(
        "tec,td->ecd", placed.astype(jnp.bfloat16), tokens, preferred_element_type=jnp.float32
    ).astype(jnp.bfloat16)
    outgoing = jnp.tile(outgoing, (quarters, 1, 1))
    arrived = lax.all_to_all(outgoing, "expert", split_axis=0, concat_axis=0, tiled=True)
    sources = arrived.shape[0]
    total_rows = sources * CAP
    rows_in = arrived.reshape(total_rows, width_part)
    gate_local = w_gate[0]
    up_local = w_up[0]
    down_local = w_down[0]
    hidden_width = gate_local.shape[0]
    contract = (((1,), (1,)), ((), ()))
    gate_term = lax.dot_general(
        rows_in, gate_local, contract, preferred_element_type=jnp.float32
    ).astype(jnp.bfloat16)
    up_term = lax.dot_general(
        rows_in, up_local, contract, preferred_element_type=jnp.float32
    ).astype(jnp.bfloat16)
    gate_parts, up_parts = (
        lax.all_to_all(gate_term, "tensor", split_axis=0, concat_axis=0, tiled=True),
        lax.all_to_all(up_term, "tensor", split_axis=0, concat_axis=0, tiled=True),
    )
    row_share = total_rows // groups
    gate_share = jnp.sum(
        gate_parts.reshape(groups, row_share, hidden_width).astype(jnp.float32), axis=0
    )
    up_share = jnp.sum(
        up_parts.reshape(groups, row_share, hidden_width).astype(jnp.float32), axis=0
    )
    hidden = (jax.nn.silu(gate_share) * up_share).astype(jnp.bfloat16)
    partial_out = jnp.dot(
        lax.all_gather(hidden, "tensor", axis=0, tiled=True),
        down_local,
        preferred_element_type=jnp.float32,
    )
    returned = lax.all_to_all(
        partial_out.reshape(sources, CAP, width_part),
        "expert",
        split_axis=0,
        concat_axis=0,
        tiled=True,
    )
    summed = jnp.sum(returned.reshape(quarters, EXPERTS, CAP, width_part), axis=0)
    selector = placed.astype(jnp.float32) * weights[:, :, None]
    mixed = jnp.einsum("tec,ecd->td", selector, summed, precision=lax.Precision.HIGHEST)
    return mixed.astype(jnp.bfloat16)


def solution(mesh):
    placed = (
        P("expert", "tensor"),
        P("expert", None),
        P("expert", None),
        P("expert", None, "tensor"),
        P("expert", None, "tensor"),
        P("expert", None, "tensor"),
    )
    return jax.shard_map(
        on_device, mesh=mesh, in_specs=placed, out_specs=P("expert", "tensor"), check_vma=False
    )
```

profile of v0, /device:TPU:1, one launch (start us, length us, event | category | flops | bytes accessed | tf_op | source)
XLA Modules:
  0.0 371.3 jit_solution(15921568439732790219)
XLA Ops:
  6.5 0.0 copy-start
  6.5 0.8 select_reduce_fusion
  7.3 0.1 copy.11
  7.4 0.2 reduce_window_sum.11
  7.6 0.1 copy.13
  7.7 1.1 convolution_convert_fusion.2
  8.8 0.1 tile.4
  8.9 41.6 %all_to_all.28 = bf16[32,48,384]{2,1,0:T(8,128)(2,1)S(1)} all-to-all(bf16[32,48,384]{2,1,0:T(8,128)(2,1)S(1)} %bitcast.28), channel_id=1, replica_groups=mesh['expert'=32,'tensor'=16] {'expert'}, dimensions={0} | all-to-all | bytes 2359296 | tf_op jit(solution)/shard_map/all_to_all | solution.py:27
  50.5 0.0 copy-done
  50.5 3.5 convolution_convert_fusion
  54.1 0.0 copy-start.1
  54.1 11.9 %all-to-all-start.2 = ((bf16[16,96,1024]{2,1,0:T(8,128)(2,1)}), bf16[16,96,1024]{2,1,0:T(8,128)(2,1)}, u32[]{:S(2)}, u32[]{:S(2)}) async-start(bf16[16,96,1024]{2,1,0:T(8,128)(2,1)} %bitcast.30), calls=%async_computation.2 | async-start | bytes 6291456 | tf_op jit(solution)/shard_map/all_to_all | solution.py:44
  66.0 0.0 copy-done.1
  66.0 3.5 convolution_convert_fusion.1
  69.5 58.6 %all-to-all-done.2 = bf16[16,96,1024]{2,1,0:T(8,128)(2,1)} async-done(((bf16[16,96,1024]{2,1,0:T(8,128)(2,1)}), bf16[16,96,1024]{2,1,0:T(8,128)(2,1)}, u32[]{:S(2)}, u32[]{:S(2)}) %all-to-all-start.2) | async-done | bytes 3145760 | tf_op jit(solution)/shard_map/all_to_all | solution.py:44
  128.1 16.4 %all-to-all-start.1 = ((bf16[16,96,1024]{2,1,0:T(8,128)(2,1)}), bf16[16,96,1024]{2,1,0:T(8,128)(2,1)}, u32[]{:S(2)}, u32[]{:S(2)}) async-start(bf16[16,96,1024]{2,1,0:T(8,128)(2,1)} %bitcast.29), calls=%async_computation.1 | async-start | bytes 6291456 | tf_op jit(solution)/shard_map/all_to_all | solution.py:43
  144.5 0.0 all-gather.2.cloned.1.call-start
  144.6 2.6 convert_reduce_fusion
  147.2 0.0 copy-start.2
  147.2 54.5 %all-to-all-done.1 = bf16[16,96,1024]{2,1,0:T(8,128)(2,1)} async-done(((bf16[16,96,1024]{2,1,0:T(8,128)(2,1)}), bf16[16,96,1024]{2,1,0:T(8,128)(2,1)}, u32[]{:S(2)}, u32[]{:S(2)}) %all-to-all-start.1) | async-done | bytes 3145760 | tf_op jit(solution)/shard_map/all_to_all | solution.py:43
  201.6 2.6 convert_reduce_fusion.1
  204.2 0.8 multiply_convert_fusion
  205.0 0.0 all-gather.2.cloned.1.call-update
  205.0 89.8 %all-gather.2.cloned.1.call-done = bf16[1536,1024]{1,0:T(8,128)(2,1)} async-done(((bf16[96,1024]{1,0:T(8,128)(2,1)}), bf16[1536,1024]{1,0:T(8,128)(2,1)}) %all-gather.2.cloned.1.call-update) | async-done | bytes 3145744 | tf_op jit(solution)/shard_map/all_gather | solution.py:55
  294.8 0.0 copy-done.2
  294.8 5.1 %fusion.1 = f32[32,48,384]{2,1,0:T(8,128)} fusion(bf16[32,48,1024]{2,1,0:T(8,128)(2,1)} %bitcast.33, bf16[1,1024,384]{2,1,0:T(8,128)(2,1)S(1)} %copy-done.2), kind=kOutput, calls=%fused_computation.7 | convolution fusion | flops 1207959552 | bytes 6291456 | tf_op jit(solution)/shard_map/dot_general | solution.py:54
  300.0 7.8 %all-to-all-start.3 = ((f32[32,48,384]{2,1,0:T(8,128)}), f32[32,48,384]{2,1,0:T(8,128)S(1)}, u32[]{:S(2)}, u32[]{:S(2)}) async-start(f32[32,48,384]{2,1,0:T(8,128)} %fusion.1), calls=%async_computation.3 | async-start | bytes 4718592 | tf_op jit(solution)/shard_map/all_to_all | solution.py:59
  307.8 55.5 %all-to-all-done.3 = f32[32,48,384]{2,1,0:T(8,128)S(1)} async-done(((f32[32,48,384]{2,1,0:T(8,128)}), f32[32,48,384]{2,1,0:T(8,128)S(1)}, u32[]{:S(2)}, u32[]{:S(2)}) %all-to-all-start.3) | async-done | bytes 2359328 | tf_op jit(solution)/shard_map/all_to_all | solution.py:59
  363.3 0.1 reduce_sum.49
  363.4 1.1 fusion
  (3 shorter events, 0.0 us)
Async XLA Ops:
  6.5 44.0 %copy-start = (bf16[1,1024,384]{2,1,0:T(8,128)(2,1)S(1)}, bf16[1,1024,384]{2,1,0:T(8,128)(2,1)}, u32[]{:S(2)}) copy-start(bf16[1,1024,384]{2,1,0:T(8,128)(2,1)} %param.10) | copy-start | bytes 2359300
  54.1 11.9 %copy-start.1 = (bf16[1,1024,384]{2,1,0:T(8,128)(2,1)S(1)}, bf16[1,1024,384]{2,1,0:T(8,128)(2,1)}, u32[]{:S(2)}) copy-start(bf16[1,1024,384]{2,1,0:T(8,128)(2,1)} %param.9) | copy-start | bytes 2359300
  54.1 74.1 %all-to-all-start.2 = ((bf16[16,96,1024]{2,1,0:T(8,128)(2,1)}), bf16[16,96,1024]{2,1,0:T(8,128)(2,1)}, u32[]{:S(2)}, u32[]{:S(2)}) async-start(bf16[16,96,1024]{2,1,0:T(8,128)(2,1)} %bitcast.30), calls=%async_computation.2 | async-start | bytes 6291456 | tf_op jit(solution)/shard_map/all_to_all | solution.py:44
  128.1 73.5 %all-to-all-start.1 = ((bf16[16,96,1024]{2,1,0:T(8,128)(2,1)}), bf16[16,96,1024]{2,1,0:T(8,128)(2,1)}, u32[]{:S(2)}, u32[]{:S(2)}) async-start(bf16[16,96,1024]{2,1,0:T(8,128)(2,1)} %bitcast.29), calls=%async_computation.1 | async-start | bytes 6291456 | tf_op jit(solution)/shard_map/all_to_all | solution.py:43
  144.5 150.3 %all-gather.2.cloned.1.call-start = ((), (), s32[]{:S(2)}) async-start(), calls=%async_computation.4 | async-start | bytes 3342336 | tf_op jit(solution)/shard_map/all_gather | solution.py:55
  147.2 147.7 %copy-start.2 = (bf16[1,1024,384]{2,1,0:T(8,128)(2,1)S(1)}, bf16[1,1024,384]{2,1,0:T(8,128)(2,1)}, u32[]{:S(2)}) copy-start(bf16[1,1024,384]{2,1,0:T(8,128)(2,1)} %param.11) | copy-start | bytes 2359300
  300.0 63.3 %all-to-all-start.3 = ((f32[32,48,384]{2,1,0:T(8,128)}), f32[32,48,384]{2,1,0:T(8,128)S(1)}, u32[]{:S(2)}, u32[]{:S(2)}) async-start(f32[32,48,384]{2,1,0:T(8,128)} %fusion.1), calls=%async_computation.3 | async-start | bytes 4718592 | tf_op jit(solution)/shard_map/all_to_all | solution.py:59
Sparse Core Ops, SparseCore 0:
  205.2 89.6 all-gather.1
where the time goes:
time: 372 us; the launch traced here: 371 us
  waiting for transfers between devices  258 us (69%)
  blocking collectives  41.6 us (11%)
  starting transfers between devices  36.1 us (10%)
  matrix products  14.4 us (4%)
  between operations  13.5 us (4%)
  other arithmetic  7.05 us (2%)
    all_gather x1, waiting for transfers between devices, on_device(): lax.all_gather(hidden, 'tensor', axis=0, tiled=True)  89.8 us
    all_to_all x1, waiting for transfers between devices, on_device(): lax.all_to_all(up_term, 'tensor', split_axis=0, concat_axis=0, tiled=True)  58.6 us
    all_to_all x1, waiting for transfers between devices, on_device(): lax.all_to_all(partial_out.reshape(sources, CAP, width_part), 'expert', s...  55.5 us
    all_to_all x1, waiting for transfers between devices, on_device(): lax.all_to_all(gate_term, 'tensor', split_axis=0, concat_axis=0, tiled=True)  54.5 us
    all_to_all x1, blocking collectives, on_device(): lax.all_to_all(outgoing, 'expert', split_axis=0, concat_axis=0, tiled=True)  41.6 us
    all_to_all x1, starting transfers between devices, on_device(): lax.all_to_all(gate_term, 'tensor', split_axis=0, concat_axis=0, tiled=True)  16.4 us
    all_to_all x1, starting transfers between devices, on_device(): lax.all_to_all(up_term, 'tensor', split_axis=0, concat_axis=0, tiled=True)  11.9 us
    all_to_all x1, starting transfers between devices, on_device(): lax.all_to_all(partial_out.reshape(sources, CAP, width_part), 'expert', s...  7.78 us
  transfers between devices with their start and end apart: 4, of which 4 were waited for; matrix products, arithmetic and copies ran while one was open for 2% of the time, Pallas kernels for 0%

commit v1 on v0

v1 whole, which is shorter than its diff:
```python
import jax
import jax.numpy as jnp
from jax import lax
from jax.sharding import Mesh
from jax.sharding import PartitionSpec as P

EXPERTS = 4
CAP = 48
LOCAL = ("zl", "core")


def shift(array, axis, step):
    size = lax.axis_size(axis)
    return lax.ppermute(array, axis, [(i, (i + step) % size) for i in range(size)])


def spread(weight):
    return (weight, shift(weight, "x", -1), shift(weight, "x", 2), shift(weight, "x", 1))


def on_device(tokens, expert_ids, gate_fixed, w_gate, w_up, w_down):
    width_part = tokens.shape[1]
    x_size = lax.axis_size("x")
    y_size = lax.axis_size("y")
    zh_size = lax.axis_size("zh")
    x_own = lax.axis_index("x")
    shard_own = lax.axis_index(LOCAL)
    expert_iota = jnp.arange(EXPERTS, dtype=jnp.int32)
    matched = expert_ids[:, :, None] == expert_iota
    routed = jnp.sum(matched.astype(jnp.int32), axis=1)
    weights = (
        jnp.sum(jnp.where(matched, gate_fixed[:, :, None], 0), axis=1).astype(jnp.float32) / 65536.0
    )
    position = jnp.cumsum(routed, axis=0) - routed
    slot_iota = jnp.arange(CAP, dtype=jnp.int32)
    placed = (position[:, :, None] == slot_iota) & (routed[:, :, None] > 0)
    outgoing = jnp.einsum(
        "tec,td->ecd", placed.astype(jnp.bfloat16), tokens, preferred_element_type=jnp.float32
    ).astype(jnp.bfloat16)
    outgoing, gate_own = lax.optimization_barrier((outgoing, w_gate[0]))
    gate_all = spread(gate_own)
    sent = jnp.broadcast_to(outgoing[:, None], (EXPERTS, x_size, CAP, width_part))
    local = lax.all_to_all(
        sent.reshape(EXPERTS * x_size, CAP, width_part),
        LOCAL + ("x",),
        split_axis=0,
        concat_axis=0,
        tiled=True,
    ).reshape(EXPERTS, x_size, CAP, width_part)
    mine = lax.dynamic_index_in_dim(local, x_own, 0, keepdims=False)
    order = [(x_own + step) % x_size for step in range(x_size)]
    mine = jnp.stack([lax.dynamic_index_in_dim(mine, place, 0, keepdims=False) for place in order])
    sent_y = jnp.broadcast_to(mine[None], (y_size, x_size, CAP, width_part))
    rows = lax.all_to_all(sent_y, "y", split_axis=0, concat_axis=0, tiled=True)
    total_rows = y_size * CAP
    rows = [rows[:, step].reshape(total_rows, width_part) for step in range(x_size)]
    contract = (((1,), (1,)), ((), ()))

    def project(blocks):
        total = None
        for row_block, block in zip(rows, blocks):
            term = lax.dot_general(row_block, block, contract, preferred_element_type=jnp.float32)
            total = term if total is None else total + term
        return total.astype(jnp.bfloat16)

    def share(term):
        parts = lax.all_to_all(term, "zh", split_axis=0, concat_axis=0, tiled=True)
        parts = parts.reshape(zh_size, total_rows // zh_size, -1)
        return jnp.sum(parts.astype(jnp.float32), axis=0)

    gate_term = project(gate_all)
    up_own, _ = lax.optimization_barrier((w_up[0], gate_all[2]))
    up_all = spread(up_own)
    gate_share = share(gate_term)
    up_term = project(up_all)
    down_own, _ = lax.optimization_barrier((w_down[0], up_all[2]))
    down_all = spread(down_own)
    up_share = share(up_term)
    hidden = (jax.nn.silu(gate_share) * up_share).astype(jnp.bfloat16)
    hidden_rows = lax.all_to_all(
        jnp.broadcast_to(hidden[None], (zh_size,) + hidden.shape),
        "zh",
        split_axis=0,
        concat_axis=0,
        tiled=True,
    ).reshape(total_rows, -1)
    outs = [
        jnp.dot(hidden_rows, block, preferred_element_type=jnp.float32)
        .astype(jnp.bfloat16)
        .reshape(y_size, CAP, width_part)
        for block in down_all
    ]
    back = lax.all_to_all(jnp.stack(outs, axis=1), "y", split_axis=0, concat_axis=0, tiled=True)
    back = jnp.sum(back.astype(jnp.float32), axis=0).astype(jnp.bfloat16)
    back = jnp.stack(
        [
            lax.dynamic_index_in_dim(back, (place - x_own) % x_size, 0, keepdims=False)
            for place in range(x_size)
        ]
    )
    back = jnp.broadcast_to(back[None], (EXPERTS, x_size, CAP, width_part))
    final = lax.all_to_all(
        back.reshape(EXPERTS * x_size, CAP, width_part),
        LOCAL + ("x",),
        split_axis=0,
        concat_axis=0,
        tiled=True,
    ).reshape(EXPERTS, x_size, CAP, width_part)
    summed = lax.dynamic_index_in_dim(final, shard_own, 1, keepdims=False).astype(jnp.float32)
    selector = placed.astype(jnp.float32) * weights[:, :, None]
    mixed = jnp.einsum("tec,ecd->td", selector, summed, precision=lax.Precision.HIGHEST)
    return mixed.astype(jnp.bfloat16)


def solution(mesh):
    expert, tensor = mesh.devices.shape
    fine = Mesh(
        mesh.devices.reshape(expert // 4, 2, 2, 4, tensor // 4), ("y", "zl", "core", "x", "zh")
    )
    rows, cols = ("y", "zl", "core"), ("x", "zh")
    placed = (
        P(rows, cols),
        P(rows, None),
        P(rows, None),
        P(rows, None, cols),
        P(rows, None, cols),
        P(rows, None, cols),
    )
    return jax.shard_map(
        on_device, mesh=fine, in_specs=placed, out_specs=P(rows, cols), check_vma=False
    )
```

time: 372 us -> 241 us (0.65)
  waiting for transfers between devices: 258 us -> 139 us
  blocking collectives: 41.6 us -> 0 us
  starting transfers between devices: 36.1 us -> 75 us
  between operations: 13.5 us -> 0.27 us
  other arithmetic: 7.05 us -> 2.74 us
  local copies, waits for them, and re-layouts: 0.3 us -> 4.22 us
    all_gather x1 -> x0, waiting for transfers between devices: 89.8 us -> none  [on_device(): lax.all_gather(hidden, 'tensor', axis=0, tiled=True)]
    all_to_all x3 -> x7, waiting for transfers between devices: 169 us -> 83.8 us  [the longest x1 32 us: on_device(): lax.all_to_all(jnp.stack(outs, axis=1), 'y', split_axis=0, concat_axis=0,...]
    ppermute x0 -> x9, waiting for transfers between devices: none -> 55.5 us  [shift(): lax.ppermute(array, axis, [(i, (i + step) % size) for i in range(size)])]
    all_to_all x1 -> x0, blocking collectives: 41.6 us -> none  [on_device(): lax.all_to_all(outgoing, 'expert', split_axis=0, concat_axis=0, tiled=True)]
    ppermute x0 -> x9, starting transfers between devices: none -> 26.3 us  [shift(): lax.ppermute(array, axis, [(i, (i + step) % size) for i in range(size)])]
    all_to_all x3 -> x7, starting transfers between devices: 36 us -> 48.7 us  [the longest x2 18.2 us: share(): parts = lax.all_to_all(term, 'zh', split_axis=0, concat_axis=0, tiled=True)]
    reduce_sum x3, other arithmetic: 5.27 us -> 0.43 us  [the longest x2 0.26 us: share(): return jnp.sum(parts.astype(jnp.float32), axis=0)]
    dot_general x3 -> x12, matrix products: 12.2 us -> 16.9 us  [the longest x8 13.5 us: project(): lax.dot_general(row_block, block, contract, preferred_element_type=jnp.fl...]
  transfers between devices with their start and end apart: 4 -> 16, of which waited for: 4 -> 13; matrix products, arithmetic and copies ran while one was open for 2% -> 7% of each run, Pallas kernels for 0% -> 0%
where the time goes in v1:
time: 241 us; the launch traced here: 240 us
  waiting for transfers between devices  139 us (58%)
  starting transfers between devices  75 us (31%)
  matrix products  18.1 us (8%)
  local copies, waits for them, and re-layouts  4.22 us (2%)
  other arithmetic  2.74 us (1%)
    ppermute x9, waiting for transfers between devices, shift(): lax.ppermute(array, axis, [(i, (i + step) % size) for i in range(size)])  55.5 us
    all_to_all x1, waiting for transfers between devices, on_device(): lax.all_to_all(jnp.stack(outs, axis=1), 'y', split_axis=0, concat_axis=0,...  32 us
    ppermute x9, starting transfers between devices, shift(): lax.ppermute(array, axis, [(i, (i + step) % size) for i in range(size)])  26.3 us
    all_to_all x2, starting transfers between devices, share(): parts = lax.all_to_all(term, 'zh', split_axis=0, concat_axis=0, tiled=True)  18.2 us
    all_to_all x2, waiting for transfers between devices, share(): parts = lax.all_to_all(term, 'zh', split_axis=0, concat_axis=0, tiled=True)  17.9 us
    dot_general x8, matrix products, project(): lax.dot_general(row_block, block, contract, preferred_element_type=jnp.fl...  13.5 us
    all_to_all x1, waiting for transfers between devices, on_device(): lax.all_to_all(sent.reshape(EXPERTS * x_size, CAP, width_part), LOCAL + (...  10.9 us
    all_to_all x1, waiting for transfers between devices, on_device(): lax.all_to_all(back.reshape(EXPERTS * x_size, CAP, width_part), LOCAL + (...  10.8 us
  transfers between devices with their start and end apart: 16, of which 13 were waited for; matrix products, arithmetic and copies ran while one was open for 7% of the time, Pallas kernels for 0%

profile of v1, /device:TPU:1, one launch (start us, length us, event | category | flops | bytes accessed | tf_op | source)
XLA Modules:
  0.0 239.6 jit_solution(6732339400470105583)
XLA Ops:
  2.2 10.2 %all-to-all-start = ((bf16[16,48,384]{2,1,0:T(8,128)(2,1)}), bf16[16,48,384]{2,1,0:T(8,128)(2,1)S(1)}, u32[]{:S(2)}, u32[]{:S(2)}) async-start(bf16[16,48,384]{2,1,0:T(8,128)(2,1)} %bitcast.2), calls=%async_computation | async-start | bytes 1179648 | tf_op jit(solution)/shard_map/all_to_all | solution.py:43
  12.4 10.9 %all-to-all-done = bf16[16,48,384]{2,1,0:T(8,128)(2,1)S(1)} async-done(((bf16[16,48,384]{2,1,0:T(8,128)(2,1)}), bf16[16,48,384]{2,1,0:T(8,128)(2,1)S(1)}, u32[]{:S(2)}, u32[]{:S(2)}) %all-to-all-start) | async-done | bytes 589856 | tf_op jit(solution)/shard_map/all_to_all | solution.py:43
  24.5 4.1 %all-to-all-start.1 = ((bf16[8,4,48,384]{3,2,1,0:T(8,128)(2,1)}), bf16[8,4,48,384]{3,2,1,0:T(8,128)(2,1)S(1)}, u32[]{:S(2)}, u32[]{:S(2)}) async-start(bf16[8,4,48,384]{3,2,1,0:T(8,128)(2,1)} %broadcast_in_dim.23), calls=%async_computation.1 | async-start | bytes 2359296 | tf_op jit(solution)/shard_map/all_to_all | solution.py:54
  28.7 3.2 %collective-permute-start.1 = (bf16[1024,384]{1,0:T(8,128)(2,1)}, bf16[1024,384]{1,0:T(8,128)(2,1)S(1)}, u32[]{:S(2)}, u32[]{:S(2)}) collective-permute-start(bf16[1024,384]{1,0:T(8,128)(2,1)} %bitcast.1), channel_id=1, source_target_pairs={{0,8},{4,12},{8,0},{12,4},{1,9},{5,13},{9,1},{13,5},{2,10},{6,14},... | collective-permute-start | bytes 2359304 | tf_op jit(solution)/shard_map/ppermute | solution.py:14
  31.9 3.0 %collective-permute-start = (bf16[1024,384]{1,0:T(8,128)(2,1)}, bf16[1024,384]{1,0:T(8,128)(2,1)}, u32[]{:S(2)}, u32[]{:S(2)}) collective-permute-start(bf16[1024,384]{1,0:T(8,128)(2,1)} %bitcast.1), channel_id=1, source_target_pairs={{0,12},{4,0},{8,4},{12,8},{1,13},{5,1},{9,5},{13,9},{2,14},{6,2},{... | collective-permute-start | bytes 2359304 | tf_op jit(solution)/shard_map/ppermute | solution.py:14
  34.9 2.3 collective-permute-start.2
  37.2 13.4 %collective-permute-done.1 = bf16[1024,384]{1,0:T(8,128)(2,1)S(1)} collective-permute-done((bf16[1024,384]{1,0:T(8,128)(2,1)}, bf16[1024,384]{1,0:T(8,128)(2,1)S(1)}, u32[]{:S(2)}, u32[]{:S(2)}) %collective-permute-start.1) | collective-permute-done | bytes 786464 | tf_op jit(solution)/shard_map/ppermute | solution.py:14
  50.6 3.1 %collective-permute-start.3 = (bf16[1024,384]{1,0:T(8,128)(2,1)}, bf16[1024,384]{1,0:T(8,128)(2,1)}, u32[]{:S(2)}, u32[]{:S(2)}) collective-permute-start(bf16[1024,384]{1,0:T(8,128)(2,1)} %bitcast.13), channel_id=1, source_target_pairs={{0,12},{4,0},{8,4},{12,8},{1,13},{5,1},{9,5},{13,9},{2,14},{6,2},{... | collective-permute-start | bytes 2359304 | tf_op jit(solution)/shard_map/ppermute | solution.py:14
  53.7 2.8 %collective-permute-start.4 = (bf16[1024,384]{1,0:T(8,128)(2,1)}, bf16[1024,384]{1,0:T(8,128)(2,1)}, u32[]{:S(2)}, u32[]{:S(2)}) collective-permute-start(bf16[1024,384]{1,0:T(8,128)(2,1)} %bitcast.13), channel_id=1, source_target_pairs={{0,8},{4,12},{8,0},{12,4},{1,9},{5,13},{9,1},{13,5},{2,10},{6,14},... | collective-permute-start | bytes 2359304 | tf_op jit(solution)/shard_map/ppermute | solution.py:14
  56.6 2.8 %collective-permute-start.5 = (bf16[1024,384]{1,0:T(8,128)(2,1)}, bf16[1024,384]{1,0:T(8,128)(2,1)S(1)}, u32[]{:S(2)}, u32[]{:S(2)}) collective-permute-start(bf16[1024,384]{1,0:T(8,128)(2,1)} %bitcast.13), channel_id=1, source_target_pairs={{0,4},{4,8},{8,12},{12,0},{1,5},{5,9},{9,13},{13,1},{2,6},{6,10},{... | collective-permute-start | bytes 2359304 | tf_op jit(solution)/shard_map/ppermute | solution.py:14
  60.8 1.8 fusion.17
  63.3 3.1 %collective-permute-done = bf16[1024,384]{1,0:T(8,128)(2,1)} collective-permute-done((bf16[1024,384]{1,0:T(8,128)(2,1)}, bf16[1024,384]{1,0:T(8,128)(2,1)}, u32[]{:S(2)}, u32[]{:S(2)}) %collective-permute-start) | collective-permute-done | bytes 786464 | tf_op jit(solution)/shard_map/ppermute | solution.py:14
  66.4 1.7 fusion.18
  69.8 2.7 %add_convert_fusion.1 = bf16[384,1024]{1,0:T(8,128)(2,1)} fusion(f32[384,1024]{1,0:T(8,128)S(1)} %fusion.19, f32[384,1024]{1,0:T(8,128)S(1)} %fusion.17, f32[384,1024]{1,0:T(8,128)S(1)} %fusion.18, bf16[384,384]{1,0:T(8,128)(2,1)S(1)} %bitcast.68, bf16[1024,384]{1,0:T(8,128)(2,1)} %collective-permute-done.2), kind=kOutput, calls=%fused_computation.3 | convolution fusion | flops 303562752 | bytes 6586368 | tf_op jit(solution)/shard_map/dot_general | solution.py:62
  72.5 9.1 %all-to-all-start.2 = ((bf16[4,96,1024]{2,1,0:T(8,128)(2,1)}), bf16[4,96,1024]{2,1,0:T(8,128)(2,1)S(1)}, u32[]{:S(2)}, u32[]{:S(2)}) async-start(bf16[4,96,1024]{2,1,0:T(8,128)(2,1)} %bitcast.12), calls=%async_computation.2 | async-start | bytes 1572864 | tf_op jit(solution)/shard_map/all_to_all | solution.py:67
  81.6 1.7 fusion.20
  83.3 1.7 fusion.21
  85.1 1.7 fusion.22
  86.8 15.5 %collective-permute-done.5 = bf16[1024,384]{1,0:T(8,128)(2,1)S(1)} collective-permute-done((bf16[1024,384]{1,0:T(8,128)(2,1)}, bf16[1024,384]{1,0:T(8,128)(2,1)S(1)}, u32[]{:S(2)}, u32[]{:S(2)}) %collective-permute-start.5) | collective-permute-done | bytes 786464 | tf_op jit(solution)/shard_map/ppermute | solution.py:14
  103.8 9.1 %all-to-all-start.3 = ((bf16[4,96,1024]{2,1,0:T(8,128)(2,1)}), bf16[4,96,1024]{2,1,0:T(8,128)(2,1)S(1)}, u32[]{:S(2)}, u32[]{:S(2)}) async-start(bf16[4,96,1024]{2,1,0:T(8,128)(2,1)} %bitcast.14), calls=%async_computation.3 | async-start | bytes 1572864 | tf_op jit(solution)/shard_map/all_to_all | solution.py:67
  113.1 17.9 %all-to-all-done.3 = bf16[4,96,1024]{2,1,0:T(8,128)(2,1)S(1)} async-done(((bf16[4,96,1024]{2,1,0:T(8,128)(2,1)}), bf16[4,96,1024]{2,1,0:T(8,128)(2,1)S(1)}, u32[]{:S(2)}, u32[]{:S(2)}) %all-to-all-start.3) | async-done | bytes 786464 | tf_op jit(solution)/shard_map/all_to_all | solution.py:67
  132.3 5.7 %all-to-all-start.4 = ((bf16[4,96,1024]{2,1,0:T(8,128)(2,1)}), bf16[4,96,1024]{2,1,0:T(8,128)(2,1)S(1)}, u32[]{:S(2)}, u32[]{:S(2)}) async-start(bf16[4,96,1024]{2,1,0:T(8,128)(2,1)} %broadcast_in_dim.24), calls=%async_computation.4 | async-start | bytes 1572864 | tf_op jit(solution)/shard_map/all_to_all | solution.py:80
  138.0 4.7 %collective-permute-start.6 = (bf16[1024,384]{1,0:T(8,128)(2,1)S(1)}, bf16[1024,384]{1,0:T(8,128)(2,1)}, u32[]{:S(2)}, u32[]{:S(2)}) collective-permute-start(bf16[1024,384]{1,0:T(8,128)(2,1)S(1)} %bitcast.86), channel_id=1, source_target_pairs={{0,12},{4,0},{8,4},{12,8},{1,13},{5,1},{9,5},{13,9},{2,14},{6,2},{... | collective-permute-start | bytes 2359304 | tf_op jit(solution)/shard_map/ppermute | solution.py:14
  142.8 1.9 collective-permute-start.7
  144.7 2.5 %collective-permute-start.8 = (bf16[1024,384]{1,0:T(8,128)(2,1)S(1)}, bf16[1024,384]{1,0:T(8,128)(2,1)S(1)}, u32[]{:S(2)}, u32[]{:S(2)}) collective-permute-start(bf16[1024,384]{1,0:T(8,128)(2,1)S(1)} %bitcast.88), channel_id=1, source_target_pairs={{0,4},{4,8},{8,12},{12,0},{1,5},{5,9},{9,13},{13,1},{2,6},{6,10},{... | collective-permute-start | bytes 2359304 | tf_op jit(solution)/shard_map/ppermute | solution.py:14
  147.2 10.7 %all-to-all-done.4 = bf16[4,96,1024]{2,1,0:T(8,128)(2,1)S(1)} async-done(((bf16[4,96,1024]{2,1,0:T(8,128)(2,1)}), bf16[4,96,1024]{2,1,0:T(8,128)(2,1)S(1)}, u32[]{:S(2)}, u32[]{:S(2)}) %all-to-all-start.4) | async-done | bytes 786464 | tf_op jit(solution)/shard_map/all_to_all | solution.py:80
  158.4 2.7 %collective-permute-done.6 = bf16[1024,384]{1,0:T(8,128)(2,1)} collective-permute-done((bf16[1024,384]{1,0:T(8,128)(2,1)S(1)}, bf16[1024,384]{1,0:T(8,128)(2,1)}, u32[]{:S(2)}, u32[]{:S(2)}) %collective-permute-start.6) | collective-permute-done | bytes 786464 | tf_op jit(solution)/shard_map/ppermute | solution.py:14
  164.7 17.7 %collective-permute-done.8 = bf16[1024,384]{1,0:T(8,128)(2,1)S(1)} collective-permute-done((bf16[1024,384]{1,0:T(8,128)(2,1)S(1)}, bf16[1024,384]{1,0:T(8,128)(2,1)S(1)}, u32[]{:S(2)}, u32[]{:S(2)}) %collective-permute-start.8) | collective-permute-done | bytes 786464 | tf_op jit(solution)/shard_map/ppermute | solution.py:14
  184.3 6.1 %all-to-all-start.5 = ((bf16[8,4,48,384]{3,2,1,0:T(8,128)(2,1)}), bf16[8,4,48,384]{3,2,1,0:T(8,128)(2,1)S(1)}, u32[]{:S(2)}, u32[]{:S(2)}) async-start(bf16[8,4,48,384]{3,2,1,0:T(8,128)(2,1)} %pad_maximum_fusion), calls=%async_computation.5 | async-start | bytes 2359296 | tf_op jit(solution)/shard_map/all_to_all | solution.py:93
  190.3 32.0 %all-to-all-done.5 = bf16[8,4,48,384]{3,2,1,0:T(8,128)(2,1)S(1)} async-done(((bf16[8,4,48,384]{3,2,1,0:T(8,128)(2,1)}), bf16[8,4,48,384]{3,2,1,0:T(8,128)(2,1)S(1)}, u32[]{:S(2)}, u32[]{:S(2)}) %all-to-all-start.5) | async-done | bytes 1179680 | tf_op jit(solution)/shard_map/all_to_all | solution.py:93
  223.5 4.3 %all-to-all-start.6 = ((bf16[16,48,384]{2,1,0:T(8,128)(2,1)}), bf16[16,48,384]{2,1,0:T(8,128)(2,1)S(1)}, u32[]{:S(2)}, u32[]{:S(2)}) async-start(bf16[16,48,384]{2,1,0:T(8,128)(2,1)} %bitcast.25), calls=%async_computation.6 | async-start | bytes 1179648 | tf_op jit(solution)/shard_map/all_to_all | solution.py:102
  227.8 10.8 %all-to-all-done.6 = bf16[16,48,384]{2,1,0:T(8,128)(2,1)S(1)} async-done(((bf16[16,48,384]{2,1,0:T(8,128)(2,1)}), bf16[16,48,384]{2,1,0:T(8,128)(2,1)S(1)}, u32[]{:S(2)}, u32[]{:S(2)}) %all-to-all-start.6) | async-done | bytes 589856 | tf_op jit(solution)/shard_map/all_to_all | solution.py:102
  (43 shorter events, 18.0 us)
Async XLA Ops:
  0.0 1.1 copy-start
  2.2 21.1 %all-to-all-start = ((bf16[16,48,384]{2,1,0:T(8,128)(2,1)}), bf16[16,48,384]{2,1,0:T(8,128)(2,1)S(1)}, u32[]{:S(2)}, u32[]{:S(2)}) async-start(bf16[16,48,384]{2,1,0:T(8,128)(2,1)} %bitcast.2), calls=%async_computation | async-start | bytes 1179648 | tf_op jit(solution)/shard_map/all_to_all | solution.py:43
  24.5 36.2 %all-to-all-start.1 = ((bf16[8,4,48,384]{3,2,1,0:T(8,128)(2,1)}), bf16[8,4,48,384]{3,2,1,0:T(8,128)(2,1)S(1)}, u32[]{:S(2)}, u32[]{:S(2)}) async-start(bf16[8,4,48,384]{3,2,1,0:T(8,128)(2,1)} %broadcast_in_dim.23), calls=%async_computation.1 | async-start | bytes 2359296 | tf_op jit(solution)/shard_map/all_to_all | solution.py:54
  28.7 21.9 %collective-permute-start.1 = (bf16[1024,384]{1,0:T(8,128)(2,1)}, bf16[1024,384]{1,0:T(8,128)(2,1)S(1)}, u32[]{:S(2)}, u32[]{:S(2)}) collective-permute-start(bf16[1024,384]{1,0:T(8,128)(2,1)} %bitcast.1), channel_id=1, source_target_pairs={{0,8},{4,12},{8,0},{12,4},{1,9},{5,13},{9,1},{13,5},{2,10},{6,14},... | collective-permute-start | bytes 2359304 | tf_op jit(solution)/shard_map/ppermute | solution.py:14
  31.9 34.5 %collective-permute-start = (bf16[1024,384]{1,0:T(8,128)(2,1)}, bf16[1024,384]{1,0:T(8,128)(2,1)}, u32[]{:S(2)}, u32[]{:S(2)}) collective-permute-start(bf16[1024,384]{1,0:T(8,128)(2,1)} %bitcast.1), channel_id=1, source_target_pairs={{0,12},{4,0},{8,4},{12,8},{1,13},{5,1},{9,5},{13,9},{2,14},{6,2},{... | collective-permute-start | bytes 2359304 | tf_op jit(solution)/shard_map/ppermute | solution.py:14
  34.9 35.0 %collective-permute-start.2 = (bf16[1024,384]{1,0:T(8,128)(2,1)}, bf16[1024,384]{1,0:T(8,128)(2,1)}, u32[]{:S(2)}, u32[]{:S(2)}) collective-permute-start(bf16[1024,384]{1,0:T(8,128)(2,1)} %bitcast.1), channel_id=1, source_target_pairs={{0,4},{4,8},{8,12},{12,0},{1,5},{5,9},{9,13},{13,1},{2,6},{6,10},{... | collective-permute-start | bytes 2359304 | tf_op jit(solution)/shard_map/ppermute | solution.py:14
  50.6 6.0 %copy-start.1 = (bf16[1024,384]{1,0:T(8,128)(2,1)}, bf16[1024,384]{1,0:T(8,128)(2,1)S(1)}, u32[]{:S(2)}) copy-start(bf16[1024,384]{1,0:T(8,128)(2,1)S(1)} %collective-permute-done.1) | copy-start | bytes 2359300
  50.6 32.8 %collective-permute-start.3 = (bf16[1024,384]{1,0:T(8,128)(2,1)}, bf16[1024,384]{1,0:T(8,128)(2,1)}, u32[]{:S(2)}, u32[]{:S(2)}) collective-permute-start(bf16[1024,384]{1,0:T(8,128)(2,1)} %bitcast.13), channel_id=1, source_target_pairs={{0,12},{4,0},{8,4},{12,8},{1,13},{5,1},{9,5},{13,9},{2,14},{6,2},{... | collective-permute-start | bytes 2359304 | tf_op jit(solution)/shard_map/ppermute | solution.py:14
  53.7 31.4 %collective-permute-start.4 = (bf16[1024,384]{1,0:T(8,128)(2,1)}, bf16[1024,384]{1,0:T(8,128)(2,1)}, u32[]{:S(2)}, u32[]{:S(2)}) collective-permute-start(bf16[1024,384]{1,0:T(8,128)(2,1)} %bitcast.13), channel_id=1, source_target_pairs={{0,8},{4,12},{8,0},{12,4},{1,9},{5,13},{9,1},{13,5},{2,10},{6,14},... | collective-permute-start | bytes 2359304 | tf_op jit(solution)/shard_map/ppermute | solution.py:14
  56.6 45.7 %collective-permute-start.5 = (bf16[1024,384]{1,0:T(8,128)(2,1)}, bf16[1024,384]{1,0:T(8,128)(2,1)S(1)}, u32[]{:S(2)}, u32[]{:S(2)}) collective-permute-start(bf16[1024,384]{1,0:T(8,128)(2,1)} %bitcast.13), channel_id=1, source_target_pairs={{0,4},{4,8},{8,12},{12,0},{1,5},{5,9},{9,13},{13,1},{2,6},{6,10},{... | collective-permute-start | bytes 2359304 | tf_op jit(solution)/shard_map/ppermute | solution.py:14
  60.8 1.8 copy-start.2
  72.5 31.4 %all-to-all-start.2 = ((bf16[4,96,1024]{2,1,0:T(8,128)(2,1)}), bf16[4,96,1024]{2,1,0:T(8,128)(2,1)S(1)}, u32[]{:S(2)}, u32[]{:S(2)}) async-start(bf16[4,96,1024]{2,1,0:T(8,128)(2,1)} %bitcast.12), calls=%async_computation.2 | async-start | bytes 1572864 | tf_op jit(solution)/shard_map/all_to_all | solution.py:67
  103.8 27.2 %all-to-all-start.3 = ((bf16[4,96,1024]{2,1,0:T(8,128)(2,1)}), bf16[4,96,1024]{2,1,0:T(8,128)(2,1)S(1)}, u32[]{:S(2)}, u32[]{:S(2)}) async-start(bf16[4,96,1024]{2,1,0:T(8,128)(2,1)} %bitcast.14), calls=%async_computation.3 | async-start | bytes 1572864 | tf_op jit(solution)/shard_map/all_to_all | solution.py:67
  131.2 6.9 %copy-start.3 = (bf16[1,1024,384]{2,1,0:T(8,128)(2,1)S(1)}, bf16[1,1024,384]{2,1,0:T(8,128)(2,1)}, u32[]{:S(2)}) copy-start(bf16[1,1024,384]{2,1,0:T(8,128)(2,1)} %param.11) | copy-start | bytes 2359300
  132.3 25.6 %all-to-all-start.4 = ((bf16[4,96,1024]{2,1,0:T(8,128)(2,1)}), bf16[4,96,1024]{2,1,0:T(8,128)(2,1)S(1)}, u32[]{:S(2)}, u32[]{:S(2)}) async-start(bf16[4,96,1024]{2,1,0:T(8,128)(2,1)} %broadcast_in_dim.24), calls=%async_computation.4 | async-start | bytes 1572864 | tf_op jit(solution)/shard_map/all_to_all | solution.py:80
  138.0 23.2 %collective-permute-start.6 = (bf16[1024,384]{1,0:T(8,128)(2,1)S(1)}, bf16[1024,384]{1,0:T(8,128)(2,1)}, u32[]{:S(2)}, u32[]{:S(2)}) collective-permute-start(bf16[1024,384]{1,0:T(8,128)(2,1)S(1)} %bitcast.86), channel_id=1, source_target_pairs={{0,12},{4,0},{8,4},{12,8},{1,13},{5,1},{9,5},{13,9},{2,14},{6,2},{... | collective-permute-start | bytes 2359304 | tf_op jit(solution)/shard_map/ppermute | solution.py:14
  142.8 21.4 %collective-permute-start.7 = (bf16[1024,384]{1,0:T(8,128)(2,1)S(1)}, bf16[1024,384]{1,0:T(8,128)(2,1)S(1)}, u32[]{:S(2)}, u32[]{:S(2)}) collective-permute-start(bf16[1024,384]{1,0:T(8,128)(2,1)S(1)} %bitcast.87), channel_id=1, source_target_pairs={{0,8},{4,12},{8,0},{12,4},{1,9},{5,13},{9,1},{13,5},{2,10},{6,14},... | collective-permute-start | bytes 2359304 | tf_op jit(solution)/shard_map/ppermute | solution.py:14
  144.7 37.8 %collective-permute-start.8 = (bf16[1024,384]{1,0:T(8,128)(2,1)S(1)}, bf16[1024,384]{1,0:T(8,128)(2,1)S(1)}, u32[]{:S(2)}, u32[]{:S(2)}) collective-permute-start(bf16[1024,384]{1,0:T(8,128)(2,1)S(1)} %bitcast.88), channel_id=1, source_target_pairs={{0,4},{4,8},{8,12},{12,0},{1,5},{5,9},{9,13},{13,1},{2,6},{6,10},{... | collective-permute-start | bytes 2359304 | tf_op jit(solution)/shard_map/ppermute | solution.py:14
  184.3 38.1 %all-to-all-start.5 = ((bf16[8,4,48,384]{3,2,1,0:T(8,128)(2,1)}), bf16[8,4,48,384]{3,2,1,0:T(8,128)(2,1)S(1)}, u32[]{:S(2)}, u32[]{:S(2)}) async-start(bf16[8,4,48,384]{3,2,1,0:T(8,128)(2,1)} %pad_maximum_fusion), calls=%async_computation.5 | async-start | bytes 2359296 | tf_op jit(solution)/shard_map/all_to_all | solution.py:93
  223.5 15.1 %all-to-all-start.6 = ((bf16[16,48,384]{2,1,0:T(8,128)(2,1)}), bf16[16,48,384]{2,1,0:T(8,128)(2,1)S(1)}, u32[]{:S(2)}, u32[]{:S(2)}) async-start(bf16[16,48,384]{2,1,0:T(8,128)(2,1)} %bitcast.25), calls=%async_computation.6 | async-start | bytes 1179648 | tf_op jit(solution)/shard_map/all_to_all | solution.py:102

commit v2 on v1

v2 whole, which is shorter than its diff:
```python
import jax
import jax.numpy as jnp
from jax import lax
from jax.sharding import Mesh
from jax.sharding import PartitionSpec as P


EXPERTS = 4
CAP = 48
LOCAL = ("zl", "core")


def shift(array, axis, step):
    size = lax.axis_size(axis)
    return lax.ppermute(array, axis, [(i, (i + step) % size) for i in range(size)])


def spread(weight):
    after = shift(weight, "x", -1)
    before = shift(weight, "x", 1)
    across = shift(weight, "x", 2)
    return (weight, after, across, before)


def on_device(tokens, expert_ids, gate_fixed, w_gate, w_up, w_down):
    width_part = tokens.shape[1]
    x_size = lax.axis_size("x")
    y_size = lax.axis_size("y")
    zh_size = lax.axis_size("zh")
    x_own = lax.axis_index("x")
    expert_iota = jnp.arange(EXPERTS, dtype=jnp.int32)
    matched = expert_ids[:, :, None] == expert_iota
    routed = jnp.sum(matched.astype(jnp.int32), axis=1)
    weights = (
        jnp.sum(jnp.where(matched, gate_fixed[:, :, None], 0), axis=1).astype(jnp.float32) / 65536.0
    )
    position = jnp.cumsum(routed, axis=0) - routed
    slot_iota = jnp.arange(CAP, dtype=jnp.int32)
    placed = (position[:, :, None] == slot_iota) & (routed[:, :, None] > 0)
    outgoing = jnp.einsum(
        "tec,td->ecd", placed.astype(jnp.bfloat16), tokens, preferred_element_type=jnp.float32
    ).astype(jnp.bfloat16)
    gate_all = spread(w_gate[0])
    sent = jnp.broadcast_to(outgoing[:, None], (EXPERTS, x_size, CAP, width_part))
    local = lax.all_to_all(
        sent.reshape(EXPERTS * x_size, CAP, width_part),
        LOCAL + ("x",),
        split_axis=0,
        concat_axis=0,
        tiled=True,
    ).reshape(EXPERTS, x_size, CAP, width_part)
    order = [(x_own + step) % x_size for step in range(x_size)]
    mine = lax.dynamic_index_in_dim(local, x_own, 0, keepdims=False)
    mine = jnp.stack([lax.dynamic_index_in_dim(mine, place, 0, keepdims=False) for place in order])
    sent_y = jnp.broadcast_to(mine[None], (y_size, x_size, CAP, width_part))
    rows = lax.all_to_all(sent_y, "y", split_axis=0, concat_axis=0, tiled=True)
    total_rows = y_size * CAP
    rows = [rows[:, step].reshape(total_rows, width_part) for step in range(x_size)]
    contract = (((1,), (1,)), ((), ()))

    def project(blocks):
        total = None
        for row_block, block in zip(rows, blocks):
            term = lax.dot_general(row_block, block, contract, preferred_element_type=jnp.float32)
            term = lax.reduce_precision(term, 8, 7)
            total = term if total is None else total + term
        return total.astype(jnp.bfloat16)

    def share(term):
        parts = lax.all_to_all(term, "zh", split_axis=0, concat_axis=0, tiled=True)
        parts = parts.reshape(zh_size, total_rows // zh_size, -1)
        return jnp.sum(parts.astype(jnp.float32), axis=0)

    gate_term = project(gate_all)
    up_own, gate_all = lax.optimization_barrier((w_up[0], gate_all))
    up_all = spread(up_own)
    gate_share = share(gate_term)
    up_term = project(up_all)
    down_own, up_all = lax.optimization_barrier((w_down[0], up_all))
    down_all = spread(down_own)
    up_share = share(up_term)
    hidden = (jax.nn.silu(gate_share) * up_share).astype(jnp.bfloat16)
    hidden_rows = lax.all_to_all(
        jnp.broadcast_to(hidden[None], (zh_size,) + hidden.shape),
        "zh",
        split_axis=0,
        concat_axis=0,
        tiled=True,
    ).reshape(total_rows, -1)
    back = jnp.zeros((y_size, x_size, CAP, width_part), jnp.bfloat16)
    for step, block in enumerate(down_all):
        out = jnp.dot(hidden_rows, block, preferred_element_type=jnp.float32).astype(jnp.bfloat16)
        out = out.reshape(y_size, 1, CAP, width_part)
        back = lax.dynamic_update_slice(back, out, (0, order[step], 0, 0))
    back = lax.all_to_all(
        back.reshape(y_size * x_size, CAP, width_part),
        ("y", "x"),
        split_axis=0,
        concat_axis=0,
        tiled=True,
    ).reshape(y_size, x_size, CAP, width_part)
    back = jnp.sum(back.astype(jnp.float32), axis=0).astype(jnp.bfloat16)
    summed = lax.all_to_all(back, LOCAL, split_axis=0, concat_axis=0, tiled=True)
    summed = summed.astype(jnp.float32)
    selector = placed.astype(jnp.float32) * weights[:, :, None]
    mixed = jnp.einsum("tec,ecd->td", selector, summed, precision=lax.Precision.HIGHEST)
    return mixed.astype(jnp.bfloat16)


def solution(mesh):
    expert, tensor = mesh.devices.shape
    fine = Mesh(
        mesh.devices.reshape(expert // 4, 2, 2, 4, tensor // 4), ("y", "zl", "core", "x", "zh")
    )
    rows, cols = ("y", "zl", "core"), ("x", "zh")
    placed = (
        P(rows, cols),
        P(rows, None),
        P(rows, None),
        P(rows, None, cols),
        P(rows, None, cols),
        P(rows, None, cols),
    )

    return jax.shard_map(
        on_device, mesh=fine, in_specs=placed, out_specs=P(rows, cols), check_vma=False
    )
```

time: 241 us -> 243 us (level)
  blocking collectives: 0 us -> 38.1 us
  waiting for transfers between devices: 139 us -> 114 us
  starting transfers between devices: 75 us -> 65.9 us
    all_to_all x2 -> x1, waiting for transfers between devices: 42.9 us -> 3.69 us  [on_device(): lax.all_to_all(back, LOCAL, split_axis=0, concat_axis=0, tiled=True)]
    all_to_all x0 -> x1, blocking collectives: none -> 38.1 us  [on_device(): lax.all_to_all(back.reshape(y_size * x_size, CAP, width_part), ('y', 'x')...]
    ppermute x9, waiting for transfers between devices: 55.5 us -> 69.9 us  [shift(): lax.ppermute(array, axis, [(i, (i + step) % size) for i in range(size)])]
    all_to_all x2 -> x1, starting transfers between devices: 10.4 us -> 6.28 us  [on_device(): lax.all_to_all(back, LOCAL, split_axis=0, concat_axis=0, tiled=True)]
    ppermute x9, starting transfers between devices: 26.3 us -> 22.7 us  [shift(): lax.ppermute(array, axis, [(i, (i + step) % size) for i in range(size)])]
    all_to_all x2, waiting for transfers between devices: 17.9 us -> 20.4 us  [share(): parts = lax.all_to_all(term, 'zh', split_axis=0, concat_axis=0, tiled=True)]
  transfers between devices with their start and end apart: 16 -> 15, of which waited for: 13 -> 11; matrix products, arithmetic and copies ran while one was open for 7% -> 7% of each run, Pallas kernels for 0% -> 0%
where the time goes in v2:
time: 243 us; the launch traced here: 242 us
  waiting for transfers between devices  114 us (47%)
  starting transfers between devices  65.9 us (27%)
  blocking collectives  38.1 us (16%)
  matrix products  17.1 us (7%)
  local copies, waits for them, and re-layouts  4.27 us (2%)
    ppermute x9, waiting for transfers between devices, shift(): lax.ppermute(array, axis, [(i, (i + step) % size) for i in range(size)])  69.9 us
    all_to_all x1, blocking collectives, on_device(): lax.all_to_all(back.reshape(y_size * x_size, CAP, width_part), ('y', 'x')...  38.1 us
    ppermute x9, starting transfers between devices, shift(): lax.ppermute(array, axis, [(i, (i + step) % size) for i in range(size)])  22.7 us
    all_to_all x2, waiting for transfers between devices, share(): parts = lax.all_to_all(term, 'zh', split_axis=0, concat_axis=0, tiled=True)  20.4 us
    all_to_all x2, starting transfers between devices, share(): parts = lax.all_to_all(term, 'zh', split_axis=0, concat_axis=0, tiled=True)  18.2 us
    dot_general x8, matrix products, project(): lax.dot_general(row_block, block, contract, preferred_element_type=jnp.fl...  11.4 us
    all_to_all x1, waiting for transfers between devices, on_device(): lax.all_to_all(sent.reshape(EXPERTS * x_size, CAP, width_part), LOCAL + (...  10.9 us
    all_to_all x1, starting transfers between devices, on_device(): lax.all_to_all(sent.reshape(EXPERTS * x_size, CAP, width_part), LOCAL + (...  10.2 us
  transfers between devices with their start and end apart: 15, of which 11 were waited for; matrix products, arithmetic and copies ran while one was open for 7% of the time, Pallas kernels for 0%

profile of v2, /device:TPU:1, one launch (start us, length us, event | category | flops | bytes accessed | tf_op | source)
XLA Modules:
  0.0 241.9 jit_solution(16689659205640427616)
XLA Ops:
  2.2 10.2 %all-to-all-start = ((bf16[16,48,384]{2,1,0:T(8,128)(2,1)}), bf16[16,48,384]{2,1,0:T(8,128)(2,1)S(1)}, u32[]{:S(2)}, u32[]{:S(2)}) async-start(bf16[16,48,384]{2,1,0:T(8,128)(2,1)} %bitcast.1), calls=%async_computation | async-start | bytes 1179648 | tf_op jit(solution)/shard_map/all_to_all | solution.py:45
  12.4 10.9 %all-to-all-done = bf16[16,48,384]{2,1,0:T(8,128)(2,1)S(1)} async-done(((bf16[16,48,384]{2,1,0:T(8,128)(2,1)}), bf16[16,48,384]{2,1,0:T(8,128)(2,1)S(1)}, u32[]{:S(2)}, u32[]{:S(2)}) %all-to-all-start) | async-done | bytes 589856 | tf_op jit(solution)/shard_map/all_to_all | solution.py:45
  24.6 4.1 %all-to-all-start.1 = ((bf16[8,4,48,384]{3,2,1,0:T(8,128)(2,1)}), bf16[8,4,48,384]{3,2,1,0:T(8,128)(2,1)S(1)}, u32[]{:S(2)}, u32[]{:S(2)}) async-start(bf16[8,4,48,384]{3,2,1,0:T(8,128)(2,1)} %broadcast_in_dim.24), calls=%async_computation.1 | async-start | bytes 2359296 | tf_op jit(solution)/shard_map/all_to_all | solution.py:56
  28.7 2.6 %collective-permute-start = (bf16[1024,384]{1,0:T(8,128)(2,1)S(1)}, bf16[1024,384]{1,0:T(8,128)(2,1)S(1)}, u32[]{:S(2)}, u32[]{:S(2)}) collective-permute-start(bf16[1024,384]{1,0:T(8,128)(2,1)S(1)} %bitcast.82), channel_id=1, source_target_pairs={{0,12},{4,0},{8,4},{12,8},{1,13},{5,1},{9,5},{13,9},{2,14},{6,2},{... | collective-permute-start | bytes 2359304 | tf_op jit(solution)/shard_map/ppermute | solution.py:15
  31.3 3.0 %collective-permute-start.1 = (bf16[1024,384]{1,0:T(8,128)(2,1)S(1)}, bf16[1024,384]{1,0:T(8,128)(2,1)S(1)}, u32[]{:S(2)}, u32[]{:S(2)}) collective-permute-start(bf16[1024,384]{1,0:T(8,128)(2,1)S(1)} %bitcast.83), channel_id=1, source_target_pairs={{0,8},{4,12},{8,0},{12,4},{1,9},{5,13},{9,1},{13,5},{2,10},{6,14},... | collective-permute-start | bytes 2359304 | tf_op jit(solution)/shard_map/ppermute | solution.py:15
  34.3 2.3 collective-permute-start.2
  36.6 12.3 %collective-permute-done = bf16[1024,384]{1,0:T(8,128)(2,1)S(1)} collective-permute-done((bf16[1024,384]{1,0:T(8,128)(2,1)S(1)}, bf16[1024,384]{1,0:T(8,128)(2,1)S(1)}, u32[]{:S(2)}, u32[]{:S(2)}) %collective-permute-start) | collective-permute-done | bytes 786464 | tf_op jit(solution)/shard_map/ppermute | solution.py:15
  48.9 4.4 %collective-permute-done.1 = bf16[1024,384]{1,0:T(8,128)(2,1)S(1)} collective-permute-done((bf16[1024,384]{1,0:T(8,128)(2,1)S(1)}, bf16[1024,384]{1,0:T(8,128)(2,1)S(1)}, u32[]{:S(2)}, u32[]{:S(2)}) %collective-permute-start.1) | collective-permute-done | bytes 786464 | tf_op jit(solution)/shard_map/ppermute | solution.py:15
  53.3 17.7 %collective-permute-done.2 = bf16[1024,384]{1,0:T(8,128)(2,1)S(1)} collective-permute-done((bf16[1024,384]{1,0:T(8,128)(2,1)S(1)}, bf16[1024,384]{1,0:T(8,128)(2,1)S(1)}, u32[]{:S(2)}, u32[]{:S(2)}) %collective-permute-start.2) | collective-permute-done | bytes 786464 | tf_op jit(solution)/shard_map/ppermute | solution.py:15
  71.0 1.9 collective-permute-start.3
  72.9 3.0 %collective-permute-start.4 = (bf16[1024,384]{1,0:T(8,128)(2,1)}, bf16[1024,384]{1,0:T(8,128)(2,1)}, u32[]{:S(2)}, u32[]{:S(2)}) collective-permute-start(bf16[1024,384]{1,0:T(8,128)(2,1)} %bitcast.86), channel_id=1, source_target_pairs={{0,8},{4,12},{8,0},{12,4},{1,9},{5,13},{9,1},{13,5},{2,10},{6,14},... | collective-permute-start | bytes 2359304 | tf_op jit(solution)/shard_map/ppermute | solution.py:15
  76.0 2.8 %collective-permute-start.5 = (bf16[1024,384]{1,0:T(8,128)(2,1)}, bf16[1024,384]{1,0:T(8,128)(2,1)S(1)}, u32[]{:S(2)}, u32[]{:S(2)}) collective-permute-start(bf16[1024,384]{1,0:T(8,128)(2,1)} %bitcast.87), channel_id=1, source_target_pairs={{0,4},{4,8},{8,12},{12,0},{1,5},{5,9},{9,13},{13,1},{2,6},{6,10},{... | collective-permute-start | bytes 2359304 | tf_op jit(solution)/shard_map/ppermute | solution.py:15
  78.9 1.8 fusion.12
  84.1 9.1 %all-to-all-start.2 = ((bf16[4,96,1024]{2,1,0:T(8,128)(2,1)}), bf16[4,96,1024]{2,1,0:T(8,128)(2,1)S(1)}, u32[]{:S(2)}, u32[]{:S(2)}) async-start(bf16[4,96,1024]{2,1,0:T(8,128)(2,1)} %bitcast.12), calls=%async_computation.2 | async-start | bytes 1572864 | tf_op jit(solution)/shard_map/all_to_all | solution.py:70
  93.2 1.7 fusion.18
  95.0 1.7 fusion.19
  96.7 1.7 fusion.20
  98.4 14.4 %collective-permute-done.5 = bf16[1024,384]{1,0:T(8,128)(2,1)S(1)} collective-permute-done((bf16[1024,384]{1,0:T(8,128)(2,1)}, bf16[1024,384]{1,0:T(8,128)(2,1)S(1)}, u32[]{:S(2)}, u32[]{:S(2)}) %collective-permute-start.5) | collective-permute-done | bytes 786464 | tf_op jit(solution)/shard_map/ppermute | solution.py:15
  114.5 9.1 %all-to-all-start.3 = ((bf16[4,96,1024]{2,1,0:T(8,128)(2,1)}), bf16[4,96,1024]{2,1,0:T(8,128)(2,1)S(1)}, u32[]{:S(2)}, u32[]{:S(2)}) async-start(bf16[4,96,1024]{2,1,0:T(8,128)(2,1)} %bitcast.14), calls=%async_computation.3 | async-start | bytes 1572864 | tf_op jit(solution)/shard_map/all_to_all | solution.py:70
  123.7 20.4 %all-to-all-done.3 = bf16[4,96,1024]{2,1,0:T(8,128)(2,1)S(1)} async-done(((bf16[4,96,1024]{2,1,0:T(8,128)(2,1)}), bf16[4,96,1024]{2,1,0:T(8,128)(2,1)S(1)}, u32[]{:S(2)}, u32[]{:S(2)}) %all-to-all-start.3) | async-done | bytes 786464 | tf_op jit(solution)/shard_map/all_to_all | solution.py:70
  145.4 4.3 %all-to-all-start.4 = ((bf16[4,96,1024]{2,1,0:T(8,128)(2,1)}), bf16[4,96,1024]{2,1,0:T(8,128)(2,1)S(1)}, u32[]{:S(2)}, u32[]{:S(2)}) async-start(bf16[4,96,1024]{2,1,0:T(8,128)(2,1)} %broadcast_in_dim.25), calls=%async_computation.4 | async-start | bytes 1572864 | tf_op jit(solution)/shard_map/all_to_all | solution.py:83
  149.7 1.9 collective-permute-start.6
  151.6 1.9 collective-permute-start.7
  153.6 3.4 %collective-permute-start.8 = (bf16[1024,384]{1,0:T(8,128)(2,1)S(1)}, bf16[1024,384]{1,0:T(8,128)(2,1)S(1)}, u32[]{:S(2)}, u32[]{:S(2)}) collective-permute-start(bf16[1024,384]{1,0:T(8,128)(2,1)S(1)} %bitcast.95), channel_id=1, source_target_pairs={{0,4},{4,8},{8,12},{12,0},{1,5},{5,9},{9,13},{13,1},{2,6},{6,10},{... | collective-permute-start | bytes 2359304 | tf_op jit(solution)/shard_map/ppermute | solution.py:15
  156.9 9.1 %all-to-all-done.4 = bf16[4,96,1024]{2,1,0:T(8,128)(2,1)S(1)} async-done(((bf16[4,96,1024]{2,1,0:T(8,128)(2,1)}), bf16[4,96,1024]{2,1,0:T(8,128)(2,1)S(1)}, u32[]{:S(2)}, u32[]{:S(2)}) %all-to-all-start.4) | async-done | bytes 786464 | tf_op jit(solution)/shard_map/all_to_all | solution.py:83
  166.8 3.1 %collective-permute-done.6 = bf16[1024,384]{1,0:T(8,128)(2,1)} collective-permute-done((bf16[1024,384]{1,0:T(8,128)(2,1)S(1)}, bf16[1024,384]{1,0:T(8,128)(2,1)}, u32[]{:S(2)}, u32[]{:S(2)}) %collective-permute-start.6) | collective-permute-done | bytes 786464 | tf_op jit(solution)/shard_map/ppermute | solution.py:15
  169.8 1.7 convolution_convert_fusion.2
  173.0 1.7 convolution_convert_fusion.1
  174.8 16.6 %collective-permute-done.8 = bf16[1024,384]{1,0:T(8,128)(2,1)S(1)} collective-permute-done((bf16[1024,384]{1,0:T(8,128)(2,1)S(1)}, bf16[1024,384]{1,0:T(8,128)(2,1)S(1)}, u32[]{:S(2)}, u32[]{:S(2)}) %collective-permute-start.8) | collective-permute-done | bytes 786464 | tf_op jit(solution)/shard_map/ppermute | solution.py:15
  192.0 38.1 %all_to_all.43 = bf16[32,48,384]{2,1,0:T(8,128)(2,1)S(1)} all-to-all(bf16[32,48,384]{2,1,0:T(8,128)(2,1)S(1)} %bitcast.67), channel_id=1, replica_groups=mesh['y'=8,'zl'=2,'core'=2,'x'=4,'zh'=4] {'y','x'}, dimensions={0} | all-to-all | bytes 2359296 | tf_op jit(solution)/shard_map/all_to_all | solution.py:95
  230.9 6.3 %all-to-all-start.6 = ((bf16[4,48,384]{2,1,0:T(8,128)(2,1)}), bf16[4,48,384]{2,1,0:T(8,128)(2,1)S(1)}, u32[]{:S(2)}, u32[]{:S(2)}) async-start(bf16[4,48,384]{2,1,0:T(8,128)(2,1)} %reduce_sum.52), calls=%async_computation.6 | async-start | bytes 294912 | tf_op jit(solution)/shard_map/all_to_all | solution.py:103
  237.2 3.7 %all-to-all-done.6 = bf16[4,48,384]{2,1,0:T(8,128)(2,1)S(1)} async-done(((bf16[4,48,384]{2,1,0:T(8,128)(2,1)}), bf16[4,48,384]{2,1,0:T(8,128)(2,1)S(1)}, u32[]{:S(2)}, u32[]{:S(2)}) %all-to-all-start.6) | async-done | bytes 147488 | tf_op jit(solution)/shard_map/all_to_all | solution.py:103
  (53 shorter events, 14.6 us)
Async XLA Ops:
  0.0 1.1 copy-start
  2.2 21.1 %all-to-all-start = ((bf16[16,48,384]{2,1,0:T(8,128)(2,1)}), bf16[16,48,384]{2,1,0:T(8,128)(2,1)S(1)}, u32[]{:S(2)}, u32[]{:S(2)}) async-start(bf16[16,48,384]{2,1,0:T(8,128)(2,1)} %bitcast.1), calls=%async_computation | async-start | bytes 1179648 | tf_op jit(solution)/shard_map/all_to_all | solution.py:45
  23.4 5.3 %copy-start.3 = (bf16[1,1024,384]{2,1,0:T(8,128)(2,1)S(1)}, bf16[1,1024,384]{2,1,0:T(8,128)(2,1)}, u32[]{:S(2)}) copy-start(bf16[1,1024,384]{2,1,0:T(8,128)(2,1)} %param.9) | copy-start | bytes 2359300
  24.6 54.2 %all-to-all-start.1 = ((bf16[8,4,48,384]{3,2,1,0:T(8,128)(2,1)}), bf16[8,4,48,384]{3,2,1,0:T(8,128)(2,1)S(1)}, u32[]{:S(2)}, u32[]{:S(2)}) async-start(bf16[8,4,48,384]{3,2,1,0:T(8,128)(2,1)} %broadcast_in_dim.24), calls=%async_computation.1 | async-start | bytes 2359296 | tf_op jit(solution)/shard_map/all_to_all | solution.py:56
  28.7 20.2 %collective-permute-start = (bf16[1024,384]{1,0:T(8,128)(2,1)S(1)}, bf16[1024,384]{1,0:T(8,128)(2,1)S(1)}, u32[]{:S(2)}, u32[]{:S(2)}) collective-permute-start(bf16[1024,384]{1,0:T(8,128)(2,1)S(1)} %bitcast.82), channel_id=1, source_target_pairs={{0,12},{4,0},{8,4},{12,8},{1,13},{5,1},{9,5},{13,9},{2,14},{6,2},{... | collective-permute-start | bytes 2359304 | tf_op jit(solution)/shard_map/ppermute | solution.py:15
  31.3 22.0 %collective-permute-start.1 = (bf16[1024,384]{1,0:T(8,128)(2,1)S(1)}, bf16[1024,384]{1,0:T(8,128)(2,1)S(1)}, u32[]{:S(2)}, u32[]{:S(2)}) collective-permute-start(bf16[1024,384]{1,0:T(8,128)(2,1)S(1)} %bitcast.83), channel_id=1, source_target_pairs={{0,8},{4,12},{8,0},{12,4},{1,9},{5,13},{9,1},{13,5},{2,10},{6,14},... | collective-permute-start | bytes 2359304 | tf_op jit(solution)/shard_map/ppermute | solution.py:15
  34.3 36.7 %collective-permute-start.2 = (bf16[1024,384]{1,0:T(8,128)(2,1)S(1)}, bf16[1024,384]{1,0:T(8,128)(2,1)S(1)}, u32[]{:S(2)}, u32[]{:S(2)}) collective-permute-start(bf16[1024,384]{1,0:T(8,128)(2,1)S(1)} %bitcast.84), channel_id=1, source_target_pairs={{0,4},{4,8},{8,12},{12,0},{1,5},{5,9},{9,13},{13,1},{2,6},{6,10},{... | collective-permute-start | bytes 2359304 | tf_op jit(solution)/shard_map/ppermute | solution.py:15
  48.9 27.1 %copy-start.4 = (bf16[1024,384]{1,0:T(8,128)(2,1)}, bf16[1024,384]{1,0:T(8,128)(2,1)S(1)}, u32[]{:S(2)}) copy-start(bf16[1024,384]{1,0:T(8,128)(2,1)S(1)} %collective-permute-done) | copy-start | bytes 2359300
  53.3 22.7 %copy-start.6 = (bf16[1024,384]{1,0:T(8,128)(2,1)}, bf16[1024,384]{1,0:T(8,128)(2,1)S(1)}, u32[]{:S(2)}) copy-start(bf16[1024,384]{1,0:T(8,128)(2,1)S(1)} %collective-permute-done.1) | copy-start | bytes 2359300
  71.0 4.9 %copy-start.1 = (bf16[1024,384]{1,0:T(8,128)(2,1)}, bf16[1024,384]{1,0:T(8,128)(2,1)S(1)}, u32[]{:S(2)}) copy-start(bf16[1024,384]{1,0:T(8,128)(2,1)S(1)} %collective-permute-done.2) | copy-start | bytes 2359300
  71.0 23.9 %collective-permute-start.3 = (bf16[1024,384]{1,0:T(8,128)(2,1)}, bf16[1024,384]{1,0:T(8,128)(2,1)}, u32[]{:S(2)}, u32[]{:S(2)}) collective-permute-start(bf16[1024,384]{1,0:T(8,128)(2,1)} %bitcast.85), channel_id=1, source_target_pairs={{0,12},{4,0},{8,4},{12,8},{1,13},{5,1},{9,5},{13,9},{2,14},{6,2},{... | collective-permute-start | bytes 2359304 | tf_op jit(solution)/shard_map/ppermute | solution.py:15
  72.9 23.8 %collective-permute-start.4 = (bf16[1024,384]{1,0:T(8,128)(2,1)}, bf16[1024,384]{1,0:T(8,128)(2,1)}, u32[]{:S(2)}, u32[]{:S(2)}) collective-permute-start(bf16[1024,384]{1,0:T(8,128)(2,1)} %bitcast.86), channel_id=1, source_target_pairs={{0,8},{4,12},{8,0},{12,4},{1,9},{5,13},{9,1},{13,5},{2,10},{6,14},... | collective-permute-start | bytes 2359304 | tf_op jit(solution)/shard_map/ppermute | solution.py:15
  76.0 36.9 %collective-permute-start.5 = (bf16[1024,384]{1,0:T(8,128)(2,1)}, bf16[1024,384]{1,0:T(8,128)(2,1)S(1)}, u32[]{:S(2)}, u32[]{:S(2)}) collective-permute-start(bf16[1024,384]{1,0:T(8,128)(2,1)} %bitcast.87), channel_id=1, source_target_pairs={{0,4},{4,8},{8,12},{12,0},{1,5},{5,9},{9,13},{13,1},{2,6},{6,10},{... | collective-permute-start | bytes 2359304 | tf_op jit(solution)/shard_map/ppermute | solution.py:15
  78.9 1.8 copy-start.5
  80.7 1.1 copy-start.7
  81.3 1.2 copy-start.2
  84.1 30.4 %all-to-all-start.2 = ((bf16[4,96,1024]{2,1,0:T(8,128)(2,1)}), bf16[4,96,1024]{2,1,0:T(8,128)(2,1)S(1)}, u32[]{:S(2)}, u32[]{:S(2)}) async-start(bf16[4,96,1024]{2,1,0:T(8,128)(2,1)} %bitcast.12), calls=%async_computation.2 | async-start | bytes 1572864 | tf_op jit(solution)/shard_map/all_to_all | solution.py:70
  114.5 29.7 %all-to-all-start.3 = ((bf16[4,96,1024]{2,1,0:T(8,128)(2,1)}), bf16[4,96,1024]{2,1,0:T(8,128)(2,1)S(1)}, u32[]{:S(2)}, u32[]{:S(2)}) async-start(bf16[4,96,1024]{2,1,0:T(8,128)(2,1)} %bitcast.14), calls=%async_computation.3 | async-start | bytes 1572864 | tf_op jit(solution)/shard_map/all_to_all | solution.py:70
  144.3 5.4 %copy-start.8 = (bf16[1,1024,384]{2,1,0:T(8,128)(2,1)S(1)}, bf16[1,1024,384]{2,1,0:T(8,128)(2,1)}, u32[]{:S(2)}) copy-start(bf16[1,1024,384]{2,1,0:T(8,128)(2,1)} %param.11) | copy-start | bytes 2359300
  145.4 20.6 %all-to-all-start.4 = ((bf16[4,96,1024]{2,1,0:T(8,128)(2,1)}), bf16[4,96,1024]{2,1,0:T(8,128)(2,1)S(1)}, u32[]{:S(2)}, u32[]{:S(2)}) async-start(bf16[4,96,1024]{2,1,0:T(8,128)(2,1)} %broadcast_in_dim.25), calls=%async_computation.4 | async-start | bytes 1572864 | tf_op jit(solution)/shard_map/all_to_all | solution.py:83
  149.7 20.1 %collective-permute-start.6 = (bf16[1024,384]{1,0:T(8,128)(2,1)S(1)}, bf16[1024,384]{1,0:T(8,128)(2,1)}, u32[]{:S(2)}, u32[]{:S(2)}) collective-permute-start(bf16[1024,384]{1,0:T(8,128)(2,1)S(1)} %bitcast.93), channel_id=1, source_target_pairs={{0,12},{4,0},{8,4},{12,8},{1,13},{5,1},{9,5},{13,9},{2,14},{6,2},{... | collective-permute-start | bytes 2359304 | tf_op jit(solution)/shard_map/ppermute | solution.py:15
  151.6 21.4 %collective-permute-start.7 = (bf16[1024,384]{1,0:T(8,128)(2,1)S(1)}, bf16[1024,384]{1,0:T(8,128)(2,1)}, u32[]{:S(2)}, u32[]{:S(2)}) collective-permute-start(bf16[1024,384]{1,0:T(8,128)(2,1)S(1)} %bitcast.94), channel_id=1, source_target_pairs={{0,8},{4,12},{8,0},{12,4},{1,9},{5,13},{9,1},{13,5},{2,10},{6,14},... | collective-permute-start | bytes 2359304 | tf_op jit(solution)/shard_map/ppermute | solution.py:15
  153.6 37.8 %collective-permute-start.8 = (bf16[1024,384]{1,0:T(8,128)(2,1)S(1)}, bf16[1024,384]{1,0:T(8,128)(2,1)S(1)}, u32[]{:S(2)}, u32[]{:S(2)}) collective-permute-start(bf16[1024,384]{1,0:T(8,128)(2,1)S(1)} %bitcast.95), channel_id=1, source_target_pairs={{0,4},{4,8},{8,12},{12,0},{1,5},{5,9},{9,13},{13,1},{2,6},{6,10},{... | collective-permute-start | bytes 2359304 | tf_op jit(solution)/shard_map/ppermute | solution.py:15
  230.9 10.0 %all-to-all-start.6 = ((bf16[4,48,384]{2,1,0:T(8,128)(2,1)}), bf16[4,48,384]{2,1,0:T(8,128)(2,1)S(1)}, u32[]{:S(2)}, u32[]{:S(2)}) async-start(bf16[4,48,384]{2,1,0:T(8,128)(2,1)} %reduce_sum.52), calls=%async_computation.6 | async-start | bytes 294912 | tf_op jit(solution)/shard_map/all_to_all | solution.py:103

commit v3 on v2

--- a/solution.py
+++ b/solution.py
@@ -1,6 +1,8 @@
 import jax
 import jax.numpy as jnp
 from jax import lax
+from jax.experimental import pallas as pl
+from jax.experimental.pallas import tpu as pltpu
 from jax.sharding import Mesh
 from jax.sharding import PartitionSpec as P
 
@@ -8,6 +10,8 @@
 EXPERTS = 4
 CAP = 48
 LOCAL = ("zl", "core")
+TILE = 256
+GRANT = 16 << 20
 
 
 def shift(array, axis, step):
@@ -15,11 +19,96 @@
     return lax.ppermute(array, axis, [(i, (i + step) % size) for i in range(size)])
 
 
-def spread(weight):
-    after = shift(weight, "x", -1)
-    before = shift(weight, "x", 1)
-    across = shift(weight, "x", 2)
-    return (weight, after, across, before)
+def beside(weight):
+    return shift(weight, "x", -1), shift(weight, "x", 1)
+
+
+def across(pair):
+    after, before = pair
+    half = after.shape[0] // 2
+    return shift(after[:half], "x", -1), shift(before[half:], "x", 1)
+
+
+def project_kernel(rows_ref, own_ref, after_ref, low_ref, high_ref, before_ref, out_ref):
+    in_low = pl.program_id(0) < pl.num_programs(0) // 2
+    opposite = jnp.where(in_low, low_ref[...], high_ref[...])
+    blocks = (own_ref[...], after_ref[...], opposite, before_ref[...])
+    sources, _, cap, depth = rows_ref.shape
+    total = None
+    for step, block in enumerate(blocks):
+        rows = rows_ref[:, step].reshape(sources * cap, depth)
+        term = lax.dot_general(
+            rows, block, (((1,), (1,)), ((), ())), preferred_element_type=jnp.float32
+        )
+        term = term.astype(jnp.bfloat16).astype(jnp.float32)
+        total = term if total is None else total + term
+    out_ref[...] = total.astype(jnp.bfloat16)
+
+
+def project(rows, own, pair, halves):
+    sources, blocks, cap, depth = rows.shape
+    width = own.shape[0]
+    steps = width // TILE
+    half = steps // 2
+    block = (TILE, depth)
+    return pl.pallas_call(
+        project_kernel,
+        out_shape=jax.ShapeDtypeStruct((sources * cap, width), jnp.bfloat16),
+        grid=(steps,),
+        in_specs=[
+            pl.BlockSpec(rows.shape, lambda i: (0, 0, 0, 0)),
+            pl.BlockSpec(block, lambda i: (i, 0)),
+            pl.BlockSpec(block, lambda i: (i, 0)),
+            pl.BlockSpec(block, lambda i: (jnp.minimum(i, half - 1), 0)),
+            pl.BlockSpec(block, lambda i: (jnp.maximum(i - half, 0), 0)),
+            pl.BlockSpec(block, lambda i: (i, 0)),
+        ],
+        out_specs=pl.BlockSpec((sources * cap, TILE), lambda i: (0, i)),
+        compiler_params=pltpu.CompilerParams(vmem_limit_bytes=GRANT),
+        cost_estimate=pl.CostEstimate(
+            flops=2 * sources * cap * blocks * depth * width,
+            bytes_accessed=2 * (rows.size + blocks * own.size + sources * cap * width),
+            transcendentals=0,
+        ),
+    )(rows, own, pair[0], *halves, pair[1])
+
+
+def expand_kernel(order_ref, hidden_ref, own_ref, after_ref, low_ref, high_ref, before_ref, out_ref):
+    sources, _, cap, width = out_ref.shape
+    half = low_ref.shape[0]
+    hidden = hidden_ref[...]
+
+    def put(step, value):
+        value = value.astype(jnp.bfloat16).reshape(sources, cap, width)
+        out_ref[:, order_ref[step]] = value
+
+    def dot(left, right):
+        return jnp.dot(left, right, preferred_element_type=jnp.float32)
+
+    put(0, dot(hidden, own_ref[...]))
+    put(1, dot(hidden, after_ref[...]))
+    put(3, dot(hidden, before_ref[...]))
+    put(2, dot(hidden[:, :half], low_ref[...]) + dot(hidden[:, half:], high_ref[...]))
+
+
+def expand(order, hidden, own, pair, halves, sources):
+    rows, width = hidden.shape
+    depth = own.shape[1]
+    cap = rows // sources
+    places = order.shape[0]
+    vmem = pl.BlockSpec(memory_space=pltpu.VMEM)
+    return pl.pallas_call(
+        expand_kernel,
+        out_shape=jax.ShapeDtypeStruct((sources, places, cap, depth), jnp.bfloat16),
+        in_specs=[pl.BlockSpec(memory_space=pltpu.SMEM)] + [vmem] * 6,
+        out_specs=vmem,
+        compiler_params=pltpu.CompilerParams(vmem_limit_bytes=GRANT),
+        cost_estimate=pl.CostEstimate(
+            flops=2 * rows * width * depth * places,
+            bytes_accessed=2 * (hidden.size + places * own.size + places * rows * depth),
+            transcendentals=0,
+        ),
+    )(order, hidden, own, pair[0], *halves, pair[1])
 
 
 def on_device(tokens, expert_ids, gate_fixed, w_gate, w_up, w_down):
@@ -40,7 +129,6 @@
     outgoing = jnp.einsum(
         "tec,td->ecd", placed.astype(jnp.bfloat16), tokens, preferred_element_type=jnp.float32
     ).astype(jnp.bfloat16)
-    gate_all = spread(w_gate[0])
     sent = jnp.broadcast_to(outgoing[:, None], (EXPERTS, x_size, CAP, width_part))
     local = lax.all_to_all(
         sent.reshape(EXPERTS * x_size, CAP, width_part),
@@ -55,43 +143,29 @@
     sent_y = jnp.broadcast_to(mine[None], (y_size, x_size, CAP, width_part))
     rows = lax.all_to_all(sent_y, "y", split_axis=0, concat_axis=0, tiled=True)
     total_rows = y_size * CAP
-    rows = [rows[:, step].reshape(total_rows, width_part) for step in range(x_size)]
-    contract = (((1,), (1,)), ((), ()))
-
-    def project(blocks):
-        total = None
-        for row_block, block in zip(rows, blocks):
-            term = lax.dot_general(row_block, block, contract, preferred_element_type=jnp.float32)
-            term = lax.reduce_precision(term, 8, 7)
-            total = term if total is None else total + term
-        return total.astype(jnp.bfloat16)
+
+    gate_own = w_gate[0]
+    gate_pair = beside(gate_own)
+    gate_halves = across(gate_pair)
+    up_own, _ = lax.optimization_barrier((w_up[0], gate_pair))
+    up_pair = beside(up_own)
+    up_halves = across(up_pair)
+    down_own, _ = lax.optimization_barrier((w_down[0], up_pair))
+    down_pair = beside(down_own)
+    down_halves = across(down_pair)
 
     def share(term):
         parts = lax.all_to_all(term, "zh", split_axis=0, concat_axis=0, tiled=True)
         parts = parts.reshape(zh_size, total_rows // zh_size, -1)
         return jnp.sum(parts.astype(jnp.float32), axis=0)
 
-    gate_term = project(gate_all)
-    up_own, gate_all = lax.optimization_barrier((w_up[0], gate_all))
-    up_all = spread(up_own)
+    gate_term = project(rows, gate_own, gate_pair, gate_halves)
     gate_share = share(gate_term)
-    up_term = project(up_all)
-    down_own, up_all = lax.optimization_barrier((w_down[0], up_all))
-    down_all = spread(down_own)
+    up_term = project(rows, up_own, up_pair, up_halves)
     up_share = share(up_term)
     hidden = (jax.nn.silu(gate_share) * up_share).astype(jnp.bfloat16)
-    hidden_rows = lax.all_to_all(
-        jnp.broadcast_to(hidden[None], (zh_size,) + hidden.shape),
-        "zh",
-        split_axis=0,
-        concat_axis=0,
-        tiled=True,
-    ).reshape(total_rows, -1)
-    back = jnp.zeros((y_size, x_size, CAP, width_part), jnp.bfloat16)
-    for step, block in enumerate(down_all):
-        out = jnp.dot(hidden_rows, block, preferred_element_type=jnp.float32).astype(jnp.bfloat16)
-        out = out.reshape(y_size, 1, CAP, width_part)
-        back = lax.dynamic_update_slice(back, out, (0, order[step], 0, 0))
+    hidden_rows = lax.all_gather(hidden, "zh", axis=0, tiled=True)
+    back = expand(jnp.stack(order), hidden_rows, down_own, down_pair, down_halves, y_size)
     back = lax.all_to_all(
         back.reshape(y_size * x_size, CAP, width_part),
         ("y", "x"),

time: 243 us -> 226 us (0.930)
  waiting for transfers between devices: 114 us -> 76.8 us
  matrix products: 17.1 us -> 1.18 us
  Pallas kernels: 0 us -> 10.1 us
  starting transfers between devices: 65.9 us -> 74.8 us
  blocking collectives: 38.1 us -> 46.8 us
  local copies, waits for them, and re-layouts: 4.27 us -> 9.15 us
  other arithmetic: 2.17 us -> 5.4 us
    all_to_all x2, waiting for transfers between devices: 20.4 us -> 0.92 us  [share(): parts = lax.all_to_all(term, 'zh', split_axis=0, concat_axis=0, tiled=True)]
    dot_general x12 -> x0, matrix products: 15.9 us -> none  [the longest x8 11.4 us: project(): lax.dot_general(row_block, block, contract, preferred_element_type=jnp.fl...]
    all_gather x0 -> x1, blocking collectives: none -> 15.8 us  [on_device(): hidden_rows = lax.all_gather(hidden, 'zh', axis=0, tiled=True)]
    pallas_call x0 -> x3, Pallas kernels: none -> 10.1 us  [the longest x2 7.77 us: project(): pl.pallas_call(project_kernel, out_shape=jax.ShapeDtypeStruct((sources *...]
    all_to_all x1 -> x0, waiting for transfers between devices: 9.07 us -> none  [on_device(): lax.all_to_all(jnp.broadcast_to(hidden[None], (zh_size,) + hidden.shape),...]
    ppermute x9 -> x12, starting transfers between devices: 22.7 us -> 31.7 us  [shift(): lax.ppermute(array, axis, [(i, (i + step) % size) for i in range(size)])]
    ppermute x9 -> x12, waiting for transfers between devices: 69.9 us -> 61.3 us  [shift(): lax.ppermute(array, axis, [(i, (i + step) % size) for i in range(size)])]
    all_to_all x1, starting transfers between devices: 6.28 us -> 14 us  [on_device(): lax.all_to_all(back, LOCAL, split_axis=0, concat_axis=0, tiled=True)]
  transfers between devices with their start and end apart: 15 -> 17, of which waited for: 11 -> 11; matrix products, arithmetic and copies ran while one was open for 7% -> 2% of each run, Pallas kernels for 0% -> 2%
where the time goes in v3:
time: 226 us; the launch traced here: 225 us
  waiting for transfers between devices  76.8 us (34%)
  starting transfers between devices  74.8 us (33%)
  blocking collectives  46.8 us (21%)
  Pallas kernels  10.1 us (4%)
  local copies, waits for them, and re-layouts  9.15 us (4%)
  other arithmetic  5.4 us (2%)
    ppermute x12, waiting for transfers between devices, shift(): lax.ppermute(array, axis, [(i, (i + step) % size) for i in range(size)])  61.3 us
    ppermute x12, starting transfers between devices, shift(): lax.ppermute(array, axis, [(i, (i + step) % size) for i in range(size)])  31.7 us
    all_to_all x1, blocking collectives, on_device(): lax.all_to_all(back.reshape(y_size * x_size, CAP, width_part), ('y', 'x')...  31.1 us
    all_gather x1, blocking collectives, on_device(): hidden_rows = lax.all_gather(hidden, 'zh', axis=0, tiled=True)  15.8 us
    all_to_all x2, starting transfers between devices, share(): parts = lax.all_to_all(term, 'zh', split_axis=0, concat_axis=0, tiled=True)  14.7 us
    all_to_all x1, starting transfers between devices, on_device(): lax.all_to_all(back, LOCAL, split_axis=0, concat_axis=0, tiled=True)  14 us
    all_to_all x1, waiting for transfers between devices, on_device(): lax.all_to_all(sent.reshape(EXPERTS * x_size, CAP, width_part), LOCAL + (...  10.9 us
    all_to_all x1, starting transfers between devices, on_device(): lax.all_to_all(sent.reshape(EXPERTS * x_size, CAP, width_part), LOCAL + (...  10.2 us
  transfers between devices with their start and end apart: 17, of which 11 were waited for; matrix products, arithmetic and copies ran while one was open for 2% of the time, Pallas kernels for 2%

profile of v3, /device:TPU:1, one launch (start us, length us, event | category | flops | bytes accessed | tf_op | source)
XLA Modules:
  0.0 224.5 jit_solution(4748689656777456314)
XLA Ops:
  2.2 10.2 %all-to-all-start = ((bf16[16,48,384]{2,1,0:T(8,128)(2,1)}), bf16[16,48,384]{2,1,0:T(8,128)(2,1)S(1)}, u32[]{:S(2)}, u32[]{:S(2)}) async-start(bf16[16,48,384]{2,1,0:T(8,128)(2,1)} %bitcast.5), calls=%async_computation | async-start | bytes 1179648 | tf_op jit(solution)/shard_map/all_to_all | solution.py:133
  12.4 10.9 %all-to-all-done = bf16[16,48,384]{2,1,0:T(8,128)(2,1)S(1)} async-done(((bf16[16,48,384]{2,1,0:T(8,128)(2,1)}), bf16[16,48,384]{2,1,0:T(8,128)(2,1)S(1)}, u32[]{:S(2)}, u32[]{:S(2)}) %all-to-all-start) | async-done | bytes 589856 | tf_op jit(solution)/shard_map/all_to_all | solution.py:133
  24.5 4.1 %all-to-all-start.1 = ((bf16[8,4,48,384]{3,2,1,0:T(8,128)(2,1)}), bf16[8,4,48,384]{3,2,1,0:T(8,128)(2,1)S(1)}, u32[]{:S(2)}, u32[]{:S(2)}) async-start(bf16[8,4,48,384]{3,2,1,0:T(8,128)(2,1)} %broadcast_in_dim.19), calls=%async_computation.1 | async-start | bytes 2359296 | tf_op jit(solution)/shard_map/all_to_all | solution.py:144
  28.7 2.6 %collective-permute-start = (bf16[1024,384]{1,0:T(8,128)(2,1)}, bf16[1024,384]{1,0:T(8,128)(2,1)S(1)}, u32[]{:S(2)}, u32[]{:S(2)}) collective-permute-start(bf16[1024,384]{1,0:T(8,128)(2,1)} %bitcast.11.own_ref), channel_id=1, source_target_pairs={{0,12},{4,0},{8,4},{12,8},{1,13},{5,1},{9,5},{13,9},{2,14},{6,2},{... | collective-permute-start | bytes 2359304 | tf_op jit(solution)/shard_map/ppermute | solution.py:19
  31.3 2.7 %collective-permute-start.2 = (bf16[1024,384]{1,0:T(8,128)(2,1)}, bf16[1024,384]{1,0:T(8,128)(2,1)S(1)}, u32[]{:S(2)}, u32[]{:S(2)}) collective-permute-start(bf16[1024,384]{1,0:T(8,128)(2,1)} %bitcast.11.own_ref), channel_id=1, source_target_pairs={{0,4},{4,8},{8,12},{12,0},{1,5},{5,9},{9,13},{13,1},{2,6},{6,10},{... | collective-permute-start | bytes 2359304 | tf_op jit(solution)/shard_map/ppermute | solution.py:19
  34.0 15.1 %collective-permute-done.after_ref = bf16[1024,384]{1,0:T(8,128)(2,1)S(1)} collective-permute-done((bf16[1024,384]{1,0:T(8,128)(2,1)}, bf16[1024,384]{1,0:T(8,128)(2,1)S(1)}, u32[]{:S(2)}, u32[]{:S(2)}) %collective-permute-start) | collective-permute-done | bytes 786464 | tf_op jit(solution)/shard_map/ppermute | solution.py:19
  49.0 4.1 %collective-permute-done.2.before_ref = bf16[1024,384]{1,0:T(8,128)(2,1)S(1)} collective-permute-done((bf16[1024,384]{1,0:T(8,128)(2,1)}, bf16[1024,384]{1,0:T(8,128)(2,1)S(1)}, u32[]{:S(2)}, u32[]{:S(2)}) %collective-permute-start.2) | collective-permute-done | bytes 786464 | tf_op jit(solution)/shard_map/ppermute | solution.py:19
  53.1 1.9 collective-permute-start.4
  55.0 3.4 %collective-permute-start.6 = (bf16[1024,384]{1,0:T(8,128)(2,1)}, bf16[1024,384]{1,0:T(8,128)(2,1)S(1)}, u32[]{:S(2)}, u32[]{:S(2)}) collective-permute-start(bf16[1024,384]{1,0:T(8,128)(2,1)} %bitcast.31), channel_id=1, source_target_pairs={{0,4},{4,8},{8,12},{12,0},{1,5},{5,9},{9,13},{13,1},{2,6},{6,10},{... | collective-permute-start | bytes 2359304 | tf_op jit(solution)/shard_map/ppermute | solution.py:19
  58.4 14.5 %collective-permute-done.4.after_ref = bf16[1024,384]{1,0:T(8,128)(2,1)S(1)} collective-permute-done((bf16[1024,384]{1,0:T(8,128)(2,1)}, bf16[1024,384]{1,0:T(8,128)(2,1)S(1)}, u32[]{:S(2)}, u32[]{:S(2)}) %collective-permute-start.4) | collective-permute-done | bytes 786464 | tf_op jit(solution)/shard_map/ppermute | solution.py:19
  72.9 3.4 %collective-permute-start.5 = (bf16[512,384]{1,0:T(8,128)(2,1)S(1)}, bf16[512,384]{1,0:T(8,128)(2,1)S(1)}, u32[]{:S(2)}, u32[]{:S(2)}) collective-permute-start(bf16[512,384]{1,0:T(8,128)(2,1)S(1)} %slice.26), channel_id=1, source_target_pairs={{0,12},{4,0},{8,4},{12,8},{1,13},{5,1},{9,5},{13,9},{2,14},{6,2},{... | collective-permute-start | bytes 1179656 | tf_op jit(solution)/shard_map/ppermute | solution.py:19
  76.4 1.9 collective-permute-start.7
  78.4 4.9 %collective-permute-done.5.low_ref = bf16[512,384]{1,0:T(8,128)(2,1)S(1)} collective-permute-done((bf16[512,384]{1,0:T(8,128)(2,1)S(1)}, bf16[512,384]{1,0:T(8,128)(2,1)S(1)}, u32[]{:S(2)}, u32[]{:S(2)}) %collective-permute-start.5) | collective-permute-done | bytes 393248 | tf_op jit(solution)/shard_map/ppermute | solution.py:19
  83.2 4.7 %collective-permute-done.7.high_ref = bf16[512,384]{1,0:T(8,128)(2,1)S(1)} collective-permute-done((bf16[512,384]{1,0:T(8,128)(2,1)S(1)}, bf16[512,384]{1,0:T(8,128)(2,1)S(1)}, u32[]{:S(2)}, u32[]{:S(2)}) %collective-permute-start.7) | collective-permute-done | bytes 393248 | tf_op jit(solution)/shard_map/ppermute | solution.py:19
  93.1 3.3 %shard_map.65 = bf16[384,1024]{1,0:T(8,128)(2,1)} custom-call(bf16[8,4,48,384]{3,2,1,0:T(8,128)(2,1)S(1)} %all-to-all-done.1.rows_ref, bf16[1024,384]{1,0:T(8,128)(2,1)S(1)} %bitcast.32, bf16[1024,384]{1,0:T(8,128)(2,1)S(1)} %copy-done.2, bf16[512,384]{1,0:T(8,128)(2,1)S(1)} %collective-permute-done.5.low_ref, bf16[512,384]{1,0:T(8,128)(2,1)S(1)} %copy-done.8, ...), custom_call_target="tpu_custom_call" | custom-call | flops 1207959552 | bytes 5111808 | tf_op jit(solution)/shard_map/pallas_call | solution.py:54
  96.4 9.1 %all-to-all-start.3 = ((bf16[4,96,1024]{2,1,0:T(8,128)(2,1)}), bf16[4,96,1024]{2,1,0:T(8,128)(2,1)}, u32[]{:S(2)}, u32[]{:S(2)}) async-start(bf16[4,96,1024]{2,1,0:T(8,128)(2,1)} %bitcast.14), calls=%async_computation.3 | async-start | bytes 1572864 | tf_op jit(solution)/shard_map/all_to_all | solution.py:158
  105.5 1.9 collective-permute-start.1
  107.5 3.4 %collective-permute-start.3 = (bf16[512,384]{1,0:T(8,128)(2,1)S(1)}, bf16[512,384]{1,0:T(8,128)(2,1)S(1)}, u32[]{:S(2)}, u32[]{:S(2)}) collective-permute-start(bf16[512,384]{1,0:T(8,128)(2,1)S(1)} %slice.25), channel_id=1, source_target_pairs={{0,4},{4,8},{8,12},{12,0},{1,5},{5,9},{9,13},{13,1},{2,6},{6,10},{... | collective-permute-start | bytes 1179656 | tf_op jit(solution)/shard_map/ppermute | solution.py:19
  110.9 3.9 %collective-permute-done.1.low_ref = bf16[512,384]{1,0:T(8,128)(2,1)S(1)} collective-permute-done((bf16[512,384]{1,0:T(8,128)(2,1)S(1)}, bf16[512,384]{1,0:T(8,128)(2,1)S(1)}, u32[]{:S(2)}, u32[]{:S(2)}) %collective-permute-start.1) | collective-permute-done | bytes 393248 | tf_op jit(solution)/shard_map/ppermute | solution.py:19
  114.8 3.2 %collective-permute-done.3.high_ref = bf16[512,384]{1,0:T(8,128)(2,1)S(1)} collective-permute-done((bf16[512,384]{1,0:T(8,128)(2,1)S(1)}, bf16[512,384]{1,0:T(8,128)(2,1)S(1)}, u32[]{:S(2)}, u32[]{:S(2)}) %collective-permute-start.3) | collective-permute-done | bytes 393248 | tf_op jit(solution)/shard_map/ppermute | solution.py:19
  118.0 4.5 %shard_map.64 = bf16[384,1024]{1,0:T(8,128)(2,1)} custom-call(bf16[8,4,48,384]{3,2,1,0:T(8,128)(2,1)S(1)} %all-to-all-done.1.rows_ref, bf16[1024,384]{1,0:T(8,128)(2,1)} %bitcast.11.own_ref, bf16[1024,384]{1,0:T(8,128)(2,1)S(1)} %collective-permute-done.after_ref, bf16[512,384]{1,0:T(8,128)(2,1)S(1)} %collective-permute-done.1.low_ref, ...), custom_call_target="tpu_custom_call" | custom-call | flops 1207959552 | bytes 5111808 | tf_op jit(solution)/shard_map/pallas_call | solution.py:54
  123.4 5.6 %all-to-all-start.2 = ((bf16[4,96,1024]{2,1,0:T(8,128)(2,1)}), bf16[4,96,1024]{2,1,0:T(8,128)(2,1)}, u32[]{:S(2)}, u32[]{:S(2)}) async-start(bf16[4,96,1024]{2,1,0:T(8,128)(2,1)} %bitcast.12), calls=%async_computation.2 | async-start | bytes 1572864 | tf_op jit(solution)/shard_map/all_to_all | solution.py:158
  129.0 1.9 collective-permute-start.8
  130.9 3.4 %collective-permute-start.10 = (bf16[1024,384]{1,0:T(8,128)(2,1)S(1)}, bf16[1024,384]{1,0:T(8,128)(2,1)S(1)}, u32[]{:S(2)}, u32[]{:S(2)}) collective-permute-start(bf16[1024,384]{1,0:T(8,128)(2,1)S(1)} %bitcast.34), channel_id=1, source_target_pairs={{0,4},{4,8},{8,12},{12,0},{1,5},{5,9},{9,13},{13,1},{2,6},{6,10},{... | collective-permute-start | bytes 2359304 | tf_op jit(solution)/shard_map/ppermute | solution.py:19
  134.4 11.0 %collective-permute-done.8.after_ref = bf16[1024,384]{1,0:T(8,128)(2,1)S(1)} collective-permute-done((bf16[1024,384]{1,0:T(8,128)(2,1)S(1)}, bf16[1024,384]{1,0:T(8,128)(2,1)S(1)}, u32[]{:S(2)}, u32[]{:S(2)}) %collective-permute-start.8) | collective-permute-done | bytes 786464 | tf_op jit(solution)/shard_map/ppermute | solution.py:19
  146.1 3.4 %collective-permute-start.9 = (bf16[512,384]{1,0:T(8,128)(2,1)}, bf16[512,384]{1,0:T(8,128)(2,1)S(1)}, u32[]{:S(2)}, u32[]{:S(2)}) collective-permute-start(bf16[512,384]{1,0:T(8,128)(2,1)} %slice.28), channel_id=1, source_target_pairs={{0,12},{4,0},{8,4},{12,8},{1,13},{5,1},{9,5},{13,9},{2,14},{6,2},{... | collective-permute-start | bytes 1179656 | tf_op jit(solution)/shard_map/ppermute | solution.py:19
  152.3 2.1 convert_reduce_fusion
  155.8 15.8 %all_gather.3.hidden_ref = bf16[384,1024]{1,0:T(8,128)(2,1)S(1)} all-gather(bf16[96,1024]{1,0:T(8,128)(2,1)S(1)} %multiply_convert_fusion), channel_id=1, replica_groups=mesh['y'=8,'zl'=2,'core'=2,'x'=4,'zh'=4] {'zh'}, dimensions={0}, use_global_device_ids=true | all-gather | bytes 983040 | tf_op jit(solution)/shard_map/all_gather | solution.py:167
  171.6 2.3 %shard_map.66 = bf16[8,4,48,384]{3,2,1,0:T(8,128)(2,1)S(1)} custom-call(s32[4]{0:T(128)S(1)} %pad_add_fusion.order_ref, bf16[384,1024]{1,0:T(8,128)(2,1)S(1)} %all_gather.3.hidden_ref, bf16[1024,384]{1,0:T(8,128)(2,1)S(1)} %bitcast.35, bf16[1024,384]{1,0:T(8,128)(2,1)S(1)} %collective-permute-done.8.after_ref, ...), custom_call_target="tpu_custom_call" | custom-call | flops 1207959552 | bytes 5111808 | tf_op jit(solution)/shard_map/pallas_call | solution.py:100
  173.9 31.1 %all_to_all.38 = bf16[32,48,384]{2,1,0:T(8,128)(2,1)S(1)} all-to-all(bf16[32,48,384]{2,1,0:T(8,128)(2,1)S(1)} %bitcast.29), channel_id=1, replica_groups=mesh['y'=8,'zl'=2,'core'=2,'x'=4,'zh'=4] {'y','x'}, dimensions={0} | all-to-all | bytes 2359296 | tf_op jit(solution)/shard_map/all_to_all | solution.py:169
  205.8 14.0 %all-to-all-start.5 = ((bf16[4,48,384]{2,1,0:T(8,128)(2,1)}), bf16[4,48,384]{2,1,0:T(8,128)(2,1)S(1)}, u32[]{:S(2)}, u32[]{:S(2)}) async-start(bf16[4,48,384]{2,1,0:T(8,128)(2,1)} %reduce_sum.52), calls=%async_computation.5 | async-start | bytes 294912 | tf_op jit(solution)/shard_map/all_to_all | solution.py:177
  219.8 3.7 %all-to-all-done.5 = bf16[4,48,384]{2,1,0:T(8,128)(2,1)S(1)} async-done(((bf16[4,48,384]{2,1,0:T(8,128)(2,1)}), bf16[4,48,384]{2,1,0:T(8,128)(2,1)S(1)}, u32[]{:S(2)}, u32[]{:S(2)}) %all-to-all-start.5) | async-done | bytes 147488 | tf_op jit(solution)/shard_map/all_to_all | solution.py:177
  (51 shorter events, 16.5 us)
Async XLA Ops:
  0.0 1.1 copy-start
  2.2 21.1 %all-to-all-start = ((bf16[16,48,384]{2,1,0:T(8,128)(2,1)}), bf16[16,48,384]{2,1,0:T(8,128)(2,1)S(1)}, u32[]{:S(2)}, u32[]{:S(2)}) async-start(bf16[16,48,384]{2,1,0:T(8,128)(2,1)} %bitcast.5), calls=%async_computation | async-start | bytes 1179648 | tf_op jit(solution)/shard_map/all_to_all | solution.py:133
  24.5 64.2 %all-to-all-start.1 = ((bf16[8,4,48,384]{3,2,1,0:T(8,128)(2,1)}), bf16[8,4,48,384]{3,2,1,0:T(8,128)(2,1)S(1)}, u32[]{:S(2)}, u32[]{:S(2)}) async-start(bf16[8,4,48,384]{3,2,1,0:T(8,128)(2,1)} %broadcast_in_dim.19), calls=%async_computation.1 | async-start | bytes 2359296 | tf_op jit(solution)/shard_map/all_to_all | solution.py:144
  28.7 20.4 %collective-permute-start = (bf16[1024,384]{1,0:T(8,128)(2,1)}, bf16[1024,384]{1,0:T(8,128)(2,1)S(1)}, u32[]{:S(2)}, u32[]{:S(2)}) collective-permute-start(bf16[1024,384]{1,0:T(8,128)(2,1)} %bitcast.11.own_ref), channel_id=1, source_target_pairs={{0,12},{4,0},{8,4},{12,8},{1,13},{5,1},{9,5},{13,9},{2,14},{6,2},{... | collective-permute-start | bytes 2359304 | tf_op jit(solution)/shard_map/ppermute | solution.py:19
  31.3 21.9 %collective-permute-start.2 = (bf16[1024,384]{1,0:T(8,128)(2,1)}, bf16[1024,384]{1,0:T(8,128)(2,1)S(1)}, u32[]{:S(2)}, u32[]{:S(2)}) collective-permute-start(bf16[1024,384]{1,0:T(8,128)(2,1)} %bitcast.11.own_ref), channel_id=1, source_target_pairs={{0,4},{4,8},{8,12},{12,0},{1,5},{5,9},{9,13},{13,1},{2,6},{6,10},{... | collective-permute-start | bytes 2359304 | tf_op jit(solution)/shard_map/ppermute | solution.py:19
  53.1 19.8 %collective-permute-start.4 = (bf16[1024,384]{1,0:T(8,128)(2,1)}, bf16[1024,384]{1,0:T(8,128)(2,1)S(1)}, u32[]{:S(2)}, u32[]{:S(2)}) collective-permute-start(bf16[1024,384]{1,0:T(8,128)(2,1)} %bitcast.30), channel_id=1, source_target_pairs={{0,12},{4,0},{8,4},{12,8},{1,13},{5,1},{9,5},{13,9},{2,14},{6,2},{... | collective-permute-start | bytes 2359304 | tf_op jit(solution)/shard_map/ppermute | solution.py:19
  55.0 21.3 %collective-permute-start.6 = (bf16[1024,384]{1,0:T(8,128)(2,1)}, bf16[1024,384]{1,0:T(8,128)(2,1)S(1)}, u32[]{:S(2)}, u32[]{:S(2)}) collective-permute-start(bf16[1024,384]{1,0:T(8,128)(2,1)} %bitcast.31), channel_id=1, source_target_pairs={{0,4},{4,8},{8,12},{12,0},{1,5},{5,9},{9,13},{13,1},{2,6},{6,10},{... | collective-permute-start | bytes 2359304 | tf_op jit(solution)/shard_map/ppermute | solution.py:19
  72.9 10.3 %copy-start.1 = (bf16[1024,384]{1,0:T(8,128)(2,1)}, bf16[1024,384]{1,0:T(8,128)(2,1)S(1)}, u32[]{:S(2)}) copy-start(bf16[1024,384]{1,0:T(8,128)(2,1)S(1)} %collective-permute-done.4.after_ref) | copy-start | bytes 2359300
  72.9 10.3 %collective-permute-start.5 = (bf16[512,384]{1,0:T(8,128)(2,1)S(1)}, bf16[512,384]{1,0:T(8,128)(2,1)S(1)}, u32[]{:S(2)}, u32[]{:S(2)}) collective-permute-start(bf16[512,384]{1,0:T(8,128)(2,1)S(1)} %slice.26), channel_id=1, source_target_pairs={{0,12},{4,0},{8,4},{12,8},{1,13},{5,1},{9,5},{13,9},{2,14},{6,2},{... | collective-permute-start | bytes 1179656 | tf_op jit(solution)/shard_map/ppermute | solution.py:19
  76.4 6.9 %copy-start.3 = (bf16[1024,384]{1,0:T(8,128)(2,1)}, bf16[1024,384]{1,0:T(8,128)(2,1)S(1)}, u32[]{:S(2)}) copy-start(bf16[1024,384]{1,0:T(8,128)(2,1)S(1)} %collective-permute-done.6.before_ref) | copy-start | bytes 2359300
  76.4 11.5 %collective-permute-start.7 = (bf16[512,384]{1,0:T(8,128)(2,1)S(1)}, bf16[512,384]{1,0:T(8,128)(2,1)S(1)}, u32[]{:S(2)}, u32[]{:S(2)}) collective-permute-start(bf16[512,384]{1,0:T(8,128)(2,1)S(1)} %slice.27), channel_id=1, source_target_pairs={{0,4},{4,8},{8,12},{12,0},{1,5},{5,9},{9,13},{13,1},{2,6},{6,10},{... | collective-permute-start | bytes 1179656 | tf_op jit(solution)/shard_map/ppermute | solution.py:19
  87.9 0.8 copy-start.7
  88.7 1.1 copy-start.2
  89.8 1.1 copy-start.4
  91.0 1.1 copy-start.5
  92.1 1.0 copy-start.8
  96.4 27.0 %all-to-all-start.3 = ((bf16[4,96,1024]{2,1,0:T(8,128)(2,1)}), bf16[4,96,1024]{2,1,0:T(8,128)(2,1)}, u32[]{:S(2)}, u32[]{:S(2)}) async-start(bf16[4,96,1024]{2,1,0:T(8,128)(2,1)} %bitcast.14), calls=%async_computation.3 | async-start | bytes 1572864 | tf_op jit(solution)/shard_map/all_to_all | solution.py:158
  105.5 9.3 %collective-permute-start.1 = (bf16[512,384]{1,0:T(8,128)(2,1)S(1)}, bf16[512,384]{1,0:T(8,128)(2,1)S(1)}, u32[]{:S(2)}, u32[]{:S(2)}) collective-permute-start(bf16[512,384]{1,0:T(8,128)(2,1)S(1)} %slice.24), channel_id=1, source_target_pairs={{0,12},{4,0},{8,4},{12,8},{1,13},{5,1},{9,5},{13,9},{2,14},{6,2},{... | collective-permute-start | bytes 1179656 | tf_op jit(solution)/shard_map/ppermute | solution.py:19
  107.5 10.5 %collective-permute-start.3 = (bf16[512,384]{1,0:T(8,128)(2,1)S(1)}, bf16[512,384]{1,0:T(8,128)(2,1)S(1)}, u32[]{:S(2)}, u32[]{:S(2)}) collective-permute-start(bf16[512,384]{1,0:T(8,128)(2,1)S(1)} %slice.25), channel_id=1, source_target_pairs={{0,4},{4,8},{8,12},{12,0},{1,5},{5,9},{9,13},{13,1},{2,6},{6,10},{... | collective-permute-start | bytes 1179656 | tf_op jit(solution)/shard_map/ppermute | solution.py:19
  122.5 6.5 %copy-start.6 = (bf16[1,1024,384]{2,1,0:T(8,128)(2,1)S(1)}, bf16[1,1024,384]{2,1,0:T(8,128)(2,1)}, u32[]{:S(2)}) copy-start(bf16[1,1024,384]{2,1,0:T(8,128)(2,1)} %param.11) | copy-start | bytes 2359300
  123.4 30.9 %all-to-all-start.2 = ((bf16[4,96,1024]{2,1,0:T(8,128)(2,1)}), bf16[4,96,1024]{2,1,0:T(8,128)(2,1)}, u32[]{:S(2)}, u32[]{:S(2)}) async-start(bf16[4,96,1024]{2,1,0:T(8,128)(2,1)} %bitcast.12), calls=%async_computation.2 | async-start | bytes 1572864 | tf_op jit(solution)/shard_map/all_to_all | solution.py:158
  129.0 16.4 %collective-permute-start.8 = (bf16[1024,384]{1,0:T(8,128)(2,1)S(1)}, bf16[1024,384]{1,0:T(8,128)(2,1)S(1)}, u32[]{:S(2)}, u32[]{:S(2)}) collective-permute-start(bf16[1024,384]{1,0:T(8,128)(2,1)S(1)} %bitcast.33), channel_id=1, source_target_pairs={{0,12},{4,0},{8,4},{12,8},{1,13},{5,1},{9,5},{13,9},{2,14},{6,2},{... | collective-permute-start | bytes 2359304 | tf_op jit(solution)/shard_map/ppermute | solution.py:19
  130.9 18.6 %collective-permute-start.10 = (bf16[1024,384]{1,0:T(8,128)(2,1)S(1)}, bf16[1024,384]{1,0:T(8,128)(2,1)S(1)}, u32[]{:S(2)}, u32[]{:S(2)}) collective-permute-start(bf16[1024,384]{1,0:T(8,128)(2,1)S(1)} %bitcast.34), channel_id=1, source_target_pairs={{0,4},{4,8},{8,12},{12,0},{1,5},{5,9},{9,13},{13,1},{2,6},{6,10},{... | collective-permute-start | bytes 2359304 | tf_op jit(solution)/shard_map/ppermute | solution.py:19
  146.1 25.5 %collective-permute-start.9 = (bf16[512,384]{1,0:T(8,128)(2,1)}, bf16[512,384]{1,0:T(8,128)(2,1)S(1)}, u32[]{:S(2)}, u32[]{:S(2)}) collective-permute-start(bf16[512,384]{1,0:T(8,128)(2,1)} %slice.28), channel_id=1, source_target_pairs={{0,12},{4,0},{8,4},{12,8},{1,13},{5,1},{9,5},{13,9},{2,14},{6,2},{... | collective-permute-start | bytes 1179656 | tf_op jit(solution)/shard_map/ppermute | solution.py:19
  150.4 21.2 %collective-permute-start.11 = (bf16[512,384]{1,0:T(8,128)(2,1)}, bf16[512,384]{1,0:T(8,128)(2,1)S(1)}, u32[]{:S(2)}, u32[]{:S(2)}) collective-permute-start(bf16[512,384]{1,0:T(8,128)(2,1)} %slice.29), channel_id=1, source_target_pairs={{0,4},{4,8},{8,12},{12,0},{1,5},{5,9},{9,13},{13,1},{2,6},{6,10},{... | collective-permute-start | bytes 1179656 | tf_op jit(solution)/shard_map/ppermute | solution.py:19
  154.3 1.4 copy-start.9
  205.8 17.7 %all-to-all-start.5 = ((bf16[4,48,384]{2,1,0:T(8,128)(2,1)}), bf16[4,48,384]{2,1,0:T(8,128)(2,1)S(1)}, u32[]{:S(2)}, u32[]{:S(2)}) async-start(bf16[4,48,384]{2,1,0:T(8,128)(2,1)} %reduce_sum.52), calls=%async_computation.5 | async-start | bytes 294912 | tf_op jit(solution)/shard_map/all_to_all | solution.py:177

commit v4 on v3

--- a/solution.py
+++ b/solution.py
@@ -29,48 +29,40 @@
     return shift(after[:half], "x", -1), shift(before[half:], "x", 1)
 
 
-def project_kernel(rows_ref, own_ref, after_ref, low_ref, high_ref, before_ref, out_ref):
-    in_low = pl.program_id(0) < pl.num_programs(0) // 2
-    opposite = jnp.where(in_low, low_ref[...], high_ref[...])
-    blocks = (own_ref[...], after_ref[...], opposite, before_ref[...])
-    sources, _, cap, depth = rows_ref.shape
-    total = None
-    for step, block in enumerate(blocks):
-        rows = rows_ref[:, step].reshape(sources * cap, depth)
-        term = lax.dot_general(
-            rows, block, (((1,), (1,)), ((), ())), preferred_element_type=jnp.float32
-        )
-        term = term.astype(jnp.bfloat16).astype(jnp.float32)
-        total = term if total is None else total + term
-    out_ref[...] = total.astype(jnp.bfloat16)
+def project_kernel(rows_ref, own_ref, after_ref, before_ref, *rest):
+    *opposite_refs, out_ref = rest
+    sources, blocks, cap, depth = rows_ref.shape
+    part = out_ref.shape[1] // len(opposite_refs)
+    rows = [rows_ref[:, step].reshape(sources * cap, depth) for step in range(blocks)]
+    for start in range(0, out_ref.shape[1], TILE):
+        tile = pl.ds(start, TILE)
+        opposite = opposite_refs[start // part][pl.ds(start % part, TILE), :]
+        total = None
+        for step, block in enumerate((own_ref[tile, :], after_ref[tile, :], opposite, before_ref[tile, :])):
+            term = lax.dot_general(
+                rows[step], block, (((1,), (1,)), ((), ())), preferred_element_type=jnp.float32
+            )
+            term = term.astype(jnp.bfloat16).astype(jnp.float32)
+            total = term if total is None else total + term
+        out_ref[:, tile] = total.astype(jnp.bfloat16)
 
 
-def project(rows, own, pair, halves):
+def project(rows, own, pair, opposite):
     sources, blocks, cap, depth = rows.shape
     width = own.shape[0]
-    steps = width // TILE
-    half = steps // 2
-    block = (TILE, depth)
+    vmem = pl.BlockSpec(memory_space=pltpu.VMEM)
     return pl.pallas_call(
         project_kernel,
         out_shape=jax.ShapeDtypeStruct((sources * cap, width), jnp.bfloat16),
-        grid=(steps,),
-        in_specs=[
-            pl.BlockSpec(rows.shape, lambda i: (0, 0, 0, 0)),
-            pl.BlockSpec(block, lambda i: (i, 0)),
-            pl.BlockSpec(block, lambda i: (i, 0)),
-            pl.BlockSpec(block, lambda i: (jnp.minimum(i, half - 1), 0)),
-            pl.BlockSpec(block, lambda i: (jnp.maximum(i - half, 0), 0)),
-            pl.BlockSpec(block, lambda i: (i, 0)),
-        ],
-        out_specs=pl.BlockSpec((sources * cap, TILE), lambda i: (0, i)),
+        in_specs=[vmem] * (4 + len(opposite)),
+        out_specs=vmem,
         compiler_params=pltpu.CompilerParams(vmem_limit_bytes=GRANT),
         cost_estimate=pl.CostEstimate(
             flops=2 * sources * cap * blocks * depth * width,
             bytes_accessed=2 * (rows.size + blocks * own.size + sources * cap * width),
             transcendentals=0,
         ),
-    )(rows, own, pair[0], *halves, pair[1])
+    )(rows, own, *pair, *opposite)
 
 
 def expand_kernel(order_ref, hidden_ref, own_ref, after_ref, low_ref, high_ref, before_ref, out_ref):
@@ -149,10 +141,7 @@
     gate_halves = across(gate_pair)
     up_own, _ = lax.optimization_barrier((w_up[0], gate_pair))
     up_pair = beside(up_own)
-    up_halves = across(up_pair)
-    down_own, _ = lax.optimization_barrier((w_down[0], up_pair))
-    down_pair = beside(down_own)
-    down_halves = across(down_pair)
+    up_across = (shift(up_own, "x", 2),)
 
     def share(term):
         parts = lax.all_to_all(term, "zh", split_axis=0, concat_axis=0, tiled=True)
@@ -161,7 +150,10 @@
 
     gate_term = project(rows, gate_own, gate_pair, gate_halves)
     gate_share = share(gate_term)
-    up_term = project(rows, up_own, up_pair, up_halves)
+    up_term = project(rows, up_own, up_pair, up_across)
+    down_own, up_term = lax.optimization_barrier((w_down[0], up_term))
+    down_pair = beside(down_own)
+    down_halves = across(down_pair)
     up_share = share(up_term)
     hidden = (jax.nn.silu(gate_share) * up_share).astype(jnp.bfloat16)
     hidden_rows = lax.all_gather(hidden, "zh", axis=0, tiled=True)

time: 226 us -> 225 us (level)
  blocking collectives: 46.8 us -> 50.8 us
  local copies, waits for them, and re-layouts: 9.15 us -> 5.65 us
  waiting for transfers between devices: 76.8 us -> 80.1 us
    ppermute x12 -> x11, waiting for transfers between devices: 61.3 us -> 65.5 us  [shift(): lax.ppermute(array, axis, [(i, (i + step) % size) for i in range(size)])]
    unnamed x20 -> x16, local copies, waits for them, and re-layouts: 5.18 us -> 1.78 us
    all_to_all x1, starting transfers between devices: 14 us -> 11.4 us  [on_device(): lax.all_to_all(back, LOCAL, split_axis=0, concat_axis=0, tiled=True)]
    ppermute x12 -> x11, starting transfers between devices: 31.7 us -> 31.8 us  [shift(): lax.ppermute(array, axis, [(i, (i + step) % size) for i in range(size)])]
  transfers between devices with their start and end apart: 17 -> 16, of which waited for: 11 -> 9; matrix products, arithmetic and copies ran while one was open for 2% -> 2% of each run, Pallas kernels for 2% -> 1%
where the time goes in v4:
time: 225 us; the launch traced here: 224 us
  waiting for transfers between devices  80.1 us (36%)
  starting transfers between devices  73.4 us (33%)
  blocking collectives  50.8 us (23%)
  Pallas kernels  8.94 us (4%)
  local copies, waits for them, and re-layouts  5.65 us (3%)
  other arithmetic  4.21 us (2%)
    ppermute x11, waiting for transfers between devices, shift(): lax.ppermute(array, axis, [(i, (i + step) % size) for i in range(size)])  65.5 us
    all_to_all x1, blocking collectives, on_device(): lax.all_to_all(back.reshape(y_size * x_size, CAP, width_part), ('y', 'x')...  32.8 us
    ppermute x11, starting transfers between devices, shift(): lax.ppermute(array, axis, [(i, (i + step) % size) for i in range(size)])  31.8 us
    all_gather x1, blocking collectives, on_device(): hidden_rows = lax.all_gather(hidden, 'zh', axis=0, tiled=True)  18 us
    all_to_all x2, starting transfers between devices, share(): parts = lax.all_to_all(term, 'zh', split_axis=0, concat_axis=0, tiled=True)  15.7 us
    all_to_all x1, starting transfers between devices, on_device(): lax.all_to_all(back, LOCAL, split_axis=0, concat_axis=0, tiled=True)  11.4 us
    all_to_all x1, waiting for transfers between devices, on_device(): lax.all_to_all(sent.reshape(EXPERTS * x_size, CAP, width_part), LOCAL + (...  10.9 us
    all_to_all x1, starting transfers between devices, on_device(): lax.all_to_all(sent.reshape(EXPERTS * x_size, CAP, width_part), LOCAL + (...  10.2 us
  transfers between devices with their start and end apart: 16, of which 9 were waited for; matrix products, arithmetic and copies ran while one was open for 2% of the time, Pallas kernels for 1%

profile of v4, /device:TPU:1, one launch (start us, length us, event | category | flops | bytes accessed | tf_op | source)
XLA Modules:
  0.0 224.5 jit_solution(1797821440837210491)
XLA Ops:
  2.2 10.2 %all-to-all-start = ((bf16[16,48,384]{2,1,0:T(8,128)(2,1)}), bf16[16,48,384]{2,1,0:T(8,128)(2,1)S(1)}, u32[]{:S(2)}, u32[]{:S(2)}) async-start(bf16[16,48,384]{2,1,0:T(8,128)(2,1)} %bitcast.5), calls=%async_computation | async-start | bytes 1179648 | tf_op jit(solution)/shard_map/all_to_all | solution.py:125
  12.4 10.9 %all-to-all-done = bf16[16,48,384]{2,1,0:T(8,128)(2,1)S(1)} async-done(((bf16[16,48,384]{2,1,0:T(8,128)(2,1)}), bf16[16,48,384]{2,1,0:T(8,128)(2,1)S(1)}, u32[]{:S(2)}, u32[]{:S(2)}) %all-to-all-start) | async-done | bytes 589856 | tf_op jit(solution)/shard_map/all_to_all | solution.py:125
  23.4 1.1 broadcast_in_dim.19
  24.5 4.1 %all-to-all-start.1 = ((bf16[8,4,48,384]{3,2,1,0:T(8,128)(2,1)}), bf16[8,4,48,384]{3,2,1,0:T(8,128)(2,1)S(1)}, u32[]{:S(2)}, u32[]{:S(2)}) async-start(bf16[8,4,48,384]{3,2,1,0:T(8,128)(2,1)} %broadcast_in_dim.19), calls=%async_computation.1 | async-start | bytes 2359296 | tf_op jit(solution)/shard_map/all_to_all | solution.py:136
  28.7 2.6 %collective-permute-start = (bf16[1024,384]{1,0:T(8,128)(2,1)}, bf16[1024,384]{1,0:T(8,128)(2,1)S(1)}, u32[]{:S(2)}, u32[]{:S(2)}) collective-permute-start(bf16[1024,384]{1,0:T(8,128)(2,1)} %bitcast.11.own_ref), channel_id=1, source_target_pairs={{0,12},{4,0},{8,4},{12,8},{1,13},{5,1},{9,5},{13,9},{2,14},{6,2},{... | collective-permute-start | bytes 2359304 | tf_op jit(solution)/shard_map/ppermute | solution.py:19
  31.2 2.7 %collective-permute-start.1 = (bf16[1024,384]{1,0:T(8,128)(2,1)}, bf16[1024,384]{1,0:T(8,128)(2,1)S(1)}, u32[]{:S(2)}, u32[]{:S(2)}) collective-permute-start(bf16[1024,384]{1,0:T(8,128)(2,1)} %bitcast.11.own_ref), channel_id=1, source_target_pairs={{0,4},{4,8},{8,12},{12,0},{1,5},{5,9},{9,13},{13,1},{2,6},{6,10},{... | collective-permute-start | bytes 2359304 | tf_op jit(solution)/shard_map/ppermute | solution.py:19
  34.0 15.1 %collective-permute-done.after_ref = bf16[1024,384]{1,0:T(8,128)(2,1)S(1)} collective-permute-done((bf16[1024,384]{1,0:T(8,128)(2,1)}, bf16[1024,384]{1,0:T(8,128)(2,1)S(1)}, u32[]{:S(2)}, u32[]{:S(2)}) %collective-permute-start) | collective-permute-done | bytes 786464 | tf_op jit(solution)/shard_map/ppermute | solution.py:19
  49.1 4.3 %collective-permute-start.2 = (bf16[512,384]{1,0:T(8,128)(2,1)S(1)}, bf16[512,384]{1,0:T(8,128)(2,1)S(1)}, u32[]{:S(2)}, u32[]{:S(2)}) collective-permute-start(bf16[512,384]{1,0:T(8,128)(2,1)S(1)} %slice.16), channel_id=1, source_target_pairs={{0,12},{4,0},{8,4},{12,8},{1,13},{5,1},{9,5},{13,9},{2,14},{6,2},{... | collective-permute-start | bytes 1179656 | tf_op jit(solution)/shard_map/ppermute | solution.py:19
  53.5 1.9 collective-permute-start.3
  55.4 5.3 %collective-permute-done.2.rest_0_ = bf16[512,384]{1,0:T(8,128)(2,1)S(1)} collective-permute-done((bf16[512,384]{1,0:T(8,128)(2,1)S(1)}, bf16[512,384]{1,0:T(8,128)(2,1)S(1)}, u32[]{:S(2)}, u32[]{:S(2)}) %collective-permute-start.2) | collective-permute-done | bytes 393248 | tf_op jit(solution)/shard_map/ppermute | solution.py:19
  60.7 5.1 %collective-permute-done.3.rest_1_ = bf16[512,384]{1,0:T(8,128)(2,1)S(1)} collective-permute-done((bf16[512,384]{1,0:T(8,128)(2,1)S(1)}, bf16[512,384]{1,0:T(8,128)(2,1)S(1)}, u32[]{:S(2)}, u32[]{:S(2)}) %collective-permute-start.3) | collective-permute-done | bytes 393248 | tf_op jit(solution)/shard_map/ppermute | solution.py:19
  67.6 3.9 %shard_map.64 = bf16[384,1024]{1,0:T(8,128)(2,1)} custom-call(bf16[8,4,48,384]{3,2,1,0:T(8,128)(2,1)S(1)} %all-to-all-done.1.rows_ref, bf16[1024,384]{1,0:T(8,128)(2,1)} %bitcast.11.own_ref, bf16[1024,384]{1,0:T(8,128)(2,1)S(1)} %collective-permute-done.after_ref, bf16[1024,384]{1,0:T(8,128)(2,1)S(1)} %collective-permute-done.1.before_ref, ...), custom_call_target="tpu_custom_call" | custom-call | flops 1207959552 | bytes 5111808 | tf_op jit(solution)/shard_map/pallas_call | solution.py:54
  71.5 9.2 %all-to-all-start.2 = ((bf16[4,96,1024]{2,1,0:T(8,128)(2,1)}), bf16[4,96,1024]{2,1,0:T(8,128)(2,1)S(1)}, u32[]{:S(2)}, u32[]{:S(2)}) async-start(bf16[4,96,1024]{2,1,0:T(8,128)(2,1)} %bitcast.12), calls=%async_computation.2 | async-start | bytes 1572864 | tf_op jit(solution)/shard_map/all_to_all | solution.py:147
  80.8 1.9 collective-permute-start.4
  82.7 3.4 %collective-permute-start.5 = (bf16[1024,384]{1,0:T(8,128)(2,1)S(1)}, bf16[1024,384]{1,0:T(8,128)(2,1)S(1)}, u32[]{:S(2)}, u32[]{:S(2)}) collective-permute-start(bf16[1024,384]{1,0:T(8,128)(2,1)S(1)} %bitcast.31), channel_id=1, source_target_pairs={{0,4},{4,8},{8,12},{12,0},{1,5},{5,9},{9,13},{13,1},{2,6},{6,10},{... | collective-permute-start | bytes 2359304 | tf_op jit(solution)/shard_map/ppermute | solution.py:19
  86.0 1.9 collective-permute-start.6
  88.0 11.2 %collective-permute-done.4.after_ref = bf16[1024,384]{1,0:T(8,128)(2,1)S(1)} collective-permute-done((bf16[1024,384]{1,0:T(8,128)(2,1)S(1)}, bf16[1024,384]{1,0:T(8,128)(2,1)S(1)}, u32[]{:S(2)}, u32[]{:S(2)}) %collective-permute-start.4) | collective-permute-done | bytes 786464 | tf_op jit(solution)/shard_map/ppermute | solution.py:19
  99.2 4.7 %collective-permute-done.5.before_ref = bf16[1024,384]{1,0:T(8,128)(2,1)S(1)} collective-permute-done((bf16[1024,384]{1,0:T(8,128)(2,1)S(1)}, bf16[1024,384]{1,0:T(8,128)(2,1)S(1)}, u32[]{:S(2)}, u32[]{:S(2)}) %collective-permute-start.5) | collective-permute-done | bytes 786464 | tf_op jit(solution)/shard_map/ppermute | solution.py:19
  103.8 13.9 %collective-permute-done.6.rest_0_ = bf16[1024,384]{1,0:T(8,128)(2,1)S(1)} collective-permute-done((bf16[1024,384]{1,0:T(8,128)(2,1)S(1)}, bf16[1024,384]{1,0:T(8,128)(2,1)S(1)}, u32[]{:S(2)}, u32[]{:S(2)}) %collective-permute-start.6) | collective-permute-done | bytes 786464 | tf_op jit(solution)/shard_map/ppermute | solution.py:19
  117.7 2.7 %shard_map.65 = bf16[384,1024]{1,0:T(8,128)(2,1)} custom-call(bf16[8,4,48,384]{3,2,1,0:T(8,128)(2,1)S(1)} %all-to-all-done.1.rows_ref, bf16[1024,384]{1,0:T(8,128)(2,1)S(1)} %bitcast.33, bf16[1024,384]{1,0:T(8,128)(2,1)S(1)} %collective-permute-done.4.after_ref, bf16[1024,384]{1,0:T(8,128)(2,1)S(1)} %collective-permute-done.5.before_ref, ...), custom_call_target="tpu_custom_call" | custom-call | flops 1207959552 | bytes 5111808 | tf_op jit(solution)/shard_map/pallas_call | solution.py:54
  120.4 6.5 %all-to-all-start.3 = ((bf16[4,96,1024]{2,1,0:T(8,128)(2,1)}), bf16[4,96,1024]{2,1,0:T(8,128)(2,1)}, u32[]{:S(2)}, u32[]{:S(2)}) async-start(bf16[4,96,1024]{2,1,0:T(8,128)(2,1)} %bitcast.15), calls=%async_computation.3 | async-start | bytes 1572864 | tf_op jit(solution)/shard_map/all_to_all | solution.py:147
  126.9 1.9 collective-permute-start.9
  128.8 4.6 %collective-permute-start.7 = (bf16[1024,384]{1,0:T(8,128)(2,1)S(1)}, bf16[1024,384]{1,0:T(8,128)(2,1)S(1)}, u32[]{:S(2)}, u32[]{:S(2)}) collective-permute-start(bf16[1024,384]{1,0:T(8,128)(2,1)S(1)} %bitcast.35), channel_id=1, source_target_pairs={{0,12},{4,0},{8,4},{12,8},{1,13},{5,1},{9,5},{13,9},{2,14},{6,2},{... | collective-permute-start | bytes 2359304 | tf_op jit(solution)/shard_map/ppermute | solution.py:19
  133.5 10.3 %collective-permute-done.9.before_ref = bf16[1024,384]{1,0:T(8,128)(2,1)S(1)} collective-permute-done((bf16[1024,384]{1,0:T(8,128)(2,1)S(1)}, bf16[1024,384]{1,0:T(8,128)(2,1)S(1)}, u32[]{:S(2)}, u32[]{:S(2)}) %collective-permute-start.9) | collective-permute-done | bytes 786464 | tf_op jit(solution)/shard_map/ppermute | solution.py:19
  144.6 2.3 %collective-permute-start.10 = (bf16[512,384]{1,0:T(8,128)(2,1)}, bf16[512,384]{1,0:T(8,128)(2,1)S(1)}, u32[]{:S(2)}, u32[]{:S(2)}) collective-permute-start(bf16[512,384]{1,0:T(8,128)(2,1)} %slice.19), channel_id=1, source_target_pairs={{0,4},{4,8},{8,12},{12,0},{1,5},{5,9},{9,13},{13,1},{2,6},{6,10},{... | collective-permute-start | bytes 1179656 | tf_op jit(solution)/shard_map/ppermute | solution.py:19
  147.7 4.3 %collective-permute-start.8 = (bf16[512,384]{1,0:T(8,128)(2,1)}, bf16[512,384]{1,0:T(8,128)(2,1)S(1)}, u32[]{:S(2)}, u32[]{:S(2)}) collective-permute-start(bf16[512,384]{1,0:T(8,128)(2,1)} %slice.18), channel_id=1, source_target_pairs={{0,12},{4,0},{8,4},{12,8},{1,13},{5,1},{9,5},{13,9},{2,14},{6,2},{... | collective-permute-start | bytes 1179656 | tf_op jit(solution)/shard_map/ppermute | solution.py:19
  152.9 1.3 convert_reduce_fusion
  154.4 18.0 %all_gather.3.hidden_ref = bf16[384,1024]{1,0:T(8,128)(2,1)S(1)} all-gather(bf16[96,1024]{1,0:T(8,128)(2,1)S(1)} %multiply_convert_fusion), channel_id=1, replica_groups=mesh['y'=8,'zl'=2,'core'=2,'x'=4,'zh'=4] {'zh'}, dimensions={0}, use_global_device_ids=true | all-gather | bytes 983040 | tf_op jit(solution)/shard_map/all_gather | solution.py:159
  172.4 2.3 %shard_map.66 = bf16[8,4,48,384]{3,2,1,0:T(8,128)(2,1)S(1)} custom-call(s32[4]{0:T(128)S(1)} %pad_add_fusion.order_ref, bf16[384,1024]{1,0:T(8,128)(2,1)S(1)} %all_gather.3.hidden_ref, bf16[1024,384]{1,0:T(8,128)(2,1)S(1)} %bitcast.36, bf16[1024,384]{1,0:T(8,128)(2,1)S(1)} %collective-permute-done.7.after_ref, ...), custom_call_target="tpu_custom_call" | custom-call | flops 1207959552 | bytes 5111808 | tf_op jit(solution)/shard_map/pallas_call | solution.py:92
  174.7 32.8 %all_to_all.38 = bf16[32,48,384]{2,1,0:T(8,128)(2,1)S(1)} all-to-all(bf16[32,48,384]{2,1,0:T(8,128)(2,1)S(1)} %bitcast.29), channel_id=1, replica_groups=mesh['y'=8,'zl'=2,'core'=2,'x'=4,'zh'=4] {'y','x'}, dimensions={0} | all-to-all | bytes 2359296 | tf_op jit(solution)/shard_map/all_to_all | solution.py:161
  208.3 11.4 %all-to-all-start.5 = ((bf16[4,48,384]{2,1,0:T(8,128)(2,1)}), bf16[4,48,384]{2,1,0:T(8,128)(2,1)S(1)}, u32[]{:S(2)}, u32[]{:S(2)}) async-start(bf16[4,48,384]{2,1,0:T(8,128)(2,1)} %reduce_sum.52), calls=%async_computation.5 | async-start | bytes 294912 | tf_op jit(solution)/shard_map/all_to_all | solution.py:169
  219.8 3.7 %all-to-all-done.5 = bf16[4,48,384]{2,1,0:T(8,128)(2,1)S(1)} async-done(((bf16[4,48,384]{2,1,0:T(8,128)(2,1)}), bf16[4,48,384]{2,1,0:T(8,128)(2,1)S(1)}, u32[]{:S(2)}, u32[]{:S(2)}) %all-to-all-start.5) | async-done | bytes 147488 | tf_op jit(solution)/shard_map/all_to_all | solution.py:169
  (43 shorter events, 8.6 us)
Async XLA Ops:
  0.0 1.1 copy-start
  2.2 21.1 %all-to-all-start = ((bf16[16,48,384]{2,1,0:T(8,128)(2,1)}), bf16[16,48,384]{2,1,0:T(8,128)(2,1)S(1)}, u32[]{:S(2)}, u32[]{:S(2)}) async-start(bf16[16,48,384]{2,1,0:T(8,128)(2,1)} %bitcast.5), calls=%async_computation | async-start | bytes 1179648 | tf_op jit(solution)/shard_map/all_to_all | solution.py:125
  24.5 42.1 %all-to-all-start.1 = ((bf16[8,4,48,384]{3,2,1,0:T(8,128)(2,1)}), bf16[8,4,48,384]{3,2,1,0:T(8,128)(2,1)S(1)}, u32[]{:S(2)}, u32[]{:S(2)}) async-start(bf16[8,4,48,384]{3,2,1,0:T(8,128)(2,1)} %broadcast_in_dim.19), calls=%async_computation.1 | async-start | bytes 2359296 | tf_op jit(solution)/shard_map/all_to_all | solution.py:136
  28.7 20.4 %collective-permute-start = (bf16[1024,384]{1,0:T(8,128)(2,1)}, bf16[1024,384]{1,0:T(8,128)(2,1)S(1)}, u32[]{:S(2)}, u32[]{:S(2)}) collective-permute-start(bf16[1024,384]{1,0:T(8,128)(2,1)} %bitcast.11.own_ref), channel_id=1, source_target_pairs={{0,12},{4,0},{8,4},{12,8},{1,13},{5,1},{9,5},{13,9},{2,14},{6,2},{... | collective-permute-start | bytes 2359304 | tf_op jit(solution)/shard_map/ppermute | solution.py:19
  31.2 22.2 %collective-permute-start.1 = (bf16[1024,384]{1,0:T(8,128)(2,1)}, bf16[1024,384]{1,0:T(8,128)(2,1)S(1)}, u32[]{:S(2)}, u32[]{:S(2)}) collective-permute-start(bf16[1024,384]{1,0:T(8,128)(2,1)} %bitcast.11.own_ref), channel_id=1, source_target_pairs={{0,4},{4,8},{8,12},{12,0},{1,5},{5,9},{9,13},{13,1},{2,6},{6,10},{... | collective-permute-start | bytes 2359304 | tf_op jit(solution)/shard_map/ppermute | solution.py:19
  49.1 11.7 %collective-permute-start.2 = (bf16[512,384]{1,0:T(8,128)(2,1)S(1)}, bf16[512,384]{1,0:T(8,128)(2,1)S(1)}, u32[]{:S(2)}, u32[]{:S(2)}) collective-permute-start(bf16[512,384]{1,0:T(8,128)(2,1)S(1)} %slice.16), channel_id=1, source_target_pairs={{0,12},{4,0},{8,4},{12,8},{1,13},{5,1},{9,5},{13,9},{2,14},{6,2},{... | collective-permute-start | bytes 1179656 | tf_op jit(solution)/shard_map/ppermute | solution.py:19
  53.5 12.4 %collective-permute-start.3 = (bf16[512,384]{1,0:T(8,128)(2,1)S(1)}, bf16[512,384]{1,0:T(8,128)(2,1)S(1)}, u32[]{:S(2)}, u32[]{:S(2)}) collective-permute-start(bf16[512,384]{1,0:T(8,128)(2,1)S(1)} %slice.17), channel_id=1, source_target_pairs={{0,4},{4,8},{8,12},{12,0},{1,5},{5,9},{9,13},{13,1},{2,6},{6,10},{... | collective-permute-start | bytes 1179656 | tf_op jit(solution)/shard_map/ppermute | solution.py:19
  65.9 0.8 copy-start.3
  66.6 1.0 copy-start.4
  71.5 9.3 %copy-start.1 = (bf16[1,1024,384]{2,1,0:T(8,128)(2,1)S(1)}, bf16[1,1024,384]{2,1,0:T(8,128)(2,1)}, u32[]{:S(2)}) copy-start(bf16[1,1024,384]{2,1,0:T(8,128)(2,1)} %param.10) | copy-start | bytes 2359300
  71.5 48.9 %all-to-all-start.2 = ((bf16[4,96,1024]{2,1,0:T(8,128)(2,1)}), bf16[4,96,1024]{2,1,0:T(8,128)(2,1)S(1)}, u32[]{:S(2)}, u32[]{:S(2)}) async-start(bf16[4,96,1024]{2,1,0:T(8,128)(2,1)} %bitcast.12), calls=%async_computation.2 | async-start | bytes 1572864 | tf_op jit(solution)/shard_map/all_to_all | solution.py:147
  80.8 18.4 %collective-permute-start.4 = (bf16[1024,384]{1,0:T(8,128)(2,1)S(1)}, bf16[1024,384]{1,0:T(8,128)(2,1)S(1)}, u32[]{:S(2)}, u32[]{:S(2)}) collective-permute-start(bf16[1024,384]{1,0:T(8,128)(2,1)S(1)} %bitcast.30), channel_id=1, source_target_pairs={{0,12},{4,0},{8,4},{12,8},{1,13},{5,1},{9,5},{13,9},{2,14},{6,2},{... | collective-permute-start | bytes 2359304 | tf_op jit(solution)/shard_map/ppermute | solution.py:19
  82.7 21.2 %collective-permute-start.5 = (bf16[1024,384]{1,0:T(8,128)(2,1)S(1)}, bf16[1024,384]{1,0:T(8,128)(2,1)S(1)}, u32[]{:S(2)}, u32[]{:S(2)}) collective-permute-start(bf16[1024,384]{1,0:T(8,128)(2,1)S(1)} %bitcast.31), channel_id=1, source_target_pairs={{0,4},{4,8},{8,12},{12,0},{1,5},{5,9},{9,13},{13,1},{2,6},{6,10},{... | collective-permute-start | bytes 2359304 | tf_op jit(solution)/shard_map/ppermute | solution.py:19
  86.0 31.7 %collective-permute-start.6 = (bf16[1024,384]{1,0:T(8,128)(2,1)S(1)}, bf16[1024,384]{1,0:T(8,128)(2,1)S(1)}, u32[]{:S(2)}, u32[]{:S(2)}) collective-permute-start(bf16[1024,384]{1,0:T(8,128)(2,1)S(1)} %bitcast.32), channel_id=1, source_target_pairs={{0,8},{4,12},{8,0},{12,4},{1,9},{5,13},{9,1},{13,5},{2,10},{6,14},... | collective-permute-start | bytes 2359304 | tf_op jit(solution)/shard_map/ppermute | solution.py:19
  120.4 6.5 %copy-start.2 = (bf16[1,1024,384]{2,1,0:T(8,128)(2,1)S(1)}, bf16[1,1024,384]{2,1,0:T(8,128)(2,1)}, u32[]{:S(2)}) copy-start(bf16[1,1024,384]{2,1,0:T(8,128)(2,1)} %param.11) | copy-start | bytes 2359300
  120.4 23.3 %copy-start.5 = (bf16[4,96,1024]{2,1,0:T(8,128)(2,1)}, bf16[4,96,1024]{2,1,0:T(8,128)(2,1)S(1)}, u32[]{:S(2)}) copy-start(bf16[4,96,1024]{2,1,0:T(8,128)(2,1)S(1)} %all-to-all-done.2) | copy-start | bytes 2359300
  120.4 32.4 %all-to-all-start.3 = ((bf16[4,96,1024]{2,1,0:T(8,128)(2,1)}), bf16[4,96,1024]{2,1,0:T(8,128)(2,1)}, u32[]{:S(2)}, u32[]{:S(2)}) async-start(bf16[4,96,1024]{2,1,0:T(8,128)(2,1)} %bitcast.15), calls=%async_computation.3 | async-start | bytes 1572864 | tf_op jit(solution)/shard_map/all_to_all | solution.py:147
  126.9 16.8 %collective-permute-start.9 = (bf16[1024,384]{1,0:T(8,128)(2,1)S(1)}, bf16[1024,384]{1,0:T(8,128)(2,1)S(1)}, u32[]{:S(2)}, u32[]{:S(2)}) collective-permute-start(bf16[1024,384]{1,0:T(8,128)(2,1)S(1)} %bitcast.34), channel_id=1, source_target_pairs={{0,4},{4,8},{8,12},{12,0},{1,5},{5,9},{9,13},{13,1},{2,6},{6,10},{... | collective-permute-start | bytes 2359304 | tf_op jit(solution)/shard_map/ppermute | solution.py:19
  128.8 18.1 %collective-permute-start.7 = (bf16[1024,384]{1,0:T(8,128)(2,1)S(1)}, bf16[1024,384]{1,0:T(8,128)(2,1)S(1)}, u32[]{:S(2)}, u32[]{:S(2)}) collective-permute-start(bf16[1024,384]{1,0:T(8,128)(2,1)S(1)} %bitcast.35), channel_id=1, source_target_pairs={{0,12},{4,0},{8,4},{12,8},{1,13},{5,1},{9,5},{13,9},{2,14},{6,2},{... | collective-permute-start | bytes 2359304 | tf_op jit(solution)/shard_map/ppermute | solution.py:19
  144.6 7.4 %copy-start.6 = (bf16[4,96,1024]{2,1,0:T(8,128)(2,1)S(1)}, bf16[4,96,1024]{2,1,0:T(8,128)(2,1)}, u32[]{:S(2)}) copy-start(bf16[4,96,1024]{2,1,0:T(8,128)(2,1)} %copy-done.5) | copy-start | bytes 2359300
  144.6 27.8 %collective-permute-start.10 = (bf16[512,384]{1,0:T(8,128)(2,1)}, bf16[512,384]{1,0:T(8,128)(2,1)S(1)}, u32[]{:S(2)}, u32[]{:S(2)}) collective-permute-start(bf16[512,384]{1,0:T(8,128)(2,1)} %slice.19), channel_id=1, source_target_pairs={{0,4},{4,8},{8,12},{12,0},{1,5},{5,9},{9,13},{13,1},{2,6},{6,10},{... | collective-permute-start | bytes 1179656 | tf_op jit(solution)/shard_map/ppermute | solution.py:19
  147.7 24.6 %collective-permute-start.8 = (bf16[512,384]{1,0:T(8,128)(2,1)}, bf16[512,384]{1,0:T(8,128)(2,1)S(1)}, u32[]{:S(2)}, u32[]{:S(2)}) collective-permute-start(bf16[512,384]{1,0:T(8,128)(2,1)} %slice.18), channel_id=1, source_target_pairs={{0,12},{4,0},{8,4},{12,8},{1,13},{5,1},{9,5},{13,9},{2,14},{6,2},{... | collective-permute-start | bytes 1179656 | tf_op jit(solution)/shard_map/ppermute | solution.py:19
  152.9 1.4 copy-start.7
  208.3 15.1 %all-to-all-start.5 = ((bf16[4,48,384]{2,1,0:T(8,128)(2,1)}), bf16[4,48,384]{2,1,0:T(8,128)(2,1)S(1)}, u32[]{:S(2)}, u32[]{:S(2)}) async-start(bf16[4,48,384]{2,1,0:T(8,128)(2,1)} %reduce_sum.52), calls=%async_computation.5 | async-start | bytes 294912 | tf_op jit(solution)/shard_map/all_to_all | solution.py:169

commit v5 on v4

--- a/solution.py
+++ b/solution.py
@@ -30,21 +30,36 @@
 
 
 def project_kernel(rows_ref, own_ref, after_ref, before_ref, *rest):
-    *opposite_refs, out_ref = rest
+    *opposite_refs, out_ref, held, sems = rest
     sources, blocks, cap, depth = rows_ref.shape
-    part = out_ref.shape[1] // len(opposite_refs)
-    rows = [rows_ref[:, step].reshape(sources * cap, depth) for step in range(blocks)]
-    for start in range(0, out_ref.shape[1], TILE):
-        tile = pl.ds(start, TILE)
-        opposite = opposite_refs[start // part][pl.ds(start % part, TILE), :]
+    tiles = out_ref.shape[1] // TILE
+    part = tiles // len(opposite_refs)
+    copies = []
+    for tile in range(tiles):
+        near = pl.ds(tile * TILE, TILE)
+        opposite = opposite_refs[tile // part].at[pl.ds(tile % part * TILE, TILE), :]
+        views = (own_ref.at[near, :], after_ref.at[near, :], opposite, before_ref.at[near, :])
+        copies.append(
+            [
+                pltpu.make_async_copy(view, held.at[tile, step], sems.at[tile, step])
+                for step, view in enumerate(views)
+            ]
+        )
+        for copy in copies[-1]:
+            copy.start()
+    for tile in range(tiles):
         total = None
-        for step, block in enumerate((own_ref[tile, :], after_ref[tile, :], opposite, before_ref[tile, :])):
+        for step in range(blocks):
+            copies[tile][step].wait()
             term = lax.dot_general(
-                rows[step], block, (((1,), (1,)), ((), ())), preferred_element_type=jnp.float32
+                rows_ref[:, step].reshape(sources * cap, depth),
+                held[tile, step],
+                (((1,), (1,)), ((), ())),
+                preferred_element_type=jnp.float32,
             )
             term = term.astype(jnp.bfloat16).astype(jnp.float32)
             total = term if total is None else total + term
-        out_ref[:, tile] = total.astype(jnp.bfloat16)
+        out_ref[:, pl.ds(tile * TILE, TILE)] = total.astype(jnp.bfloat16)
 
 
 def project(rows, own, pair, opposite):
@@ -54,8 +69,14 @@
     return pl.pallas_call(
         project_kernel,
         out_shape=jax.ShapeDtypeStruct((sources * cap, width), jnp.bfloat16),
-        in_specs=[vmem] * (4 + len(opposite)),
+        in_specs=[vmem]
+        + [pl.BlockSpec(memory_space=pl.ANY)] * 3
+        + [pl.BlockSpec(memory_space=pltpu.HBM)] * len(opposite),
         out_specs=vmem,
+        scratch_shapes=[
+            pltpu.VMEM((width // TILE, blocks, TILE, depth), jnp.bfloat16),
+            pltpu.SemaphoreType.DMA((width // TILE, blocks)),
+        ],
         compiler_params=pltpu.CompilerParams(vmem_limit_bytes=GRANT),
         cost_estimate=pl.CostEstimate(
             flops=2 * sources * cap * blocks * depth * width,
@@ -65,25 +86,15 @@
     )(rows, own, *pair, *opposite)
 
 
-def expand_kernel(order_ref, hidden_ref, own_ref, after_ref, low_ref, high_ref, before_ref, out_ref):
+def expand_kernel(order_ref, hidden_ref, own_ref, after_ref, before_ref, across_ref, out_ref):
     sources, _, cap, width = out_ref.shape
-    half = low_ref.shape[0]
     hidden = hidden_ref[...]
-
-    def put(step, value):
-        value = value.astype(jnp.bfloat16).reshape(sources, cap, width)
-        out_ref[:, order_ref[step]] = value
-
-    def dot(left, right):
-        return jnp.dot(left, right, preferred_element_type=jnp.float32)
-
-    put(0, dot(hidden, own_ref[...]))
-    put(1, dot(hidden, after_ref[...]))
-    put(3, dot(hidden, before_ref[...]))
-    put(2, dot(hidden[:, :half], low_ref[...]) + dot(hidden[:, half:], high_ref[...]))
-
-
-def expand(order, hidden, own, pair, halves, sources):
+    for step, block in ((0, own_ref), (1, after_ref), (3, before_ref), (2, across_ref)):
+        term = jnp.dot(hidden, block[...], preferred_element_type=jnp.float32)
+        out_ref[:, order_ref[step]] = term.astype(jnp.bfloat16).reshape(sources, cap, width)
+
+
+def expand(order, hidden, own, pair, opposite, sources):
     rows, width = hidden.shape
     depth = own.shape[1]
     cap = rows // sources
@@ -92,7 +103,7 @@
     return pl.pallas_call(
         expand_kernel,
         out_shape=jax.ShapeDtypeStruct((sources, places, cap, depth), jnp.bfloat16),
-        in_specs=[pl.BlockSpec(memory_space=pltpu.SMEM)] + [vmem] * 6,
+        in_specs=[pl.BlockSpec(memory_space=pltpu.SMEM)] + [vmem] * 5,
         out_specs=vmem,
         compiler_params=pltpu.CompilerParams(vmem_limit_bytes=GRANT),
         cost_estimate=pl.CostEstimate(
@@ -100,7 +111,7 @@
             bytes_accessed=2 * (hidden.size + places * own.size + places * rows * depth),
             transcendentals=0,
         ),
-    )(order, hidden, own, pair[0], *halves, pair[1])
+    )(order, hidden, own, *pair, *opposite)
 
 
 def on_device(tokens, expert_ids, gate_fixed, w_gate, w_up, w_down):
@@ -141,7 +152,8 @@
     gate_halves = across(gate_pair)
     up_own, _ = lax.optimization_barrier((w_up[0], gate_pair))
     up_pair = beside(up_own)
-    up_across = (shift(up_own, "x", 2),)
+    up_last, _ = lax.optimization_barrier((w_up[0], gate_halves))
+    up_across = (shift(up_last, "x", 2),)
 
     def share(term):
         parts = lax.all_to_all(term, "zh", split_axis=0, concat_axis=0, tiled=True)
@@ -153,11 +165,11 @@
     up_term = project(rows, up_own, up_pair, up_across)
     down_own, up_term = lax.optimization_barrier((w_down[0], up_term))
     down_pair = beside(down_own)
-    down_halves = across(down_pair)
+    down_across = (shift(down_own, "x", 2),)
     up_share = share(up_term)
     hidden = (jax.nn.silu(gate_share) * up_share).astype(jnp.bfloat16)
     hidden_rows = lax.all_gather(hidden, "zh", axis=0, tiled=True)
-    back = expand(jnp.stack(order), hidden_rows, down_own, down_pair, down_halves, y_size)
+    back = expand(jnp.stack(order), hidden_rows, down_own, down_pair, down_across, y_size)
     back = lax.all_to_all(
         back.reshape(y_size * x_size, CAP, width_part),
         ("y", "x"),

time: 225 us -> 241 us (1.071)
  Pallas kernels: 8.94 us -> 23.9 us
  starting transfers between devices: 73.4 us -> 67.5 us
  local copies, waits for them, and re-layouts: 5.65 us -> 11.3 us
    pallas_call x2, Pallas kernels: 6.6 us -> 21.5 us  [project(): pl.pallas_call(project_kernel, out_shape=jax.ShapeDtypeStruct((sources *...]
    ppermute x11 -> x10, waiting for transfers between devices: 65.5 us -> 54.2 us  [shift(): lax.ppermute(array, axis, [(i, (i + step) % size) for i in range(size)])]
    all_to_all x2, waiting for transfers between devices: 0.01 us -> 9.01 us  [share(): parts = lax.all_to_all(term, 'zh', split_axis=0, concat_axis=0, tiled=True)]
    unnamed x16 -> x26, local copies, waits for them, and re-layouts: 1.78 us -> 8.96 us
    ppermute x11 -> x10, starting transfers between devices: 31.8 us -> 29.7 us  [shift(): lax.ppermute(array, axis, [(i, (i + step) % size) for i in range(size)])]
  transfers between devices with their start and end apart: 16 -> 15, of which waited for: 9 -> 10; matrix products, arithmetic and copies ran while one was open for 2% -> 2% of each run, Pallas kernels for 1% -> 4%
where the time goes in v5:
time: 241 us; the launch traced here: 239 us
  waiting for transfers between devices  77.8 us (32%)
  starting transfers between devices  67.5 us (28%)
  blocking collectives  52.3 us (22%)
  Pallas kernels  23.9 us (10%)
  local copies, waits for them, and re-layouts  11.3 us (5%)
  other arithmetic  5.4 us (2%)
    ppermute x10, waiting for transfers between devices, shift(): lax.ppermute(array, axis, [(i, (i + step) % size) for i in range(size)])  54.2 us
    all_to_all x1, blocking collectives, on_device(): lax.all_to_all(back.reshape(y_size * x_size, CAP, width_part), ('y', 'x')...  34.1 us
    ppermute x10, starting transfers between devices, shift(): lax.ppermute(array, axis, [(i, (i + step) % size) for i in range(size)])  29.7 us
    pallas_call x2, Pallas kernels, project(): pl.pallas_call(project_kernel, out_shape=jax.ShapeDtypeStruct((sources *...  21.5 us
    all_gather x1, blocking collectives, on_device(): hidden_rows = lax.all_gather(hidden, 'zh', axis=0, tiled=True)  18.2 us
    all_to_all x2, starting transfers between devices, share(): parts = lax.all_to_all(term, 'zh', split_axis=0, concat_axis=0, tiled=True)  14.2 us
    all_to_all x1, waiting for transfers between devices, on_device(): lax.all_to_all(sent.reshape(EXPERTS * x_size, CAP, width_part), LOCAL + (...  10.9 us
    all_to_all x1, starting transfers between devices, on_device(): lax.all_to_all(sent.reshape(EXPERTS * x_size, CAP, width_part), LOCAL + (...  10.2 us
  transfers between devices with their start and end apart: 15, of which 10 were waited for; matrix products, arithmetic and copies ran while one was open for 2% of the time, Pallas kernels for 4%

profile of v5, /device:TPU:1, one launch (start us, length us, event | category | flops | bytes accessed | tf_op | source)
XLA Modules:
  0.0 239.5 jit_solution(830284816662165747)
XLA Ops:
  2.2 10.2 %all-to-all-start = ((bf16[16,48,384]{2,1,0:T(8,128)(2,1)}), bf16[16,48,384]{2,1,0:T(8,128)(2,1)S(1)}, u32[]{:S(2)}, u32[]{:S(2)}) async-start(bf16[16,48,384]{2,1,0:T(8,128)(2,1)} %bitcast.5), calls=%async_computation | async-start | bytes 1179648 | tf_op jit(solution)/shard_map/all_to_all | solution.py:136
  12.4 10.9 %all-to-all-done = bf16[16,48,384]{2,1,0:T(8,128)(2,1)S(1)} async-done(((bf16[16,48,384]{2,1,0:T(8,128)(2,1)}), bf16[16,48,384]{2,1,0:T(8,128)(2,1)S(1)}, u32[]{:S(2)}, u32[]{:S(2)}) %all-to-all-start) | async-done | bytes 589856 | tf_op jit(solution)/shard_map/all_to_all | solution.py:136
  24.6 4.1 %all-to-all-start.1 = ((bf16[8,4,48,384]{3,2,1,0:T(8,128)(2,1)}), bf16[8,4,48,384]{3,2,1,0:T(8,128)(2,1)S(1)}, u32[]{:S(2)}, u32[]{:S(2)}) async-start(bf16[8,4,48,384]{3,2,1,0:T(8,128)(2,1)} %broadcast_in_dim.19), calls=%async_computation.1 | async-start | bytes 2359296 | tf_op jit(solution)/shard_map/all_to_all | solution.py:147
  28.7 2.7 %collective-permute-start = (bf16[1024,384]{1,0:T(8,128)(2,1)}, bf16[1024,384]{1,0:T(8,128)(2,1)S(1)}, u32[]{:S(2)}, u32[]{:S(2)}) collective-permute-start(bf16[1024,384]{1,0:T(8,128)(2,1)} %bitcast.11.own_ref), channel_id=1, source_target_pairs={{0,12},{4,0},{8,4},{12,8},{1,13},{5,1},{9,5},{13,9},{2,14},{6,2},{... | collective-permute-start | bytes 2359304 | tf_op jit(solution)/shard_map/ppermute | solution.py:19
  31.4 2.7 %collective-permute-start.1 = (bf16[1024,384]{1,0:T(8,128)(2,1)}, bf16[1024,384]{1,0:T(8,128)(2,1)S(1)}, u32[]{:S(2)}, u32[]{:S(2)}) collective-permute-start(bf16[1024,384]{1,0:T(8,128)(2,1)} %bitcast.11.own_ref), channel_id=1, source_target_pairs={{0,4},{4,8},{8,12},{12,0},{1,5},{5,9},{9,13},{13,1},{2,6},{6,10},{... | collective-permute-start | bytes 2359304 | tf_op jit(solution)/shard_map/ppermute | solution.py:19
  34.1 15.1 %collective-permute-done.after_ref = bf16[1024,384]{1,0:T(8,128)(2,1)S(1)} collective-permute-done((bf16[1024,384]{1,0:T(8,128)(2,1)}, bf16[1024,384]{1,0:T(8,128)(2,1)S(1)}, u32[]{:S(2)}, u32[]{:S(2)}) %collective-permute-start) | collective-permute-done | bytes 786464 | tf_op jit(solution)/shard_map/ppermute | solution.py:19
  49.3 4.3 %collective-permute-start.2 = (bf16[512,384]{1,0:T(8,128)(2,1)S(1)}, bf16[512,384]{1,0:T(8,128)(2,1)S(1)}, u32[]{:S(2)}, u32[]{:S(2)}) collective-permute-start(bf16[512,384]{1,0:T(8,128)(2,1)S(1)} %slice.8), channel_id=1, source_target_pairs={{0,12},{4,0},{8,4},{12,8},{1,13},{5,1},{9,5},{13,9},{2,14},{6,2},{... | collective-permute-start | bytes 1179656 | tf_op jit(solution)/shard_map/ppermute | solution.py:19
  53.7 1.9 collective-permute-start.3
  55.6 4.6 %collective-permute-start.4 = (bf16[1024,384]{1,0:T(8,128)(2,1)S(1)}, bf16[1024,384]{1,0:T(8,128)(2,1)S(1)}, u32[]{:S(2)}, u32[]{:S(2)}) collective-permute-start(bf16[1024,384]{1,0:T(8,128)(2,1)S(1)} %bitcast.30), channel_id=1, source_target_pairs={{0,12},{4,0},{8,4},{12,8},{1,13},{5,1},{9,5},{13,9},{2,14},{6,2},{... | collective-permute-start | bytes 2359304 | tf_op jit(solution)/shard_map/ppermute | solution.py:19
  60.2 1.9 collective-permute-start.5
  62.1 3.9 %collective-permute-done.3.rest_1_ = bf16[512,384]{1,0:T(8,128)(2,1)S(1)} collective-permute-done((bf16[512,384]{1,0:T(8,128)(2,1)S(1)}, bf16[512,384]{1,0:T(8,128)(2,1)S(1)}, u32[]{:S(2)}, u32[]{:S(2)}) %collective-permute-start.3) | collective-permute-done | bytes 393248 | tf_op jit(solution)/shard_map/ppermute | solution.py:19
  66.8 1.9 collective-permute-start.6
  68.7 10.3 %collective-permute-done.4.after_ref = bf16[1024,384]{1,0:T(8,128)(2,1)S(1)} collective-permute-done((bf16[1024,384]{1,0:T(8,128)(2,1)S(1)}, bf16[1024,384]{1,0:T(8,128)(2,1)S(1)}, u32[]{:S(2)}, u32[]{:S(2)}) %collective-permute-start.4) | collective-permute-done | bytes 786464 | tf_op jit(solution)/shard_map/ppermute | solution.py:19
  79.9 4.2 %collective-permute-done.5.before_ref = bf16[1024,384]{1,0:T(8,128)(2,1)S(1)} collective-permute-done((bf16[1024,384]{1,0:T(8,128)(2,1)S(1)}, bf16[1024,384]{1,0:T(8,128)(2,1)S(1)}, u32[]{:S(2)}, u32[]{:S(2)}) %collective-permute-start.5) | collective-permute-done | bytes 786464 | tf_op jit(solution)/shard_map/ppermute | solution.py:19
  85.0 13.6 %collective-permute-done.6.rest_0_ = bf16[1024,384]{1,0:T(8,128)(2,1)S(1)} collective-permute-done((bf16[1024,384]{1,0:T(8,128)(2,1)S(1)}, bf16[1024,384]{1,0:T(8,128)(2,1)S(1)}, u32[]{:S(2)}, u32[]{:S(2)}) %collective-permute-start.6) | collective-permute-done | bytes 786464 | tf_op jit(solution)/shard_map/ppermute | solution.py:19
  104.0 11.2 %shard_map.65 = bf16[384,1024]{1,0:T(8,128)(2,1)} custom-call(bf16[8,4,48,384]{3,2,1,0:T(8,128)(2,1)S(1)} %all-to-all-done.1.rows_ref, bf16[1024,384]{1,0:T(8,128)(2,1)S(1)} %bitcast.33, bf16[1024,384]{1,0:T(8,128)(2,1)S(1)} %copy-done.4, bf16[1024,384]{1,0:T(8,128)(2,1)S(1)} %copy-done.6, bf16[1024,384]{1,0:T(8,128)(2,1)S(1)} %copy-done.8), custom_call_target="tpu_custom_call" | custom-call | flops 1207959552 | bytes 5111808 | tf_op jit(solution)/shard_map/pallas_call | solution.py:69
  115.3 9.1 %all-to-all-start.3 = ((bf16[4,96,1024]{2,1,0:T(8,128)(2,1)}), bf16[4,96,1024]{2,1,0:T(8,128)(2,1)}, u32[]{:S(2)}, u32[]{:S(2)}) async-start(bf16[4,96,1024]{2,1,0:T(8,128)(2,1)} %bitcast.15), calls=%async_computation.3 | async-start | bytes 1572864 | tf_op jit(solution)/shard_map/all_to_all | solution.py:159
  125.4 10.3 %shard_map.64 = bf16[384,1024]{1,0:T(8,128)(2,1)} custom-call(bf16[8,4,48,384]{3,2,1,0:T(8,128)(2,1)S(1)} %all-to-all-done.1.rows_ref, bf16[1024,384]{1,0:T(8,128)(2,1)} %bitcast.11.own_ref, bf16[1024,384]{1,0:T(8,128)(2,1)S(1)} %collective-permute-done.after_ref, bf16[1024,384]{1,0:T(8,128)(2,1)S(1)} %collective-permute-done.1.before_ref, ...), custom_call_target="tpu_custom_call" | custom-call | flops 1207959552 | bytes 5111808 | tf_op jit(solution)/shard_map/pallas_call | solution.py:69
  135.7 7.3 %all-to-all-done.3 = bf16[4,96,1024]{2,1,0:T(8,128)(2,1)} async-done(((bf16[4,96,1024]{2,1,0:T(8,128)(2,1)}), bf16[4,96,1024]{2,1,0:T(8,128)(2,1)}, u32[]{:S(2)}, u32[]{:S(2)}) %all-to-all-start.3) | async-done | bytes 786464 | tf_op jit(solution)/shard_map/all_to_all | solution.py:159
  142.9 5.1 %all-to-all-start.2 = ((bf16[4,96,1024]{2,1,0:T(8,128)(2,1)}), bf16[4,96,1024]{2,1,0:T(8,128)(2,1)}, u32[]{:S(2)}, u32[]{:S(2)}) async-start(bf16[4,96,1024]{2,1,0:T(8,128)(2,1)} %bitcast.12), calls=%async_computation.2 | async-start | bytes 1572864 | tf_op jit(solution)/shard_map/all_to_all | solution.py:159
  148.1 1.9 collective-permute-start.7
  150.0 3.4 %collective-permute-start.8 = (bf16[1024,384]{1,0:T(8,128)(2,1)S(1)}, bf16[1024,384]{1,0:T(8,128)(2,1)S(1)}, u32[]{:S(2)}, u32[]{:S(2)}) collective-permute-start(bf16[1024,384]{1,0:T(8,128)(2,1)S(1)} %bitcast.35), channel_id=1, source_target_pairs={{0,4},{4,8},{8,12},{12,0},{1,5},{5,9},{9,13},{13,1},{2,6},{6,10},{... | collective-permute-start | bytes 2359304 | tf_op jit(solution)/shard_map/ppermute | solution.py:19
  153.4 4.4 %collective-permute-start.9 = (bf16[1024,384]{1,0:T(8,128)(2,1)S(1)}, bf16[1024,384]{1,0:T(8,128)(2,1)S(1)}, u32[]{:S(2)}, u32[]{:S(2)}) collective-permute-start(bf16[1024,384]{1,0:T(8,128)(2,1)S(1)} %bitcast.36), channel_id=1, source_target_pairs={{0,8},{4,12},{8,0},{12,4},{1,9},{5,13},{9,1},{13,5},{2,10},{6,14},... | collective-permute-start | bytes 2359304 | tf_op jit(solution)/shard_map/ppermute | solution.py:19
  157.8 2.0 convert_reduce_fusion
  159.8 1.7 all-to-all-done.2
  161.6 1.3 convert_reduce_fusion.1
  163.1 18.2 %all_gather.3.hidden_ref = bf16[384,1024]{1,0:T(8,128)(2,1)S(1)} all-gather(bf16[96,1024]{1,0:T(8,128)(2,1)S(1)} %multiply_convert_fusion), channel_id=1, replica_groups=mesh['y'=8,'zl'=2,'core'=2,'x'=4,'zh'=4] {'zh'}, dimensions={0}, use_global_device_ids=true | all-gather | bytes 983040 | tf_op jit(solution)/shard_map/all_gather | solution.py:171
  181.3 7.1 %collective-permute-done.9.across_ref = bf16[1024,384]{1,0:T(8,128)(2,1)S(1)} collective-permute-done((bf16[1024,384]{1,0:T(8,128)(2,1)S(1)}, bf16[1024,384]{1,0:T(8,128)(2,1)S(1)}, u32[]{:S(2)}, u32[]{:S(2)}) %collective-permute-start.9) | collective-permute-done | bytes 786464 | tf_op jit(solution)/shard_map/ppermute | solution.py:19
  188.3 2.3 shard_map.66
  190.7 34.1 %all_to_all.38 = bf16[32,48,384]{2,1,0:T(8,128)(2,1)S(1)} all-to-all(bf16[32,48,384]{2,1,0:T(8,128)(2,1)S(1)} %bitcast.29), channel_id=1, replica_groups=mesh['y'=8,'zl'=2,'core'=2,'x'=4,'zh'=4] {'y','x'}, dimensions={0} | all-to-all | bytes 2359296 | tf_op jit(solution)/shard_map/all_to_all | solution.py:173
  225.7 9.2 %all-to-all-start.5 = ((bf16[4,48,384]{2,1,0:T(8,128)(2,1)}), bf16[4,48,384]{2,1,0:T(8,128)(2,1)S(1)}, u32[]{:S(2)}, u32[]{:S(2)}) async-start(bf16[4,48,384]{2,1,0:T(8,128)(2,1)} %reduce_sum.52), calls=%async_computation.5 | async-start | bytes 294912 | tf_op jit(solution)/shard_map/all_to_all | solution.py:181
  234.8 3.7 %all-to-all-done.5 = bf16[4,48,384]{2,1,0:T(8,128)(2,1)S(1)} async-done(((bf16[4,48,384]{2,1,0:T(8,128)(2,1)}), bf16[4,48,384]{2,1,0:T(8,128)(2,1)S(1)}, u32[]{:S(2)}, u32[]{:S(2)}) %all-to-all-start.5) | async-done | bytes 147488 | tf_op jit(solution)/shard_map/all_to_all | solution.py:181
  (49 shorter events, 14.5 us)
Async XLA Ops:
  0.0 1.1 copy-start
  2.2 21.1 %all-to-all-start = ((bf16[16,48,384]{2,1,0:T(8,128)(2,1)}), bf16[16,48,384]{2,1,0:T(8,128)(2,1)S(1)}, u32[]{:S(2)}, u32[]{:S(2)}) async-start(bf16[16,48,384]{2,1,0:T(8,128)(2,1)} %bitcast.5), calls=%async_computation | async-start | bytes 1179648 | tf_op jit(solution)/shard_map/all_to_all | solution.py:136
  24.6 74.9 %all-to-all-start.1 = ((bf16[8,4,48,384]{3,2,1,0:T(8,128)(2,1)}), bf16[8,4,48,384]{3,2,1,0:T(8,128)(2,1)S(1)}, u32[]{:S(2)}, u32[]{:S(2)}) async-start(bf16[8,4,48,384]{3,2,1,0:T(8,128)(2,1)} %broadcast_in_dim.19), calls=%async_computation.1 | async-start | bytes 2359296 | tf_op jit(solution)/shard_map/all_to_all | solution.py:147
  28.7 26.9 %copy-start.1 = (bf16[1,1024,384]{2,1,0:T(8,128)(2,1)S(1)}, bf16[1,1024,384]{2,1,0:T(8,128)(2,1)}, u32[]{:S(2)}) copy-start(bf16[1,1024,384]{2,1,0:T(8,128)(2,1)} %param.10) | copy-start | bytes 2359300
  28.7 20.5 %collective-permute-start = (bf16[1024,384]{1,0:T(8,128)(2,1)}, bf16[1024,384]{1,0:T(8,128)(2,1)S(1)}, u32[]{:S(2)}, u32[]{:S(2)}) collective-permute-start(bf16[1024,384]{1,0:T(8,128)(2,1)} %bitcast.11.own_ref), channel_id=1, source_target_pairs={{0,12},{4,0},{8,4},{12,8},{1,13},{5,1},{9,5},{13,9},{2,14},{6,2},{... | collective-permute-start | bytes 2359304 | tf_op jit(solution)/shard_map/ppermute | solution.py:19
  31.4 22.2 %collective-permute-start.1 = (bf16[1024,384]{1,0:T(8,128)(2,1)}, bf16[1024,384]{1,0:T(8,128)(2,1)S(1)}, u32[]{:S(2)}, u32[]{:S(2)}) collective-permute-start(bf16[1024,384]{1,0:T(8,128)(2,1)} %bitcast.11.own_ref), channel_id=1, source_target_pairs={{0,4},{4,8},{8,12},{12,0},{1,5},{5,9},{9,13},{13,1},{2,6},{6,10},{... | collective-permute-start | bytes 2359304 | tf_op jit(solution)/shard_map/ppermute | solution.py:19
  49.3 12.9 %collective-permute-start.2 = (bf16[512,384]{1,0:T(8,128)(2,1)S(1)}, bf16[512,384]{1,0:T(8,128)(2,1)S(1)}, u32[]{:S(2)}, u32[]{:S(2)}) collective-permute-start(bf16[512,384]{1,0:T(8,128)(2,1)S(1)} %slice.8), channel_id=1, source_target_pairs={{0,12},{4,0},{8,4},{12,8},{1,13},{5,1},{9,5},{13,9},{2,14},{6,2},{... | collective-permute-start | bytes 1179656 | tf_op jit(solution)/shard_map/ppermute | solution.py:19
  53.7 12.4 %collective-permute-start.3 = (bf16[512,384]{1,0:T(8,128)(2,1)S(1)}, bf16[512,384]{1,0:T(8,128)(2,1)S(1)}, u32[]{:S(2)}, u32[]{:S(2)}) collective-permute-start(bf16[512,384]{1,0:T(8,128)(2,1)S(1)} %slice.9), channel_id=1, source_target_pairs={{0,4},{4,8},{8,12},{12,0},{1,5},{5,9},{9,13},{13,1},{2,6},{6,10},{... | collective-permute-start | bytes 1179656 | tf_op jit(solution)/shard_map/ppermute | solution.py:19
  55.6 23.4 %collective-permute-start.4 = (bf16[1024,384]{1,0:T(8,128)(2,1)S(1)}, bf16[1024,384]{1,0:T(8,128)(2,1)S(1)}, u32[]{:S(2)}, u32[]{:S(2)}) collective-permute-start(bf16[1024,384]{1,0:T(8,128)(2,1)S(1)} %bitcast.30), channel_id=1, source_target_pairs={{0,12},{4,0},{8,4},{12,8},{1,13},{5,1},{9,5},{13,9},{2,14},{6,2},{... | collective-permute-start | bytes 2359304 | tf_op jit(solution)/shard_map/ppermute | solution.py:19
  60.2 23.9 %collective-permute-start.5 = (bf16[1024,384]{1,0:T(8,128)(2,1)S(1)}, bf16[1024,384]{1,0:T(8,128)(2,1)S(1)}, u32[]{:S(2)}, u32[]{:S(2)}) collective-permute-start(bf16[1024,384]{1,0:T(8,128)(2,1)S(1)} %bitcast.31), channel_id=1, source_target_pairs={{0,4},{4,8},{8,12},{12,0},{1,5},{5,9},{9,13},{13,1},{2,6},{6,10},{... | collective-permute-start | bytes 2359304 | tf_op jit(solution)/shard_map/ppermute | solution.py:19
  66.0 0.8 copy-start.10
  66.8 31.8 %collective-permute-start.6 = (bf16[1024,384]{1,0:T(8,128)(2,1)S(1)}, bf16[1024,384]{1,0:T(8,128)(2,1)S(1)}, u32[]{:S(2)}, u32[]{:S(2)}) collective-permute-start(bf16[1024,384]{1,0:T(8,128)(2,1)S(1)} %bitcast.32), channel_id=1, source_target_pairs={{0,8},{4,12},{8,0},{12,4},{1,9},{5,13},{9,1},{13,5},{2,10},{6,14},... | collective-permute-start | bytes 2359304 | tf_op jit(solution)/shard_map/ppermute | solution.py:19
  79.0 0.9 copy-start.3
  84.1 0.9 copy-start.5
  98.6 0.9 copy-start.7
  99.5 1.1 copy-start.2
  100.6 1.1 copy-start.4
  101.7 1.1 copy-start.6
  102.9 1.1 copy-start.8
  115.3 27.7 %all-to-all-start.3 = ((bf16[4,96,1024]{2,1,0:T(8,128)(2,1)}), bf16[4,96,1024]{2,1,0:T(8,128)(2,1)}, u32[]{:S(2)}, u32[]{:S(2)}) async-start(bf16[4,96,1024]{2,1,0:T(8,128)(2,1)} %bitcast.15), calls=%async_computation.3 | async-start | bytes 1572864 | tf_op jit(solution)/shard_map/all_to_all | solution.py:159
  124.4 1.0 copy-start.11
  135.7 12.4 %copy-start.9 = (bf16[1,1024,384]{2,1,0:T(8,128)(2,1)S(1)}, bf16[1,1024,384]{2,1,0:T(8,128)(2,1)}, u32[]{:S(2)}) copy-start(bf16[1,1024,384]{2,1,0:T(8,128)(2,1)} %param.11) | copy-start | bytes 2359300
  142.9 18.6 %all-to-all-start.2 = ((bf16[4,96,1024]{2,1,0:T(8,128)(2,1)}), bf16[4,96,1024]{2,1,0:T(8,128)(2,1)}, u32[]{:S(2)}, u32[]{:S(2)}) async-start(bf16[4,96,1024]{2,1,0:T(8,128)(2,1)} %bitcast.12), calls=%async_computation.2 | async-start | bytes 1572864 | tf_op jit(solution)/shard_map/all_to_all | solution.py:159
  148.1 33.2 %collective-permute-start.7 = (bf16[1024,384]{1,0:T(8,128)(2,1)S(1)}, bf16[1024,384]{1,0:T(8,128)(2,1)S(1)}, u32[]{:S(2)}, u32[]{:S(2)}) collective-permute-start(bf16[1024,384]{1,0:T(8,128)(2,1)S(1)} %bitcast.34), channel_id=1, source_target_pairs={{0,12},{4,0},{8,4},{12,8},{1,13},{5,1},{9,5},{13,9},{2,14},{6,2},{... | collective-permute-start | bytes 2359304 | tf_op jit(solution)/shard_map/ppermute | solution.py:19
  150.0 31.3 %collective-permute-start.8 = (bf16[1024,384]{1,0:T(8,128)(2,1)S(1)}, bf16[1024,384]{1,0:T(8,128)(2,1)S(1)}, u32[]{:S(2)}, u32[]{:S(2)}) collective-permute-start(bf16[1024,384]{1,0:T(8,128)(2,1)S(1)} %bitcast.35), channel_id=1, source_target_pairs={{0,4},{4,8},{8,12},{12,0},{1,5},{5,9},{9,13},{13,1},{2,6},{6,10},{... | collective-permute-start | bytes 2359304 | tf_op jit(solution)/shard_map/ppermute | solution.py:19
  153.4 35.0 %collective-permute-start.9 = (bf16[1024,384]{1,0:T(8,128)(2,1)S(1)}, bf16[1024,384]{1,0:T(8,128)(2,1)S(1)}, u32[]{:S(2)}, u32[]{:S(2)}) collective-permute-start(bf16[1024,384]{1,0:T(8,128)(2,1)S(1)} %bitcast.36), channel_id=1, source_target_pairs={{0,8},{4,12},{8,0},{12,4},{1,9},{5,13},{9,1},{13,5},{2,10},{6,14},... | collective-permute-start | bytes 2359304 | tf_op jit(solution)/shard_map/ppermute | solution.py:19
  161.6 1.4 copy-start.12
  225.7 12.9 %all-to-all-start.5 = ((bf16[4,48,384]{2,1,0:T(8,128)(2,1)}), bf16[4,48,384]{2,1,0:T(8,128)(2,1)S(1)}, u32[]{:S(2)}, u32[]{:S(2)}) async-start(bf16[4,48,384]{2,1,0:T(8,128)(2,1)} %reduce_sum.52), calls=%async_computation.5 | async-start | bytes 294912 | tf_op jit(solution)/shard_map/all_to_all | solution.py:181

commit v6 on v4

--- a/solution.py
+++ b/solution.py
@@ -29,61 +29,76 @@
     return shift(after[:half], "x", -1), shift(before[half:], "x", 1)
 
 
+def block_term(rows_ref, step, block):
+    sources, _, cap, depth = rows_ref.shape
+    term = lax.dot_general(
+        rows_ref[:, step].reshape(sources * cap, depth),
+        block,
+        (((1,), (1,)), ((), ())),
+        preferred_element_type=jnp.float32,
+    )
+    return term.astype(jnp.bfloat16).astype(jnp.float32)
+
+
 def project_kernel(rows_ref, own_ref, after_ref, before_ref, *rest):
     *opposite_refs, out_ref = rest
-    sources, blocks, cap, depth = rows_ref.shape
-    part = out_ref.shape[1] // len(opposite_refs)
-    rows = [rows_ref[:, step].reshape(sources * cap, depth) for step in range(blocks)]
+    width = out_ref.shape[1]
+    for start in range(0, width, TILE):
+        tile = pl.ds(start, TILE)
+        total = block_term(rows_ref, 0, own_ref[tile, :])
+        total += block_term(rows_ref, 1, after_ref[tile, :])
+        total += block_term(rows_ref, 3, before_ref[tile, :])
+        if opposite_refs:
+            part = width // len(opposite_refs)
+            opposite = opposite_refs[start // part]
+            total += block_term(rows_ref, 2, opposite[pl.ds(start % part, TILE), :])
+        out_ref[:, tile] = total.astype(out_ref.dtype)
+
+
+def finish_kernel(rows_ref, total_ref, opposite_ref, out_ref):
     for start in range(0, out_ref.shape[1], TILE):
         tile = pl.ds(start, TILE)
-        opposite = opposite_refs[start // part][pl.ds(start % part, TILE), :]
-        total = None
-        for step, block in enumerate((own_ref[tile, :], after_ref[tile, :], opposite, before_ref[tile, :])):
-            term = lax.dot_general(
-                rows[step], block, (((1,), (1,)), ((), ())), preferred_element_type=jnp.float32
-            )
-            term = term.astype(jnp.bfloat16).astype(jnp.float32)
-            total = term if total is None else total + term
-        out_ref[:, tile] = total.astype(jnp.bfloat16)
-
-
-def project(rows, own, pair, opposite):
-    sources, blocks, cap, depth = rows.shape
+        total = total_ref[:, tile] + block_term(rows_ref, 2, opposite_ref[tile, :])
+        out_ref[:, tile] = total.astype(out_ref.dtype)
+
+
+def project(rows, own, pair, opposite=()):
     width = own.shape[0]
+    dtype = jnp.bfloat16 if opposite else jnp.float32
+    return product(project_kernel, rows, width, dtype, own, *pair, *opposite)
+
+
+def finish(rows, total, opposite):
+    return product(finish_kernel, rows, opposite.shape[0], jnp.bfloat16, total, opposite)
+
+
+def product(kernel, rows, width, dtype, *operands):
+    sources, _, cap, _ = rows.shape
+    used = sum(operand.size for operand in operands)
     vmem = pl.BlockSpec(memory_space=pltpu.VMEM)
     return pl.pallas_call(
-        project_kernel,
-        out_shape=jax.ShapeDtypeStruct((sources * cap, width), jnp.bfloat16),
-        in_specs=[vmem] * (4 + len(opposite)),
+        kernel,
+        out_shape=jax.ShapeDtypeStruct((sources * cap, width), dtype),
+        in_specs=[vmem] * (1 + len(operands)),
         out_specs=vmem,
         compiler_params=pltpu.CompilerParams(vmem_limit_bytes=GRANT),
         cost_estimate=pl.CostEstimate(
-            flops=2 * sources * cap * blocks * depth * width,
-            bytes_accessed=2 * (rows.size + blocks * own.size + sources * cap * width),
+            flops=2 * sources * cap * used,
+            bytes_accessed=2 * (rows.size + used + sources * cap * width),
             transcendentals=0,
         ),
-    )(rows, own, *pair, *opposite)
-
-
-def expand_kernel(order_ref, hidden_ref, own_ref, after_ref, low_ref, high_ref, before_ref, out_ref):
+    )(rows, *operands)
+
+
+def expand_kernel(order_ref, hidden_ref, own_ref, after_ref, before_ref, across_ref, out_ref):
     sources, _, cap, width = out_ref.shape
-    half = low_ref.shape[0]
     hidden = hidden_ref[...]
-
-    def put(step, value):
-        value = value.astype(jnp.bfloat16).reshape(sources, cap, width)
-        out_ref[:, order_ref[step]] = value
-
-    def dot(left, right):
-        return jnp.dot(left, right, preferred_element_type=jnp.float32)
-
-    put(0, dot(hidden, own_ref[...]))
-    put(1, dot(hidden, after_ref[...]))
-    put(3, dot(hidden, before_ref[...]))
-    put(2, dot(hidden[:, :half], low_ref[...]) + dot(hidden[:, half:], high_ref[...]))
-
-
-def expand(order, hidden, own, pair, halves, sources):
+    for step, block in ((0, own_ref), (1, after_ref), (3, before_ref), (2, across_ref)):
+        term = jnp.dot(hidden, block[...], preferred_element_type=jnp.float32)
+        out_ref[:, order_ref[step]] = term.astype(jnp.bfloat16).reshape(sources, cap, width)
+
+
+def expand(order, hidden, own, pair, opposite, sources):
     rows, width = hidden.shape
     depth = own.shape[1]
     cap = rows // sources
@@ -92,7 +107,7 @@
     return pl.pallas_call(
         expand_kernel,
         out_shape=jax.ShapeDtypeStruct((sources, places, cap, depth), jnp.bfloat16),
-        in_specs=[pl.BlockSpec(memory_space=pltpu.SMEM)] + [vmem] * 6,
+        in_specs=[pl.BlockSpec(memory_space=pltpu.SMEM)] + [vmem] * 5,
         out_specs=vmem,
         compiler_params=pltpu.CompilerParams(vmem_limit_bytes=GRANT),
         cost_estimate=pl.CostEstimate(
@@ -100,7 +115,7 @@
             bytes_accessed=2 * (hidden.size + places * own.size + places * rows * depth),
             transcendentals=0,
         ),
-    )(order, hidden, own, pair[0], *halves, pair[1])
+    )(order, hidden, own, *pair, *opposite)
 
 
 def on_device(tokens, expert_ids, gate_fixed, w_gate, w_up, w_down):
@@ -141,7 +156,6 @@
     gate_halves = across(gate_pair)
     up_own, _ = lax.optimization_barrier((w_up[0], gate_pair))
     up_pair = beside(up_own)
-    up_across = (shift(up_own, "x", 2),)
 
     def share(term):
         parts = lax.all_to_all(term, "zh", split_axis=0, concat_axis=0, tiled=True)
@@ -149,15 +163,18 @@
         return jnp.sum(parts.astype(jnp.float32), axis=0)
 
     gate_term = project(rows, gate_own, gate_pair, gate_halves)
+    up_last, gate_term = lax.optimization_barrier((w_up[0], gate_term))
+    up_across = shift(up_last, "x", 2)
     gate_share = share(gate_term)
-    up_term = project(rows, up_own, up_pair, up_across)
+    up_open = project(rows, up_own, up_pair)
+    up_term = finish(rows, up_open, up_across)
     down_own, up_term = lax.optimization_barrier((w_down[0], up_term))
     down_pair = beside(down_own)
-    down_halves = across(down_pair)
+    down_across = (shift(down_own, "x", 2),)
     up_share = share(up_term)
     hidden = (jax.nn.silu(gate_share) * up_share).astype(jnp.bfloat16)
     hidden_rows = lax.all_gather(hidden, "zh", axis=0, tiled=True)
-    back = expand(jnp.stack(order), hidden_rows, down_own, down_pair, down_halves, y_size)
+    back = expand(jnp.stack(order), hidden_rows, down_own, down_pair, down_across, y_size)
     back = lax.all_to_all(
         back.reshape(y_size * x_size, CAP, width_part),
         ("y", "x"),

time: 225 us -> 216 us (0.960)
  starting transfers between devices: 73.4 us -> 69.7 us
  blocking collectives: 50.8 us -> 47.8 us
  waiting for transfers between devices: 80.1 us -> 77.4 us
    ppermute x11 -> x10, waiting for transfers between devices: 65.5 us -> 54.8 us  [shift(): lax.ppermute(array, axis, [(i, (i + step) % size) for i in range(size)])]
    all_to_all x2, waiting for transfers between devices: 0.01 us -> 8 us  [share(): parts = lax.all_to_all(term, 'zh', split_axis=0, concat_axis=0, tiled=True)]
    ppermute x11 -> x10, starting transfers between devices: 31.8 us -> 28.9 us  [shift(): lax.ppermute(array, axis, [(i, (i + step) % size) for i in range(size)])]
    all_gather x1, blocking collectives: 18 us -> 15.6 us  [on_device(): hidden_rows = lax.all_gather(hidden, 'zh', axis=0, tiled=True)]
    pallas_call x2 -> x3, Pallas kernels: 6.6 us -> 6.79 us  [product(): pl.pallas_call(kernel, out_shape=jax.ShapeDtypeStruct((sources * cap, wid...]
  transfers between devices with their start and end apart: 16 -> 15, of which waited for: 9 -> 10; matrix products, arithmetic and copies ran while one was open for 2% -> 2% of each run, Pallas kernels for 1% -> 1%
where the time goes in v6:
time: 216 us; the launch traced here: 215 us
  waiting for transfers between devices  77.4 us (36%)
  starting transfers between devices  69.7 us (32%)
  blocking collectives  47.8 us (22%)
  Pallas kernels  9.12 us (4%)
  other arithmetic  5.37 us (2%)
  local copies, waits for them, and re-layouts  4.04 us (2%)
    ppermute x10, waiting for transfers between devices, shift(): lax.ppermute(array, axis, [(i, (i + step) % size) for i in range(size)])  54.8 us
    all_to_all x1, blocking collectives, on_device(): lax.all_to_all(back.reshape(y_size * x_size, CAP, width_part), ('y', 'x')...  32.2 us
    ppermute x10, starting transfers between devices, shift(): lax.ppermute(array, axis, [(i, (i + step) % size) for i in range(size)])  28.9 us
    all_to_all x2, starting transfers between devices, share(): parts = lax.all_to_all(term, 'zh', split_axis=0, concat_axis=0, tiled=True)  15.7 us
    all_gather x1, blocking collectives, on_device(): hidden_rows = lax.all_gather(hidden, 'zh', axis=0, tiled=True)  15.6 us
    all_to_all x1, waiting for transfers between devices, on_device(): lax.all_to_all(sent.reshape(EXPERTS * x_size, CAP, width_part), LOCAL + (...  10.9 us
    all_to_all x1, starting transfers between devices, on_device(): lax.all_to_all(back, LOCAL, split_axis=0, concat_axis=0, tiled=True)  10.7 us
    all_to_all x1, starting transfers between devices, on_device(): lax.all_to_all(sent.reshape(EXPERTS * x_size, CAP, width_part), LOCAL + (...  10.2 us
  transfers between devices with their start and end apart: 15, of which 10 were waited for; matrix products, arithmetic and copies ran while one was open for 2% of the time, Pallas kernels for 1%

profile of v6, /device:TPU:1, one launch (start us, length us, event | category | flops | bytes accessed | tf_op | source)
XLA Modules:
  0.0 214.7 jit_solution(18029312513998476880)
XLA Ops:
  2.2 10.2 %all-to-all-start = ((bf16[16,48,384]{2,1,0:T(8,128)(2,1)}), bf16[16,48,384]{2,1,0:T(8,128)(2,1)S(1)}, u32[]{:S(2)}, u32[]{:S(2)}) async-start(bf16[16,48,384]{2,1,0:T(8,128)(2,1)} %bitcast.6), calls=%async_computation | async-start | bytes 1179648 | tf_op jit(solution)/shard_map/all_to_all | solution.py:140
  12.4 10.9 %all-to-all-done = bf16[16,48,384]{2,1,0:T(8,128)(2,1)S(1)} async-done(((bf16[16,48,384]{2,1,0:T(8,128)(2,1)}), bf16[16,48,384]{2,1,0:T(8,128)(2,1)S(1)}, u32[]{:S(2)}, u32[]{:S(2)}) %all-to-all-start) | async-done | bytes 589856 | tf_op jit(solution)/shard_map/all_to_all | solution.py:140
  24.5 4.1 %all-to-all-start.1 = ((bf16[8,4,48,384]{3,2,1,0:T(8,128)(2,1)}), bf16[8,4,48,384]{3,2,1,0:T(8,128)(2,1)S(1)}, u32[]{:S(2)}, u32[]{:S(2)}) async-start(bf16[8,4,48,384]{3,2,1,0:T(8,128)(2,1)} %broadcast_in_dim.19), calls=%async_computation.1 | async-start | bytes 2359296 | tf_op jit(solution)/shard_map/all_to_all | solution.py:151
  28.7 2.6 %collective-permute-start = (bf16[1024,384]{1,0:T(8,128)(2,1)}, bf16[1024,384]{1,0:T(8,128)(2,1)S(1)}, u32[]{:S(2)}, u32[]{:S(2)}) collective-permute-start(bf16[1024,384]{1,0:T(8,128)(2,1)} %bitcast.12.own_ref), channel_id=1, source_target_pairs={{0,12},{4,0},{8,4},{12,8},{1,13},{5,1},{9,5},{13,9},{2,14},{6,2},{... | collective-permute-start | bytes 2359304 | tf_op jit(solution)/shard_map/ppermute | solution.py:19
  31.2 2.7 %collective-permute-start.1 = (bf16[1024,384]{1,0:T(8,128)(2,1)}, bf16[1024,384]{1,0:T(8,128)(2,1)S(1)}, u32[]{:S(2)}, u32[]{:S(2)}) collective-permute-start(bf16[1024,384]{1,0:T(8,128)(2,1)} %bitcast.12.own_ref), channel_id=1, source_target_pairs={{0,4},{4,8},{8,12},{12,0},{1,5},{5,9},{9,13},{13,1},{2,6},{6,10},{... | collective-permute-start | bytes 2359304 | tf_op jit(solution)/shard_map/ppermute | solution.py:19
  33.9 15.1 %collective-permute-done.after_ref = bf16[1024,384]{1,0:T(8,128)(2,1)S(1)} collective-permute-done((bf16[1024,384]{1,0:T(8,128)(2,1)}, bf16[1024,384]{1,0:T(8,128)(2,1)S(1)}, u32[]{:S(2)}, u32[]{:S(2)}) %collective-permute-start) | collective-permute-done | bytes 786464 | tf_op jit(solution)/shard_map/ppermute | solution.py:19
  49.1 4.3 %collective-permute-start.2 = (bf16[512,384]{1,0:T(8,128)(2,1)S(1)}, bf16[512,384]{1,0:T(8,128)(2,1)S(1)}, u32[]{:S(2)}, u32[]{:S(2)}) collective-permute-start(bf16[512,384]{1,0:T(8,128)(2,1)S(1)} %slice.8), channel_id=1, source_target_pairs={{0,12},{4,0},{8,4},{12,8},{1,13},{5,1},{9,5},{13,9},{2,14},{6,2},{... | collective-permute-start | bytes 1179656 | tf_op jit(solution)/shard_map/ppermute | solution.py:19
  53.5 1.9 collective-permute-start.3
  55.4 5.3 %collective-permute-done.2.rest_0_ = bf16[512,384]{1,0:T(8,128)(2,1)S(1)} collective-permute-done((bf16[512,384]{1,0:T(8,128)(2,1)S(1)}, bf16[512,384]{1,0:T(8,128)(2,1)S(1)}, u32[]{:S(2)}, u32[]{:S(2)}) %collective-permute-start.2) | collective-permute-done | bytes 393248 | tf_op jit(solution)/shard_map/ppermute | solution.py:19
  60.7 5.1 %collective-permute-done.3.rest_1_ = bf16[512,384]{1,0:T(8,128)(2,1)S(1)} collective-permute-done((bf16[512,384]{1,0:T(8,128)(2,1)S(1)}, bf16[512,384]{1,0:T(8,128)(2,1)S(1)}, u32[]{:S(2)}, u32[]{:S(2)}) %collective-permute-start.3) | collective-permute-done | bytes 393248 | tf_op jit(solution)/shard_map/ppermute | solution.py:19
  67.6 3.9 %shard_map.64 = bf16[384,1024]{1,0:T(8,128)(2,1)} custom-call(bf16[8,4,48,384]{3,2,1,0:T(8,128)(2,1)S(1)} %all-to-all-done.1.rows_ref, bf16[1024,384]{1,0:T(8,128)(2,1)} %bitcast.12.own_ref, bf16[1024,384]{1,0:T(8,128)(2,1)S(1)} %collective-permute-done.after_ref, bf16[1024,384]{1,0:T(8,128)(2,1)S(1)} %collective-permute-done.1.before_ref, ...), custom_call_target="tpu_custom_call" | custom-call | flops 1207959552 | bytes 5111808 | tf_op jit(solution)/shard_map/pallas_call | solution.py:79
  71.5 9.3 %all-to-all-start.2 = ((bf16[4,96,1024]{2,1,0:T(8,128)(2,1)}), bf16[4,96,1024]{2,1,0:T(8,128)(2,1)S(1)}, u32[]{:S(2)}, u32[]{:S(2)}) async-start(bf16[4,96,1024]{2,1,0:T(8,128)(2,1)} %bitcast.13), calls=%async_computation.2 | async-start | bytes 1572864 | tf_op jit(solution)/shard_map/all_to_all | solution.py:161
  80.7 1.9 collective-permute-start.4
  82.7 3.4 %collective-permute-start.5 = (bf16[1024,384]{1,0:T(8,128)(2,1)S(1)}, bf16[1024,384]{1,0:T(8,128)(2,1)S(1)}, u32[]{:S(2)}, u32[]{:S(2)}) collective-permute-start(bf16[1024,384]{1,0:T(8,128)(2,1)S(1)} %bitcast.31), channel_id=1, source_target_pairs={{0,4},{4,8},{8,12},{12,0},{1,5},{5,9},{9,13},{13,1},{2,6},{6,10},{... | collective-permute-start | bytes 2359304 | tf_op jit(solution)/shard_map/ppermute | solution.py:19
  86.0 1.9 collective-permute-start.6
  87.9 11.2 %collective-permute-done.4.after_ref = bf16[1024,384]{1,0:T(8,128)(2,1)S(1)} collective-permute-done((bf16[1024,384]{1,0:T(8,128)(2,1)S(1)}, bf16[1024,384]{1,0:T(8,128)(2,1)S(1)}, u32[]{:S(2)}, u32[]{:S(2)}) %collective-permute-start.4) | collective-permute-done | bytes 786464 | tf_op jit(solution)/shard_map/ppermute | solution.py:19
  99.2 4.7 %collective-permute-done.5.before_ref = bf16[1024,384]{1,0:T(8,128)(2,1)S(1)} collective-permute-done((bf16[1024,384]{1,0:T(8,128)(2,1)S(1)}, bf16[1024,384]{1,0:T(8,128)(2,1)S(1)}, u32[]{:S(2)}, u32[]{:S(2)}) %collective-permute-start.5) | collective-permute-done | bytes 786464 | tf_op jit(solution)/shard_map/ppermute | solution.py:19
  103.8 1.4 shard_map.65.total_ref
  105.3 12.4 %collective-permute-done.6.opposite_ref = bf16[1024,384]{1,0:T(8,128)(2,1)S(1)} collective-permute-done((bf16[1024,384]{1,0:T(8,128)(2,1)S(1)}, bf16[1024,384]{1,0:T(8,128)(2,1)S(1)}, u32[]{:S(2)}, u32[]{:S(2)}) %collective-permute-start.6) | collective-permute-done | bytes 786464 | tf_op jit(solution)/shard_map/ppermute | solution.py:19
  117.7 1.5 shard_map.66
  119.2 6.5 %all-to-all-start.3 = ((bf16[4,96,1024]{2,1,0:T(8,128)(2,1)}), bf16[4,96,1024]{2,1,0:T(8,128)(2,1)}, u32[]{:S(2)}, u32[]{:S(2)}) async-start(bf16[4,96,1024]{2,1,0:T(8,128)(2,1)} %bitcast.15), calls=%async_computation.3 | async-start | bytes 1572864 | tf_op jit(solution)/shard_map/all_to_all | solution.py:161
  125.8 2.6 %collective-permute-start.7 = (bf16[1024,384]{1,0:T(8,128)(2,1)S(1)}, bf16[1024,384]{1,0:T(8,128)(2,1)S(1)}, u32[]{:S(2)}, u32[]{:S(2)}) collective-permute-start(bf16[1024,384]{1,0:T(8,128)(2,1)S(1)} %bitcast.34), channel_id=1, source_target_pairs={{0,12},{4,0},{8,4},{12,8},{1,13},{5,1},{9,5},{13,9},{2,14},{6,2},{... | collective-permute-start | bytes 2359304 | tf_op jit(solution)/shard_map/ppermute | solution.py:19
  128.4 2.6 %collective-permute-start.8 = (bf16[1024,384]{1,0:T(8,128)(2,1)S(1)}, bf16[1024,384]{1,0:T(8,128)(2,1)S(1)}, u32[]{:S(2)}, u32[]{:S(2)}) collective-permute-start(bf16[1024,384]{1,0:T(8,128)(2,1)S(1)} %bitcast.35), channel_id=1, source_target_pairs={{0,4},{4,8},{8,12},{12,0},{1,5},{5,9},{9,13},{13,1},{2,6},{6,10},{... | collective-permute-start | bytes 2359304 | tf_op jit(solution)/shard_map/ppermute | solution.py:19
  131.0 4.9 %collective-permute-start.9 = (bf16[1024,384]{1,0:T(8,128)(2,1)S(1)}, bf16[1024,384]{1,0:T(8,128)(2,1)S(1)}, u32[]{:S(2)}, u32[]{:S(2)}) collective-permute-start(bf16[1024,384]{1,0:T(8,128)(2,1)S(1)} %bitcast.36), channel_id=1, source_target_pairs={{0,8},{4,12},{8,0},{12,4},{1,9},{5,13},{9,1},{13,5},{2,10},{6,14},... | collective-permute-start | bytes 2359304 | tf_op jit(solution)/shard_map/ppermute | solution.py:19
  135.9 2.0 convert_reduce_fusion.1
  138.0 8.0 %all-to-all-done.3 = bf16[4,96,1024]{2,1,0:T(8,128)(2,1)} async-done(((bf16[4,96,1024]{2,1,0:T(8,128)(2,1)}), bf16[4,96,1024]{2,1,0:T(8,128)(2,1)}, u32[]{:S(2)}, u32[]{:S(2)}) %all-to-all-start.3) | async-done | bytes 786464 | tf_op jit(solution)/shard_map/all_to_all | solution.py:161
  146.0 1.3 convert_reduce_fusion
  147.4 15.6 %all_gather.3.hidden_ref = bf16[384,1024]{1,0:T(8,128)(2,1)S(1)} all-gather(bf16[96,1024]{1,0:T(8,128)(2,1)S(1)} %multiply_convert_fusion), channel_id=1, replica_groups=mesh['y'=8,'zl'=2,'core'=2,'x'=4,'zh'=4] {'zh'}, dimensions={0}, use_global_device_ids=true | all-gather | bytes 983040 | tf_op jit(solution)/shard_map/all_gather | solution.py:176
  163.9 2.3 %shard_map.67 = bf16[8,4,48,384]{3,2,1,0:T(8,128)(2,1)S(1)} custom-call(s32[4]{0:T(128)S(1)} %pad_add_fusion.order_ref, bf16[384,1024]{1,0:T(8,128)(2,1)S(1)} %all_gather.3.hidden_ref, bf16[1024,384]{1,0:T(8,128)(2,1)S(1)} %bitcast.37, bf16[1024,384]{1,0:T(8,128)(2,1)S(1)} %collective-permute-done.7.after_ref, ...), custom_call_target="tpu_custom_call" | custom-call | flops 1207959552 | bytes 5111808 | tf_op jit(solution)/shard_map/pallas_call | solution.py:107
  166.3 32.2 %all_to_all.38 = bf16[32,48,384]{2,1,0:T(8,128)(2,1)S(1)} all-to-all(bf16[32,48,384]{2,1,0:T(8,128)(2,1)S(1)} %bitcast.29), channel_id=1, replica_groups=mesh['y'=8,'zl'=2,'core'=2,'x'=4,'zh'=4] {'y','x'}, dimensions={0} | all-to-all | bytes 2359296 | tf_op jit(solution)/shard_map/all_to_all | solution.py:178
  199.3 10.7 %all-to-all-start.5 = ((bf16[4,48,384]{2,1,0:T(8,128)(2,1)}), bf16[4,48,384]{2,1,0:T(8,128)(2,1)S(1)}, u32[]{:S(2)}, u32[]{:S(2)}) async-start(bf16[4,48,384]{2,1,0:T(8,128)(2,1)} %reduce_sum.52), calls=%async_computation.5 | async-start | bytes 294912 | tf_op jit(solution)/shard_map/all_to_all | solution.py:186
  210.0 3.7 %all-to-all-done.5 = bf16[4,48,384]{2,1,0:T(8,128)(2,1)S(1)} async-done(((bf16[4,48,384]{2,1,0:T(8,128)(2,1)}), bf16[4,48,384]{2,1,0:T(8,128)(2,1)S(1)}, u32[]{:S(2)}, u32[]{:S(2)}) %all-to-all-start.5) | async-done | bytes 147488 | tf_op jit(solution)/shard_map/all_to_all | solution.py:186
  (38 shorter events, 8.2 us)
Async XLA Ops:
  0.0 1.1 copy-start
  2.2 21.1 %all-to-all-start = ((bf16[16,48,384]{2,1,0:T(8,128)(2,1)}), bf16[16,48,384]{2,1,0:T(8,128)(2,1)S(1)}, u32[]{:S(2)}, u32[]{:S(2)}) async-start(bf16[16,48,384]{2,1,0:T(8,128)(2,1)} %bitcast.6), calls=%async_computation | async-start | bytes 1179648 | tf_op jit(solution)/shard_map/all_to_all | solution.py:140
  24.5 42.1 %all-to-all-start.1 = ((bf16[8,4,48,384]{3,2,1,0:T(8,128)(2,1)}), bf16[8,4,48,384]{3,2,1,0:T(8,128)(2,1)S(1)}, u32[]{:S(2)}, u32[]{:S(2)}) async-start(bf16[8,4,48,384]{3,2,1,0:T(8,128)(2,1)} %broadcast_in_dim.19), calls=%async_computation.1 | async-start | bytes 2359296 | tf_op jit(solution)/shard_map/all_to_all | solution.py:151
  28.7 20.4 %collective-permute-start = (bf16[1024,384]{1,0:T(8,128)(2,1)}, bf16[1024,384]{1,0:T(8,128)(2,1)S(1)}, u32[]{:S(2)}, u32[]{:S(2)}) collective-permute-start(bf16[1024,384]{1,0:T(8,128)(2,1)} %bitcast.12.own_ref), channel_id=1, source_target_pairs={{0,12},{4,0},{8,4},{12,8},{1,13},{5,1},{9,5},{13,9},{2,14},{6,2},{... | collective-permute-start | bytes 2359304 | tf_op jit(solution)/shard_map/ppermute | solution.py:19
  31.2 22.2 %collective-permute-start.1 = (bf16[1024,384]{1,0:T(8,128)(2,1)}, bf16[1024,384]{1,0:T(8,128)(2,1)S(1)}, u32[]{:S(2)}, u32[]{:S(2)}) collective-permute-start(bf16[1024,384]{1,0:T(8,128)(2,1)} %bitcast.12.own_ref), channel_id=1, source_target_pairs={{0,4},{4,8},{8,12},{12,0},{1,5},{5,9},{9,13},{13,1},{2,6},{6,10},{... | collective-permute-start | bytes 2359304 | tf_op jit(solution)/shard_map/ppermute | solution.py:19
  49.1 11.7 %collective-permute-start.2 = (bf16[512,384]{1,0:T(8,128)(2,1)S(1)}, bf16[512,384]{1,0:T(8,128)(2,1)S(1)}, u32[]{:S(2)}, u32[]{:S(2)}) collective-permute-start(bf16[512,384]{1,0:T(8,128)(2,1)S(1)} %slice.8), channel_id=1, source_target_pairs={{0,12},{4,0},{8,4},{12,8},{1,13},{5,1},{9,5},{13,9},{2,14},{6,2},{... | collective-permute-start | bytes 1179656 | tf_op jit(solution)/shard_map/ppermute | solution.py:19
  53.5 12.4 %collective-permute-start.3 = (bf16[512,384]{1,0:T(8,128)(2,1)S(1)}, bf16[512,384]{1,0:T(8,128)(2,1)S(1)}, u32[]{:S(2)}, u32[]{:S(2)}) collective-permute-start(bf16[512,384]{1,0:T(8,128)(2,1)S(1)} %slice.9), channel_id=1, source_target_pairs={{0,4},{4,8},{8,12},{12,0},{1,5},{5,9},{9,13},{13,1},{2,6},{6,10},{... | collective-permute-start | bytes 1179656 | tf_op jit(solution)/shard_map/ppermute | solution.py:19
  65.8 0.8 copy-start.3
  66.6 1.0 copy-start.4
  71.5 9.3 %copy-start.1 = (bf16[1,1024,384]{2,1,0:T(8,128)(2,1)S(1)}, bf16[1,1024,384]{2,1,0:T(8,128)(2,1)}, u32[]{:S(2)}) copy-start(bf16[1,1024,384]{2,1,0:T(8,128)(2,1)} %param.10) | copy-start | bytes 2359300
  71.5 47.7 %all-to-all-start.2 = ((bf16[4,96,1024]{2,1,0:T(8,128)(2,1)}), bf16[4,96,1024]{2,1,0:T(8,128)(2,1)S(1)}, u32[]{:S(2)}, u32[]{:S(2)}) async-start(bf16[4,96,1024]{2,1,0:T(8,128)(2,1)} %bitcast.13), calls=%async_computation.2 | async-start | bytes 1572864 | tf_op jit(solution)/shard_map/all_to_all | solution.py:161
  80.7 18.4 %collective-permute-start.4 = (bf16[1024,384]{1,0:T(8,128)(2,1)S(1)}, bf16[1024,384]{1,0:T(8,128)(2,1)S(1)}, u32[]{:S(2)}, u32[]{:S(2)}) collective-permute-start(bf16[1024,384]{1,0:T(8,128)(2,1)S(1)} %bitcast.30), channel_id=1, source_target_pairs={{0,12},{4,0},{8,4},{12,8},{1,13},{5,1},{9,5},{13,9},{2,14},{6,2},{... | collective-permute-start | bytes 2359304 | tf_op jit(solution)/shard_map/ppermute | solution.py:19
  82.7 21.2 %collective-permute-start.5 = (bf16[1024,384]{1,0:T(8,128)(2,1)S(1)}, bf16[1024,384]{1,0:T(8,128)(2,1)S(1)}, u32[]{:S(2)}, u32[]{:S(2)}) collective-permute-start(bf16[1024,384]{1,0:T(8,128)(2,1)S(1)} %bitcast.31), channel_id=1, source_target_pairs={{0,4},{4,8},{8,12},{12,0},{1,5},{5,9},{9,13},{13,1},{2,6},{6,10},{... | collective-permute-start | bytes 2359304 | tf_op jit(solution)/shard_map/ppermute | solution.py:19
  86.0 31.6 %collective-permute-start.6 = (bf16[1024,384]{1,0:T(8,128)(2,1)S(1)}, bf16[1024,384]{1,0:T(8,128)(2,1)S(1)}, u32[]{:S(2)}, u32[]{:S(2)}) collective-permute-start(bf16[1024,384]{1,0:T(8,128)(2,1)S(1)} %bitcast.32), channel_id=1, source_target_pairs={{0,8},{4,12},{8,0},{12,4},{1,9},{5,13},{9,1},{13,5},{2,10},{6,14},... | collective-permute-start | bytes 2359304 | tf_op jit(solution)/shard_map/ppermute | solution.py:19
  119.2 6.6 %copy-start.2 = (bf16[1,1024,384]{2,1,0:T(8,128)(2,1)S(1)}, bf16[1,1024,384]{2,1,0:T(8,128)(2,1)}, u32[]{:S(2)}) copy-start(bf16[1,1024,384]{2,1,0:T(8,128)(2,1)} %param.11) | copy-start | bytes 2359300
  119.2 6.6 %copy-start.5 = (bf16[4,96,1024]{2,1,0:T(8,128)(2,1)}, bf16[4,96,1024]{2,1,0:T(8,128)(2,1)S(1)}, u32[]{:S(2)}) copy-start(bf16[4,96,1024]{2,1,0:T(8,128)(2,1)S(1)} %all-to-all-done.2) | copy-start | bytes 2359300
  119.2 26.8 %all-to-all-start.3 = ((bf16[4,96,1024]{2,1,0:T(8,128)(2,1)}), bf16[4,96,1024]{2,1,0:T(8,128)(2,1)}, u32[]{:S(2)}, u32[]{:S(2)}) async-start(bf16[4,96,1024]{2,1,0:T(8,128)(2,1)} %bitcast.15), calls=%async_computation.3 | async-start | bytes 1572864 | tf_op jit(solution)/shard_map/all_to_all | solution.py:161
  125.8 37.3 %collective-permute-start.7 = (bf16[1024,384]{1,0:T(8,128)(2,1)S(1)}, bf16[1024,384]{1,0:T(8,128)(2,1)S(1)}, u32[]{:S(2)}, u32[]{:S(2)}) collective-permute-start(bf16[1024,384]{1,0:T(8,128)(2,1)S(1)} %bitcast.34), channel_id=1, source_target_pairs={{0,12},{4,0},{8,4},{12,8},{1,13},{5,1},{9,5},{13,9},{2,14},{6,2},{... | collective-permute-start | bytes 2359304 | tf_op jit(solution)/shard_map/ppermute | solution.py:19
  128.4 34.6 %collective-permute-start.8 = (bf16[1024,384]{1,0:T(8,128)(2,1)S(1)}, bf16[1024,384]{1,0:T(8,128)(2,1)S(1)}, u32[]{:S(2)}, u32[]{:S(2)}) collective-permute-start(bf16[1024,384]{1,0:T(8,128)(2,1)S(1)} %bitcast.35), channel_id=1, source_target_pairs={{0,4},{4,8},{8,12},{12,0},{1,5},{5,9},{9,13},{13,1},{2,6},{6,10},{... | collective-permute-start | bytes 2359304 | tf_op jit(solution)/shard_map/ppermute | solution.py:19
  131.0 32.9 %collective-permute-start.9 = (bf16[1024,384]{1,0:T(8,128)(2,1)S(1)}, bf16[1024,384]{1,0:T(8,128)(2,1)S(1)}, u32[]{:S(2)}, u32[]{:S(2)}) collective-permute-start(bf16[1024,384]{1,0:T(8,128)(2,1)S(1)} %bitcast.36), channel_id=1, source_target_pairs={{0,8},{4,12},{8,0},{12,4},{1,9},{5,13},{9,1},{13,5},{2,10},{6,14},... | collective-permute-start | bytes 2359304 | tf_op jit(solution)/shard_map/ppermute | solution.py:19
  146.0 1.4 copy-start.6
  199.3 14.4 %all-to-all-start.5 = ((bf16[4,48,384]{2,1,0:T(8,128)(2,1)}), bf16[4,48,384]{2,1,0:T(8,128)(2,1)S(1)}, u32[]{:S(2)}, u32[]{:S(2)}) async-start(bf16[4,48,384]{2,1,0:T(8,128)(2,1)} %reduce_sum.52), calls=%async_computation.5 | async-start | bytes 294912 | tf_op jit(solution)/shard_map/all_to_all | solution.py:186

commit v7 on v6

--- a/solution.py
+++ b/solution.py
@@ -1,3 +1,5 @@
+import functools
+
 import jax
 import jax.numpy as jnp
 from jax import lax
@@ -40,44 +42,32 @@
     return term.astype(jnp.bfloat16).astype(jnp.float32)
 
 
-def project_kernel(rows_ref, own_ref, after_ref, before_ref, *rest):
-    *opposite_refs, out_ref = rest
+def project_kernel(steps, rows_ref, *refs):
+    *block_refs, out_ref = refs
     width = out_ref.shape[1]
+    opened = block_refs.pop(0) if block_refs[0].shape == out_ref.shape else None
     for start in range(0, width, TILE):
         tile = pl.ds(start, TILE)
-        total = block_term(rows_ref, 0, own_ref[tile, :])
-        total += block_term(rows_ref, 1, after_ref[tile, :])
-        total += block_term(rows_ref, 3, before_ref[tile, :])
-        if opposite_refs:
-            part = width // len(opposite_refs)
-            opposite = opposite_refs[start // part]
-            total += block_term(rows_ref, 2, opposite[pl.ds(start % part, TILE), :])
+        total = None if opened is None else opened[:, tile]
+        pieces = list(block_refs)
+        for step in steps:
+            block = pieces.pop(0)
+            if block.shape[0] == width:
+                block = block[tile, :]
+            else:
+                other, part = pieces.pop(0), block.shape[0]
+                block = (block if start < part else other)[pl.ds(start % part, TILE), :]
+            term = block_term(rows_ref, step, block)
+            total = term if total is None else total + term
         out_ref[:, tile] = total.astype(out_ref.dtype)
 
 
-def finish_kernel(rows_ref, total_ref, opposite_ref, out_ref):
-    for start in range(0, out_ref.shape[1], TILE):
-        tile = pl.ds(start, TILE)
-        total = total_ref[:, tile] + block_term(rows_ref, 2, opposite_ref[tile, :])
-        out_ref[:, tile] = total.astype(out_ref.dtype)
-
-
-def project(rows, own, pair, opposite=()):
-    width = own.shape[0]
-    dtype = jnp.bfloat16 if opposite else jnp.float32
-    return product(project_kernel, rows, width, dtype, own, *pair, *opposite)
-
-
-def finish(rows, total, opposite):
-    return product(finish_kernel, rows, opposite.shape[0], jnp.bfloat16, total, opposite)
-
-
-def product(kernel, rows, width, dtype, *operands):
+def project(steps, rows, width, dtype, *operands):
     sources, _, cap, _ = rows.shape
     used = sum(operand.size for operand in operands)
     vmem = pl.BlockSpec(memory_space=pltpu.VMEM)
     return pl.pallas_call(
-        kernel,
+        functools.partial(project_kernel, steps),
         out_shape=jax.ShapeDtypeStruct((sources * cap, width), dtype),
         in_specs=[vmem] * (1 + len(operands)),
         out_specs=vmem,
@@ -88,6 +78,48 @@
             transcendentals=0,
         ),
     )(rows, *operands)
+
+
+def gate_kernel(rows_ref, after_ref, before_ref, own_ref, low_ref, high_ref, out_ref, own, opposite, sems):
+    half = low_ref.shape[0]
+    copies = (
+        pltpu.make_async_copy(own_ref, own, sems.at[0]),
+        pltpu.make_async_copy(low_ref, opposite.at[pl.ds(0, half), :], sems.at[1]),
+        pltpu.make_async_copy(high_ref, opposite.at[pl.ds(half, half), :], sems.at[2]),
+    )
+    for copy in copies:
+        copy.start()
+    total = block_term(rows_ref, 1, after_ref[...]) + block_term(rows_ref, 3, before_ref[...])
+    copies[0].wait()
+    total += block_term(rows_ref, 0, own[...])
+    copies[1].wait()
+    copies[2].wait()
+    total += block_term(rows_ref, 2, opposite[...])
+    out_ref[...] = total.astype(out_ref.dtype)
+
+
+def project_gate(rows, own, pair, halves):
+    sources, blocks, cap, depth = rows.shape
+    width = own.shape[0]
+    vmem = pl.BlockSpec(memory_space=pltpu.VMEM)
+    anywhere = pl.BlockSpec(memory_space=pl.ANY)
+    return pl.pallas_call(
+        gate_kernel,
+        out_shape=jax.ShapeDtypeStruct((sources * cap, width), jnp.bfloat16),
+        in_specs=[vmem] * 3 + [anywhere] * 3,
+        out_specs=vmem,
+        scratch_shapes=[
+            pltpu.VMEM((width, depth), jnp.bfloat16),
+            pltpu.VMEM((width, depth), jnp.bfloat16),
+            pltpu.SemaphoreType.DMA((3,)),
+        ],
+        compiler_params=pltpu.CompilerParams(vmem_limit_bytes=GRANT),
+        cost_estimate=pl.CostEstimate(
+            flops=2 * sources * cap * blocks * own.size,
+            bytes_accessed=2 * (rows.size + blocks * own.size + sources * cap * width),
+            transcendentals=0,
+        ),
+    )(rows, *pair, own, *[pltpu.with_memory_space_constraint(half, pltpu.HBM) for half in halves])
 
 
 def expand_kernel(order_ref, hidden_ref, own_ref, after_ref, before_ref, across_ref, out_ref):
@@ -152,25 +184,32 @@
     total_rows = y_size * CAP
 
     gate_own = w_gate[0]
+    width = gate_own.shape[0]
     gate_pair = beside(gate_own)
     gate_halves = across(gate_pair)
-    up_own, _ = lax.optimization_barrier((w_up[0], gate_pair))
-    up_pair = beside(up_own)
+    up_own = w_up[0]
+    half = width // 2
+    up_low, up_high, _ = lax.optimization_barrier((up_own[:half], up_own[half:], gate_pair))
+    after_low = shift(up_low, "x", -1)
+    before_high = shift(up_high, "x", 1)
+    after_high = shift(up_high, "x", -1)
+    before_low = shift(up_low, "x", 1)
+    up_across = shift(after_low, "x", -1), shift(before_high, "x", 1)
+    down_last, _ = lax.optimization_barrier((w_down[0], up_across[0]))
+    down_across = (shift(down_last, "x", 2),)
 
     def share(term):
         parts = lax.all_to_all(term, "zh", split_axis=0, concat_axis=0, tiled=True)
         parts = parts.reshape(zh_size, total_rows // zh_size, -1)
         return jnp.sum(parts.astype(jnp.float32), axis=0)
 
-    gate_term = project(rows, gate_own, gate_pair, gate_halves)
-    up_last, gate_term = lax.optimization_barrier((w_up[0], gate_term))
-    up_across = shift(up_last, "x", 2)
+    gate_term = project_gate(rows, gate_own, gate_pair, gate_halves)
     gate_share = share(gate_term)
-    up_open = project(rows, up_own, up_pair)
-    up_term = finish(rows, up_open, up_across)
+    up_pair = after_low, after_high, before_low, before_high
+    up_open = project((0, 1, 3), rows, width, jnp.float32, up_own, *up_pair)
+    up_term = project((2,), rows, width, jnp.bfloat16, up_open, *up_across)
     down_own, up_term = lax.optimization_barrier((w_down[0], up_term))
     down_pair = beside(down_own)
-    down_across = (shift(down_own, "x", 2),)
     up_share = share(up_term)
     hidden = (jax.nn.silu(gate_share) * up_share).astype(jnp.bfloat16)
     hidden_rows = lax.all_gather(hidden, "zh", axis=0, tiled=True)

time: 216 us -> 213 us (0.986)
  waiting for transfers between devices: 77.4 us -> 64.6 us
  blocking collectives: 47.8 us -> 54.5 us
  local copies, waits for them, and re-layouts: 4.04 us -> 6.67 us
    ppermute x10 -> x13, waiting for transfers between devices: 54.8 us -> 39.4 us  [shift(): lax.ppermute(array, axis, [(i, (i + step) % size) for i in range(size)])]
    ppermute x10 -> x13, starting transfers between devices: 28.9 us -> 34.7 us  [shift(): lax.ppermute(array, axis, [(i, (i + step) % size) for i in range(size)])]
    all_to_all x1, blocking collectives: 32.2 us -> 37.8 us  [on_device(): lax.all_to_all(back.reshape(y_size * x_size, CAP, width_part), ('y', 'x')...]
    all_to_all x1, starting transfers between devices: 10.7 us -> 6.05 us  [on_device(): lax.all_to_all(back, LOCAL, split_axis=0, concat_axis=0, tiled=True)]
    all_to_all x2, waiting for transfers between devices: 8 us -> 10.6 us  [share(): parts = lax.all_to_all(term, 'zh', split_axis=0, concat_axis=0, tiled=True)]
    unnamed x14 -> x26, local copies, waits for them, and re-layouts: 1.78 us -> 4.29 us
  transfers between devices with their start and end apart: 15 -> 18, of which waited for: 10 -> 14; matrix products, arithmetic and copies ran while one was open for 2% -> 2% of each run, Pallas kernels for 1% -> 3%
where the time goes in v7:
time: 213 us; the launch traced here: 212 us
  starting transfers between devices  68.9 us (32%)
  waiting for transfers between devices  64.6 us (30%)
  blocking collectives  54.5 us (26%)
  Pallas kernels  10.6 us (5%)
  local copies, waits for them, and re-layouts  6.67 us (3%)
  other arithmetic  5.39 us (3%)
    ppermute x13, waiting for transfers between devices, shift(): lax.ppermute(array, axis, [(i, (i + step) % size) for i in range(size)])  39.4 us
    all_to_all x1, blocking collectives, on_device(): lax.all_to_all(back.reshape(y_size * x_size, CAP, width_part), ('y', 'x')...  37.8 us
    ppermute x13, starting transfers between devices, shift(): lax.ppermute(array, axis, [(i, (i + step) % size) for i in range(size)])  34.7 us
    all_gather x1, blocking collectives, on_device(): hidden_rows = lax.all_gather(hidden, 'zh', axis=0, tiled=True)  16.7 us
    all_to_all x2, starting transfers between devices, share(): parts = lax.all_to_all(term, 'zh', split_axis=0, concat_axis=0, tiled=True)  13.6 us
    all_to_all x1, waiting for transfers between devices, on_device(): lax.all_to_all(sent.reshape(EXPERTS * x_size, CAP, width_part), LOCAL + (...  10.9 us
    all_to_all x2, waiting for transfers between devices, share(): parts = lax.all_to_all(term, 'zh', split_axis=0, concat_axis=0, tiled=True)  10.6 us
    all_to_all x1, starting transfers between devices, on_device(): lax.all_to_all(sent.reshape(EXPERTS * x_size, CAP, width_part), LOCAL + (...  10.2 us
  transfers between devices with their start and end apart: 18, of which 14 were waited for; matrix products, arithmetic and copies ran while one was open for 2% of the time, Pallas kernels for 3%

profile of v7, /device:TPU:1, one launch (start us, length us, event | category | flops | bytes accessed | tf_op | source)
XLA Modules:
  0.0 212.1 jit_solution(11207893859810565739)
XLA Ops:
  2.2 10.2 %all-to-all-start = ((bf16[16,48,384]{2,1,0:T(8,128)(2,1)}), bf16[16,48,384]{2,1,0:T(8,128)(2,1)S(1)}, u32[]{:S(2)}, u32[]{:S(2)}) async-start(bf16[16,48,384]{2,1,0:T(8,128)(2,1)} %bitcast.5), calls=%async_computation | async-start | bytes 1179648 | tf_op jit(solution)/shard_map/all_to_all | solution.py:172
  12.4 10.9 %all-to-all-done = bf16[16,48,384]{2,1,0:T(8,128)(2,1)S(1)} async-done(((bf16[16,48,384]{2,1,0:T(8,128)(2,1)}), bf16[16,48,384]{2,1,0:T(8,128)(2,1)S(1)}, u32[]{:S(2)}, u32[]{:S(2)}) %all-to-all-start) | async-done | bytes 589856 | tf_op jit(solution)/shard_map/all_to_all | solution.py:172
  24.6 4.3 %all-to-all-start.1 = ((bf16[8,4,48,384]{3,2,1,0:T(8,128)(2,1)}), bf16[8,4,48,384]{3,2,1,0:T(8,128)(2,1)S(1)}, u32[]{:S(2)}, u32[]{:S(2)}) async-start(bf16[8,4,48,384]{3,2,1,0:T(8,128)(2,1)} %broadcast_in_dim.19), calls=%async_computation.1 | async-start | bytes 2359296 | tf_op jit(solution)/shard_map/all_to_all | solution.py:183
  28.8 2.6 %collective-permute-start = (bf16[1024,384]{1,0:T(8,128)(2,1)}, bf16[1024,384]{1,0:T(8,128)(2,1)S(1)}, u32[]{:S(2)}, u32[]{:S(2)}) collective-permute-start(bf16[1024,384]{1,0:T(8,128)(2,1)} %bitcast.35), channel_id=1, source_target_pairs={{0,12},{4,0},{8,4},{12,8},{1,13},{5,1},{9,5},{13,9},{2,14},{6,2},{... | collective-permute-start | bytes 2359304 | tf_op jit(solution)/shard_map/ppermute | solution.py:21
  31.4 2.7 %collective-permute-start.1 = (bf16[1024,384]{1,0:T(8,128)(2,1)}, bf16[1024,384]{1,0:T(8,128)(2,1)S(1)}, u32[]{:S(2)}, u32[]{:S(2)}) collective-permute-start(bf16[1024,384]{1,0:T(8,128)(2,1)} %bitcast.36), channel_id=1, source_target_pairs={{0,4},{4,8},{8,12},{12,0},{1,5},{5,9},{9,13},{13,1},{2,6},{6,10},{... | collective-permute-start | bytes 2359304 | tf_op jit(solution)/shard_map/ppermute | solution.py:21
  34.2 15.0 %collective-permute-done.after_ref = bf16[1024,384]{1,0:T(8,128)(2,1)S(1)} collective-permute-done((bf16[1024,384]{1,0:T(8,128)(2,1)}, bf16[1024,384]{1,0:T(8,128)(2,1)S(1)}, u32[]{:S(2)}, u32[]{:S(2)}) %collective-permute-start) | collective-permute-done | bytes 786464 | tf_op jit(solution)/shard_map/ppermute | solution.py:21
  49.2 4.1 %collective-permute-done.1.before_ref = bf16[1024,384]{1,0:T(8,128)(2,1)S(1)} collective-permute-done((bf16[1024,384]{1,0:T(8,128)(2,1)}, bf16[1024,384]{1,0:T(8,128)(2,1)S(1)}, u32[]{:S(2)}, u32[]{:S(2)}) %collective-permute-start.1) | collective-permute-done | bytes 786464 | tf_op jit(solution)/shard_map/ppermute | solution.py:21
  55.2 3.4 %collective-permute-start.7 = (bf16[512,384]{1,0:T(8,128)(2,1)S(1)}, bf16[512,384]{1,0:T(8,128)(2,1)}, u32[]{:S(2)}, u32[]{:S(2)}) collective-permute-start(bf16[512,384]{1,0:T(8,128)(2,1)S(1)} %get-tuple-element.11), channel_id=1, source_target_pairs={{0,4},{4,8},{8,12},{12,0},{1,5},{5,9},{9,13},{13,1},{2,6},{6,10},{... | collective-permute-start | bytes 1179656 | tf_op jit(solution)/shard_map/ppermute | solution.py:21
  58.6 3.1 %collective-permute-start.5 = (bf16[512,384]{1,0:T(8,128)(2,1)S(1)}, bf16[512,384]{1,0:T(8,128)(2,1)S(1)}, u32[]{:S(2)}, u32[]{:S(2)}) collective-permute-start(bf16[512,384]{1,0:T(8,128)(2,1)S(1)} %get-tuple-element.11), channel_id=1, source_target_pairs={{0,12},{4,0},{8,4},{12,8},{1,13},{5,1},{9,5},{13,9},{2,14},{6,2},{... | collective-permute-start | bytes 1179656 | tf_op jit(solution)/shard_map/ppermute | solution.py:21
  61.7 2.2 %collective-permute-start.6 = (bf16[512,384]{1,0:T(8,128)(2,1)S(1)}, bf16[512,384]{1,0:T(8,128)(2,1)S(1)}, u32[]{:S(2)}, u32[]{:S(2)}) collective-permute-start(bf16[512,384]{1,0:T(8,128)(2,1)S(1)} %get-tuple-element.10), channel_id=1, source_target_pairs={{0,4},{4,8},{8,12},{12,0},{1,5},{5,9},{9,13},{13,1},{2,6},{6,10},{... | collective-permute-start | bytes 1179656 | tf_op jit(solution)/shard_map/ppermute | solution.py:21
  64.5 3.7 %collective-permute-start.8 = (bf16[512,384]{1,0:T(8,128)(2,1)S(1)}, bf16[512,384]{1,0:T(8,128)(2,1)}, u32[]{:S(2)}, u32[]{:S(2)}) collective-permute-start(bf16[512,384]{1,0:T(8,128)(2,1)S(1)} %collective-permute-done.4.refs_1_), channel_id=1, source_target_pairs={{0,12},{4,0},{8,4},{12,8},{1,13},{5,1},{9,5},{13,9},{2,14},{6,2},{... | collective-permute-start | bytes 1179656 | tf_op jit(solution)/shard_map/ppermute | solution.py:21
  70.2 2.7 %collective-permute-done.5.refs_2_ = bf16[512,384]{1,0:T(8,128)(2,1)S(1)} collective-permute-done((bf16[512,384]{1,0:T(8,128)(2,1)S(1)}, bf16[512,384]{1,0:T(8,128)(2,1)S(1)}, u32[]{:S(2)}, u32[]{:S(2)}) %collective-permute-start.5) | collective-permute-done | bytes 393248 | tf_op jit(solution)/shard_map/ppermute | solution.py:21
  73.6 2.4 %collective-permute-done.6.refs_3_ = bf16[512,384]{1,0:T(8,128)(2,1)S(1)} collective-permute-done((bf16[512,384]{1,0:T(8,128)(2,1)S(1)}, bf16[512,384]{1,0:T(8,128)(2,1)S(1)}, u32[]{:S(2)}, u32[]{:S(2)}) %collective-permute-start.6) | collective-permute-done | bytes 393248 | tf_op jit(solution)/shard_map/ppermute | solution.py:21
  78.7 2.4 %shard_map.65.refs_0_ = f32[384,1024]{1,0:T(8,128)S(1)} custom-call(bf16[8,4,48,384]{3,2,1,0:T(8,128)(2,1)S(1)} %all-to-all-done.1.rows_ref, bf16[1024,384]{1,0:T(8,128)(2,1)S(1)} %bitcast.34, bf16[512,384]{1,0:T(8,128)(2,1)S(1)} %collective-permute-done.4.refs_1_, bf16[512,384]{1,0:T(8,128)(2,1)S(1)} %copy-done.7, bf16[512,384]{1,0:T(8,128)(2,1)S(1)} %copy-done.9, ...), custom_call_target="tpu_custom_call" | custom-call | flops 905969664 | bytes 4325376 | tf_op jit(solution)/shard_map/pallas_call | solution.py:69
  81.4 3.1 %collective-permute-done.9.refs_2_ = bf16[512,384]{1,0:T(8,128)(2,1)} collective-permute-done((bf16[512,384]{1,0:T(8,128)(2,1)}, bf16[512,384]{1,0:T(8,128)(2,1)}, u32[]{:S(2)}, u32[]{:S(2)}) %collective-permute-start.9) | collective-permute-done | bytes 393248 | tf_op jit(solution)/shard_map/ppermute | solution.py:21
  84.5 2.6 %shard_map.66 = bf16[384,1024]{1,0:T(8,128)(2,1)} custom-call(bf16[8,4,48,384]{3,2,1,0:T(8,128)(2,1)S(1)} %all-to-all-done.1.rows_ref, f32[384,1024]{1,0:T(8,128)S(1)} %shard_map.65.refs_0_, bf16[512,384]{1,0:T(8,128)(2,1)} %collective-permute-done.8.refs_1_, bf16[512,384]{1,0:T(8,128)(2,1)} %collective-permute-done.9.refs_2_), custom_call_target="tpu_custom_call" | custom-call | flops 603979776 | bytes 3538944 | tf_op jit(solution)/shard_map/pallas_call | solution.py:69
  87.1 9.3 %all-to-all-start.3 = ((bf16[4,96,1024]{2,1,0:T(8,128)(2,1)}), bf16[4,96,1024]{2,1,0:T(8,128)(2,1)}, u32[]{:S(2)}, u32[]{:S(2)}) async-start(bf16[4,96,1024]{2,1,0:T(8,128)(2,1)} %bitcast.17), calls=%async_computation.3 | async-start | bytes 1572864 | tf_op jit(solution)/shard_map/all_to_all | solution.py:202
  98.5 3.4 %collective-permute-start.3 = (bf16[512,384]{1,0:T(8,128)(2,1)S(1)}, bf16[512,384]{1,0:T(8,128)(2,1)S(1)}, u32[]{:S(2)}, u32[]{:S(2)}) collective-permute-start(bf16[512,384]{1,0:T(8,128)(2,1)S(1)} %slice.25), channel_id=1, source_target_pairs={{0,4},{4,8},{8,12},{12,0},{1,5},{5,9},{9,13},{13,1},{2,6},{6,10},{... | collective-permute-start | bytes 1179656 | tf_op jit(solution)/shard_map/ppermute | solution.py:21
  101.9 4.8 %collective-permute-done.2.low_ref = bf16[512,384]{1,0:T(8,128)(2,1)S(1)} collective-permute-done((bf16[512,384]{1,0:T(8,128)(2,1)S(1)}, bf16[512,384]{1,0:T(8,128)(2,1)S(1)}, u32[]{:S(2)}, u32[]{:S(2)}) %collective-permute-start.2) | collective-permute-done | bytes 393248 | tf_op jit(solution)/shard_map/ppermute | solution.py:21
  106.7 3.2 %collective-permute-done.3.high_ref = bf16[512,384]{1,0:T(8,128)(2,1)S(1)} collective-permute-done((bf16[512,384]{1,0:T(8,128)(2,1)S(1)}, bf16[512,384]{1,0:T(8,128)(2,1)S(1)}, u32[]{:S(2)}, u32[]{:S(2)}) %collective-permute-start.3) | collective-permute-done | bytes 393248 | tf_op jit(solution)/shard_map/ppermute | solution.py:21
  110.6 3.2 %shard_map.64 = bf16[384,1024]{1,0:T(8,128)(2,1)} custom-call(bf16[8,4,48,384]{3,2,1,0:T(8,128)(2,1)S(1)} %all-to-all-done.1.rows_ref, bf16[1024,384]{1,0:T(8,128)(2,1)S(1)} %collective-permute-done.after_ref, bf16[1024,384]{1,0:T(8,128)(2,1)S(1)} %copy-done.3, bf16[1024,384]{1,0:T(8,128)(2,1)S(1)} %bitcast.37, bf16[512,384]{1,0:T(8,128)(2,1)} %copy-done.11, ...), custom_call_target="tpu_custom_call" | custom-call | flops 1207959552 | bytes 5111808 | tf_op jit(solution)/shard_map/pallas_call | solution.py:106
  113.9 2.3 %all-to-all-done.3 = bf16[4,96,1024]{2,1,0:T(8,128)(2,1)} async-done(((bf16[4,96,1024]{2,1,0:T(8,128)(2,1)}), bf16[4,96,1024]{2,1,0:T(8,128)(2,1)}, u32[]{:S(2)}, u32[]{:S(2)}) %all-to-all-start.3) | async-done | bytes 786464 | tf_op jit(solution)/shard_map/all_to_all | solution.py:202
  116.2 4.4 %all-to-all-start.2 = ((bf16[4,96,1024]{2,1,0:T(8,128)(2,1)}), bf16[4,96,1024]{2,1,0:T(8,128)(2,1)}, u32[]{:S(2)}, u32[]{:S(2)}) async-start(bf16[4,96,1024]{2,1,0:T(8,128)(2,1)} %bitcast.12), calls=%async_computation.2 | async-start | bytes 1572864 | tf_op jit(solution)/shard_map/all_to_all | solution.py:202
  120.7 2.5 %collective-permute-start.12 = (bf16[1024,384]{1,0:T(8,128)(2,1)S(1)}, bf16[1024,384]{1,0:T(8,128)(2,1)S(1)}, u32[]{:S(2)}, u32[]{:S(2)}) collective-permute-start(bf16[1024,384]{1,0:T(8,128)(2,1)S(1)} %bitcast.38), channel_id=1, source_target_pairs={{0,8},{4,12},{8,0},{12,4},{1,9},{5,13},{9,1},{13,5},{2,10},{6,14},... | collective-permute-start | bytes 2359304 | tf_op jit(solution)/shard_map/ppermute | solution.py:21
  123.2 3.4 %collective-permute-start.10 = (bf16[1024,384]{1,0:T(8,128)(2,1)S(1)}, bf16[1024,384]{1,0:T(8,128)(2,1)S(1)}, u32[]{:S(2)}, u32[]{:S(2)}) collective-permute-start(bf16[1024,384]{1,0:T(8,128)(2,1)S(1)} %bitcast.39), channel_id=1, source_target_pairs={{0,12},{4,0},{8,4},{12,8},{1,13},{5,1},{9,5},{13,9},{2,14},{6,2},{... | collective-permute-start | bytes 2359304 | tf_op jit(solution)/shard_map/ppermute | solution.py:21
  130.6 8.2 %all-to-all-done.2 = bf16[4,96,1024]{2,1,0:T(8,128)(2,1)} async-done(((bf16[4,96,1024]{2,1,0:T(8,128)(2,1)}), bf16[4,96,1024]{2,1,0:T(8,128)(2,1)}, u32[]{:S(2)}, u32[]{:S(2)}) %all-to-all-start.2) | async-done | bytes 786464 | tf_op jit(solution)/shard_map/all_to_all | solution.py:202
  140.4 16.7 %all_gather.3.hidden_ref = bf16[384,1024]{1,0:T(8,128)(2,1)S(1)} all-gather(bf16[96,1024]{1,0:T(8,128)(2,1)S(1)} %multiply_convert_fusion), channel_id=1, replica_groups=mesh['y'=8,'zl'=2,'core'=2,'x'=4,'zh'=4] {'zh'}, dimensions={0}, use_global_device_ids=true | all-gather | bytes 983040 | tf_op jit(solution)/shard_map/all_gather | solution.py:215
  157.1 3.3 %collective-permute-done.11.before_ref = bf16[1024,384]{1,0:T(8,128)(2,1)S(1)} collective-permute-done((bf16[1024,384]{1,0:T(8,128)(2,1)S(1)}, bf16[1024,384]{1,0:T(8,128)(2,1)S(1)}, u32[]{:S(2)}, u32[]{:S(2)}) %collective-permute-start.11) | collective-permute-done | bytes 786464 | tf_op jit(solution)/shard_map/ppermute | solution.py:21
  160.4 2.3 %shard_map.67 = bf16[8,4,48,384]{3,2,1,0:T(8,128)(2,1)S(1)} custom-call(s32[4]{0:T(128)S(1)} %pad_add_fusion.order_ref, bf16[384,1024]{1,0:T(8,128)(2,1)S(1)} %all_gather.3.hidden_ref, bf16[1024,384]{1,0:T(8,128)(2,1)S(1)} %bitcast.41, bf16[1024,384]{1,0:T(8,128)(2,1)S(1)} %collective-permute-done.10.after_ref, ...), custom_call_target="tpu_custom_call" | custom-call | flops 1207959552 | bytes 5111808 | tf_op jit(solution)/shard_map/pallas_call | solution.py:139
  162.7 37.8 %all_to_all.38 = bf16[32,48,384]{2,1,0:T(8,128)(2,1)S(1)} all-to-all(bf16[32,48,384]{2,1,0:T(8,128)(2,1)S(1)} %bitcast.33), channel_id=1, replica_groups=mesh['y'=8,'zl'=2,'core'=2,'x'=4,'zh'=4] {'y','x'}, dimensions={0} | all-to-all | bytes 2359296 | tf_op jit(solution)/shard_map/all_to_all | solution.py:217
  201.3 6.1 %all-to-all-start.5 = ((bf16[4,48,384]{2,1,0:T(8,128)(2,1)}), bf16[4,48,384]{2,1,0:T(8,128)(2,1)S(1)}, u32[]{:S(2)}, u32[]{:S(2)}) async-start(bf16[4,48,384]{2,1,0:T(8,128)(2,1)} %reduce_sum.52), calls=%async_computation.5 | async-start | bytes 294912 | tf_op jit(solution)/shard_map/all_to_all | solution.py:225
  207.4 3.7 %all-to-all-done.5 = bf16[4,48,384]{2,1,0:T(8,128)(2,1)S(1)} async-done(((bf16[4,48,384]{2,1,0:T(8,128)(2,1)}), bf16[4,48,384]{2,1,0:T(8,128)(2,1)S(1)}, u32[]{:S(2)}, u32[]{:S(2)}) %all-to-all-start.5) | async-done | bytes 147488 | tf_op jit(solution)/shard_map/all_to_all | solution.py:225
  (57 shorter events, 21.9 us)
Async XLA Ops:
  0.0 1.1 copy-start
  2.2 21.1 %all-to-all-start = ((bf16[16,48,384]{2,1,0:T(8,128)(2,1)}), bf16[16,48,384]{2,1,0:T(8,128)(2,1)S(1)}, u32[]{:S(2)}, u32[]{:S(2)}) async-start(bf16[16,48,384]{2,1,0:T(8,128)(2,1)} %bitcast.5), calls=%async_computation | async-start | bytes 1179648 | tf_op jit(solution)/shard_map/all_to_all | solution.py:172
  24.6 9.6 %copy-start.1 = (bf16[1,1024,384]{2,1,0:T(8,128)(2,1)S(1)}, bf16[1,1024,384]{2,1,0:T(8,128)(2,1)}, u32[]{:S(2)}) copy-start(bf16[1,1024,384]{2,1,0:T(8,128)(2,1)} %param.10) | copy-start | bytes 2359300
  24.6 52.2 %all-to-all-start.1 = ((bf16[8,4,48,384]{3,2,1,0:T(8,128)(2,1)}), bf16[8,4,48,384]{3,2,1,0:T(8,128)(2,1)S(1)}, u32[]{:S(2)}, u32[]{:S(2)}) async-start(bf16[8,4,48,384]{3,2,1,0:T(8,128)(2,1)} %broadcast_in_dim.19), calls=%async_computation.1 | async-start | bytes 2359296 | tf_op jit(solution)/shard_map/all_to_all | solution.py:183
  28.8 20.4 %collective-permute-start = (bf16[1024,384]{1,0:T(8,128)(2,1)}, bf16[1024,384]{1,0:T(8,128)(2,1)S(1)}, u32[]{:S(2)}, u32[]{:S(2)}) collective-permute-start(bf16[1024,384]{1,0:T(8,128)(2,1)} %bitcast.35), channel_id=1, source_target_pairs={{0,12},{4,0},{8,4},{12,8},{1,13},{5,1},{9,5},{13,9},{2,14},{6,2},{... | collective-permute-start | bytes 2359304 | tf_op jit(solution)/shard_map/ppermute | solution.py:21
  31.4 21.9 %collective-permute-start.1 = (bf16[1024,384]{1,0:T(8,128)(2,1)}, bf16[1024,384]{1,0:T(8,128)(2,1)S(1)}, u32[]{:S(2)}, u32[]{:S(2)}) collective-permute-start(bf16[1024,384]{1,0:T(8,128)(2,1)} %bitcast.36), channel_id=1, source_target_pairs={{0,4},{4,8},{8,12},{12,0},{1,5},{5,9},{9,13},{13,1},{2,6},{6,10},{... | collective-permute-start | bytes 2359304 | tf_op jit(solution)/shard_map/ppermute | solution.py:21
  53.3 19.6 %copy-start.2 = (bf16[1024,384]{1,0:T(8,128)(2,1)}, bf16[1024,384]{1,0:T(8,128)(2,1)S(1)}, u32[]{:S(2)}) copy-start(bf16[1024,384]{1,0:T(8,128)(2,1)S(1)} %collective-permute-done.1.before_ref) | copy-start | bytes 2359300
  53.3 11.2 %collective-permute-start.4 = (bf16[512,384]{1,0:T(8,128)(2,1)S(1)}, bf16[512,384]{1,0:T(8,128)(2,1)S(1)}, u32[]{:S(2)}, u32[]{:S(2)}) collective-permute-start(bf16[512,384]{1,0:T(8,128)(2,1)S(1)} %get-tuple-element.10), channel_id=1, source_target_pairs={{0,12},{4,0},{8,4},{12,8},{1,13},{5,1},{9,5},{13,9},{2,14},{6,2},{... | collective-permute-start | bytes 1179656 | tf_op jit(solution)/shard_map/ppermute | solution.py:21
  55.2 13.0 %collective-permute-start.7 = (bf16[512,384]{1,0:T(8,128)(2,1)S(1)}, bf16[512,384]{1,0:T(8,128)(2,1)}, u32[]{:S(2)}, u32[]{:S(2)}) collective-permute-start(bf16[512,384]{1,0:T(8,128)(2,1)S(1)} %get-tuple-element.11), channel_id=1, source_target_pairs={{0,4},{4,8},{8,12},{12,0},{1,5},{5,9},{9,13},{13,1},{2,6},{6,10},{... | collective-permute-start | bytes 1179656 | tf_op jit(solution)/shard_map/ppermute | solution.py:21
  58.6 14.3 %collective-permute-start.5 = (bf16[512,384]{1,0:T(8,128)(2,1)S(1)}, bf16[512,384]{1,0:T(8,128)(2,1)S(1)}, u32[]{:S(2)}, u32[]{:S(2)}) collective-permute-start(bf16[512,384]{1,0:T(8,128)(2,1)S(1)} %get-tuple-element.11), channel_id=1, source_target_pairs={{0,12},{4,0},{8,4},{12,8},{1,13},{5,1},{9,5},{13,9},{2,14},{6,2},{... | collective-permute-start | bytes 1179656 | tf_op jit(solution)/shard_map/ppermute | solution.py:21
  61.7 14.3 %collective-permute-start.6 = (bf16[512,384]{1,0:T(8,128)(2,1)S(1)}, bf16[512,384]{1,0:T(8,128)(2,1)S(1)}, u32[]{:S(2)}, u32[]{:S(2)}) collective-permute-start(bf16[512,384]{1,0:T(8,128)(2,1)S(1)} %get-tuple-element.10), channel_id=1, source_target_pairs={{0,4},{4,8},{8,12},{12,0},{1,5},{5,9},{9,13},{13,1},{2,6},{6,10},{... | collective-permute-start | bytes 1179656 | tf_op jit(solution)/shard_map/ppermute | solution.py:21
  64.5 16.9 %collective-permute-start.8 = (bf16[512,384]{1,0:T(8,128)(2,1)S(1)}, bf16[512,384]{1,0:T(8,128)(2,1)}, u32[]{:S(2)}, u32[]{:S(2)}) collective-permute-start(bf16[512,384]{1,0:T(8,128)(2,1)S(1)} %collective-permute-done.4.refs_1_), channel_id=1, source_target_pairs={{0,12},{4,0},{8,4},{12,8},{1,13},{5,1},{9,5},{13,9},{2,14},{6,2},{... | collective-permute-start | bytes 1179656 | tf_op jit(solution)/shard_map/ppermute | solution.py:21
  68.2 16.3 %collective-permute-start.9 = (bf16[512,384]{1,0:T(8,128)(2,1)}, bf16[512,384]{1,0:T(8,128)(2,1)}, u32[]{:S(2)}, u32[]{:S(2)}) collective-permute-start(bf16[512,384]{1,0:T(8,128)(2,1)} %collective-permute-done.7.refs_4_), channel_id=1, source_target_pairs={{0,4},{4,8},{8,12},{12,0},{1,5},{5,9},{9,13},{13,1},{2,6},{6,10},{... | collective-permute-start | bytes 1179656 | tf_op jit(solution)/shard_map/ppermute | solution.py:21
  72.8 0.8 copy-start.6
  76.0 0.8 copy-start.8
  76.7 1.0 copy-start.7
  77.7 1.0 copy-start.9
  87.1 11.4 %copy-start.3 = (bf16[1024,384]{1,0:T(8,128)(2,1)S(1)}, bf16[1024,384]{1,0:T(8,128)(2,1)}, u32[]{:S(2)}) copy-start(bf16[1024,384]{1,0:T(8,128)(2,1)} %copy-done.2) | copy-start | bytes 2359300
  87.1 29.1 %all-to-all-start.3 = ((bf16[4,96,1024]{2,1,0:T(8,128)(2,1)}), bf16[4,96,1024]{2,1,0:T(8,128)(2,1)}, u32[]{:S(2)}, u32[]{:S(2)}) async-start(bf16[4,96,1024]{2,1,0:T(8,128)(2,1)} %bitcast.17), calls=%async_computation.3 | async-start | bytes 1572864 | tf_op jit(solution)/shard_map/all_to_all | solution.py:202
  96.4 14.3 %copy-start.4 = (bf16[1,1024,384]{2,1,0:T(8,128)(2,1)S(1)}, bf16[1,1024,384]{2,1,0:T(8,128)(2,1)}, u32[]{:S(2)}) copy-start(bf16[1,1024,384]{2,1,0:T(8,128)(2,1)} %param.9) | copy-start | bytes 2359300
  96.4 10.2 %collective-permute-start.2 = (bf16[512,384]{1,0:T(8,128)(2,1)S(1)}, bf16[512,384]{1,0:T(8,128)(2,1)S(1)}, u32[]{:S(2)}, u32[]{:S(2)}) collective-permute-start(bf16[512,384]{1,0:T(8,128)(2,1)S(1)} %slice.24), channel_id=1, source_target_pairs={{0,12},{4,0},{8,4},{12,8},{1,13},{5,1},{9,5},{13,9},{2,14},{6,2},{... | collective-permute-start | bytes 1179656 | tf_op jit(solution)/shard_map/ppermute | solution.py:21
  98.5 11.3 %collective-permute-start.3 = (bf16[512,384]{1,0:T(8,128)(2,1)S(1)}, bf16[512,384]{1,0:T(8,128)(2,1)S(1)}, u32[]{:S(2)}, u32[]{:S(2)}) collective-permute-start(bf16[512,384]{1,0:T(8,128)(2,1)S(1)} %slice.25), channel_id=1, source_target_pairs={{0,4},{4,8},{8,12},{12,0},{1,5},{5,9},{9,13},{13,1},{2,6},{6,10},{... | collective-permute-start | bytes 1179656 | tf_op jit(solution)/shard_map/ppermute | solution.py:21
  106.7 3.2 %copy-start.11 = (bf16[512,384]{1,0:T(8,128)(2,1)}, bf16[512,384]{1,0:T(8,128)(2,1)S(1)}, u32[]{:S(2)}) copy-start(bf16[512,384]{1,0:T(8,128)(2,1)S(1)} %collective-permute-done.2.low_ref) | copy-start | bytes 1179652
  109.9 0.8 copy-start.12
  113.9 6.8 %copy-start.5 = (bf16[1,1024,384]{2,1,0:T(8,128)(2,1)S(1)}, bf16[1,1024,384]{2,1,0:T(8,128)(2,1)}, u32[]{:S(2)}) copy-start(bf16[1,1024,384]{2,1,0:T(8,128)(2,1)} %param.11) | copy-start | bytes 2359300
  116.2 22.7 %all-to-all-start.2 = ((bf16[4,96,1024]{2,1,0:T(8,128)(2,1)}), bf16[4,96,1024]{2,1,0:T(8,128)(2,1)}, u32[]{:S(2)}, u32[]{:S(2)}) async-start(bf16[4,96,1024]{2,1,0:T(8,128)(2,1)} %bitcast.12), calls=%async_computation.2 | async-start | bytes 1572864 | tf_op jit(solution)/shard_map/all_to_all | solution.py:202
  120.7 36.4 %collective-permute-start.12 = (bf16[1024,384]{1,0:T(8,128)(2,1)S(1)}, bf16[1024,384]{1,0:T(8,128)(2,1)S(1)}, u32[]{:S(2)}, u32[]{:S(2)}) collective-permute-start(bf16[1024,384]{1,0:T(8,128)(2,1)S(1)} %bitcast.38), channel_id=1, source_target_pairs={{0,8},{4,12},{8,0},{12,4},{1,9},{5,13},{9,1},{13,5},{2,10},{6,14},... | collective-permute-start | bytes 2359304 | tf_op jit(solution)/shard_map/ppermute | solution.py:21
  123.2 33.9 %collective-permute-start.10 = (bf16[1024,384]{1,0:T(8,128)(2,1)S(1)}, bf16[1024,384]{1,0:T(8,128)(2,1)S(1)}, u32[]{:S(2)}, u32[]{:S(2)}) collective-permute-start(bf16[1024,384]{1,0:T(8,128)(2,1)S(1)} %bitcast.39), channel_id=1, source_target_pairs={{0,12},{4,0},{8,4},{12,8},{1,13},{5,1},{9,5},{13,9},{2,14},{6,2},{... | collective-permute-start | bytes 2359304 | tf_op jit(solution)/shard_map/ppermute | solution.py:21
  126.6 33.7 %collective-permute-start.11 = (bf16[1024,384]{1,0:T(8,128)(2,1)S(1)}, bf16[1024,384]{1,0:T(8,128)(2,1)S(1)}, u32[]{:S(2)}, u32[]{:S(2)}) collective-permute-start(bf16[1024,384]{1,0:T(8,128)(2,1)S(1)} %bitcast.40), channel_id=1, source_target_pairs={{0,4},{4,8},{8,12},{12,0},{1,5},{5,9},{9,13},{13,1},{2,6},{6,10},{... | collective-permute-start | bytes 2359304 | tf_op jit(solution)/shard_map/ppermute | solution.py:21
  138.9 1.4 copy-start.10
  201.3 9.8 %all-to-all-start.5 = ((bf16[4,48,384]{2,1,0:T(8,128)(2,1)}), bf16[4,48,384]{2,1,0:T(8,128)(2,1)S(1)}, u32[]{:S(2)}, u32[]{:S(2)}) async-start(bf16[4,48,384]{2,1,0:T(8,128)(2,1)} %reduce_sum.52), calls=%async_computation.5 | async-start | bytes 294912 | tf_op jit(solution)/shard_map/all_to_all | solution.py:225

commit v8 on v7

--- a/solution.py
+++ b/solution.py
@@ -187,16 +187,9 @@
     width = gate_own.shape[0]
     gate_pair = beside(gate_own)
     gate_halves = across(gate_pair)
-    up_own = w_up[0]
-    half = width // 2
-    up_low, up_high, _ = lax.optimization_barrier((up_own[:half], up_own[half:], gate_pair))
-    after_low = shift(up_low, "x", -1)
-    before_high = shift(up_high, "x", 1)
-    after_high = shift(up_high, "x", -1)
-    before_low = shift(up_low, "x", 1)
-    up_across = shift(after_low, "x", -1), shift(before_high, "x", 1)
-    down_last, _ = lax.optimization_barrier((w_down[0], up_across[0]))
-    down_across = (shift(down_last, "x", 2),)
+    up_own, _ = lax.optimization_barrier((w_up[0], gate_pair))
+    up_pair = beside(up_own)
+    up_across = across(up_pair)
 
     def share(term):
         parts = lax.all_to_all(term, "zh", split_axis=0, concat_axis=0, tiled=True)
@@ -205,11 +198,11 @@
 
     gate_term = project_gate(rows, gate_own, gate_pair, gate_halves)
     gate_share = share(gate_term)
-    up_pair = after_low, after_high, before_low, before_high
     up_open = project((0, 1, 3), rows, width, jnp.float32, up_own, *up_pair)
     up_term = project((2,), rows, width, jnp.bfloat16, up_open, *up_across)
     down_own, up_term = lax.optimization_barrier((w_down[0], up_term))
     down_pair = beside(down_own)
+    down_across = (shift(down_own, "x", 2),)
     up_share = share(up_term)
     hidden = (jax.nn.silu(gate_share) * up_share).astype(jnp.bfloat16)
     hidden_rows = lax.all_gather(hidden, "zh", axis=0, tiled=True)

time: 213 us -> 214 us (level)
  blocking collectives: 54.5 us -> 47.9 us
  waiting for transfers between devices: 64.6 us -> 71 us
    ppermute x13 -> x11, waiting for transfers between devices: 39.4 us -> 46.7 us  [shift(): lax.ppermute(array, axis, [(i, (i + step) % size) for i in range(size)])]
    ppermute x13 -> x11, starting transfers between devices: 34.7 us -> 28.9 us  [shift(): lax.ppermute(array, axis, [(i, (i + step) % size) for i in range(size)])]
    all_to_all x1, starting transfers between devices: 6.05 us -> 11.3 us  [on_device(): lax.all_to_all(back, LOCAL, split_axis=0, concat_axis=0, tiled=True)]
    all_to_all x1, blocking collectives: 37.8 us -> 33.3 us  [on_device(): lax.all_to_all(back.reshape(y_size * x_size, CAP, width_part), ('y', 'x')...]
    unnamed x26 -> x20, local copies, waits for them, and re-layouts: 4.29 us -> 4.34 us
  transfers between devices with their start and end apart: 18 -> 16, of which waited for: 14 -> 11; matrix products, arithmetic and copies ran while one was open for 2% -> 3% of each run, Pallas kernels for 3% -> 2%
where the time goes in v8:
time: 214 us; the launch traced here: 213 us
  waiting for transfers between devices  71 us (33%)
  starting transfers between devices  69.1 us (32%)
  blocking collectives  47.9 us (22%)
  Pallas kernels  9.7 us (5%)
  local copies, waits for them, and re-layouts  8.35 us (4%)
  other arithmetic  5.38 us (3%)
    ppermute x11, waiting for transfers between devices, shift(): lax.ppermute(array, axis, [(i, (i + step) % size) for i in range(size)])  46.7 us
    all_to_all x1, blocking collectives, on_device(): lax.all_to_all(back.reshape(y_size * x_size, CAP, width_part), ('y', 'x')...  33.3 us
    ppermute x11, starting transfers between devices, shift(): lax.ppermute(array, axis, [(i, (i + step) % size) for i in range(size)])  28.9 us
    all_gather x1, blocking collectives, on_device(): hidden_rows = lax.all_gather(hidden, 'zh', axis=0, tiled=True)  14.6 us
    all_to_all x2, starting transfers between devices, share(): parts = lax.all_to_all(term, 'zh', split_axis=0, concat_axis=0, tiled=True)  14.5 us
    all_to_all x1, starting transfers between devices, on_device(): lax.all_to_all(back, LOCAL, split_axis=0, concat_axis=0, tiled=True)  11.3 us
    all_to_all x1, waiting for transfers between devices, on_device(): lax.all_to_all(sent.reshape(EXPERTS * x_size, CAP, width_part), LOCAL + (...  10.9 us
    all_to_all x1, starting transfers between devices, on_device(): lax.all_to_all(sent.reshape(EXPERTS * x_size, CAP, width_part), LOCAL + (...  10.2 us
  transfers between devices with their start and end apart: 16, of which 11 were waited for; matrix products, arithmetic and copies ran while one was open for 3% of the time, Pallas kernels for 2%

profile of v8, /device:TPU:1, one launch (start us, length us, event | category | flops | bytes accessed | tf_op | source)
XLA Modules:
  0.0 212.8 jit_solution(9228401722079331175)
XLA Ops:
  2.2 10.2 %all-to-all-start = ((bf16[16,48,384]{2,1,0:T(8,128)(2,1)}), bf16[16,48,384]{2,1,0:T(8,128)(2,1)S(1)}, u32[]{:S(2)}, u32[]{:S(2)}) async-start(bf16[16,48,384]{2,1,0:T(8,128)(2,1)} %bitcast.5), calls=%async_computation | async-start | bytes 1179648 | tf_op jit(solution)/shard_map/all_to_all | solution.py:172
  12.4 10.9 %all-to-all-done = bf16[16,48,384]{2,1,0:T(8,128)(2,1)S(1)} async-done(((bf16[16,48,384]{2,1,0:T(8,128)(2,1)}), bf16[16,48,384]{2,1,0:T(8,128)(2,1)S(1)}, u32[]{:S(2)}, u32[]{:S(2)}) %all-to-all-start) | async-done | bytes 589856 | tf_op jit(solution)/shard_map/all_to_all | solution.py:172
  24.5 4.1 %all-to-all-start.1 = ((bf16[8,4,48,384]{3,2,1,0:T(8,128)(2,1)}), bf16[8,4,48,384]{3,2,1,0:T(8,128)(2,1)S(1)}, u32[]{:S(2)}, u32[]{:S(2)}) async-start(bf16[8,4,48,384]{3,2,1,0:T(8,128)(2,1)} %broadcast_in_dim.19), calls=%async_computation.1 | async-start | bytes 2359296 | tf_op jit(solution)/shard_map/all_to_all | solution.py:183
  28.7 2.6 %collective-permute-start = (bf16[1024,384]{1,0:T(8,128)(2,1)}, bf16[1024,384]{1,0:T(8,128)(2,1)S(1)}, u32[]{:S(2)}, u32[]{:S(2)}) collective-permute-start(bf16[1024,384]{1,0:T(8,128)(2,1)} %bitcast.11.own_ref), channel_id=1, source_target_pairs={{0,12},{4,0},{8,4},{12,8},{1,13},{5,1},{9,5},{13,9},{2,14},{6,2},{... | collective-permute-start | bytes 2359304 | tf_op jit(solution)/shard_map/ppermute | solution.py:21
  31.3 2.7 %collective-permute-start.1 = (bf16[1024,384]{1,0:T(8,128)(2,1)}, bf16[1024,384]{1,0:T(8,128)(2,1)S(1)}, u32[]{:S(2)}, u32[]{:S(2)}) collective-permute-start(bf16[1024,384]{1,0:T(8,128)(2,1)} %bitcast.11.own_ref), channel_id=1, source_target_pairs={{0,4},{4,8},{8,12},{12,0},{1,5},{5,9},{9,13},{13,1},{2,6},{6,10},{... | collective-permute-start | bytes 2359304 | tf_op jit(solution)/shard_map/ppermute | solution.py:21
  34.0 15.1 %collective-permute-done.after_ref = bf16[1024,384]{1,0:T(8,128)(2,1)S(1)} collective-permute-done((bf16[1024,384]{1,0:T(8,128)(2,1)}, bf16[1024,384]{1,0:T(8,128)(2,1)S(1)}, u32[]{:S(2)}, u32[]{:S(2)}) %collective-permute-start) | collective-permute-done | bytes 786464 | tf_op jit(solution)/shard_map/ppermute | solution.py:21
  49.1 4.1 %collective-permute-done.1.before_ref = bf16[1024,384]{1,0:T(8,128)(2,1)S(1)} collective-permute-done((bf16[1024,384]{1,0:T(8,128)(2,1)}, bf16[1024,384]{1,0:T(8,128)(2,1)S(1)}, u32[]{:S(2)}, u32[]{:S(2)}) %collective-permute-start.1) | collective-permute-done | bytes 786464 | tf_op jit(solution)/shard_map/ppermute | solution.py:21
  53.1 1.9 collective-permute-start.4
  55.0 3.4 %collective-permute-start.5 = (bf16[1024,384]{1,0:T(8,128)(2,1)}, bf16[1024,384]{1,0:T(8,128)(2,1)S(1)}, u32[]{:S(2)}, u32[]{:S(2)}) collective-permute-start(bf16[1024,384]{1,0:T(8,128)(2,1)} %bitcast.31), channel_id=1, source_target_pairs={{0,4},{4,8},{8,12},{12,0},{1,5},{5,9},{9,13},{13,1},{2,6},{6,10},{... | collective-permute-start | bytes 2359304 | tf_op jit(solution)/shard_map/ppermute | solution.py:21
  58.4 14.5 %collective-permute-done.4.refs_1_ = bf16[1024,384]{1,0:T(8,128)(2,1)S(1)} collective-permute-done((bf16[1024,384]{1,0:T(8,128)(2,1)}, bf16[1024,384]{1,0:T(8,128)(2,1)S(1)}, u32[]{:S(2)}, u32[]{:S(2)}) %collective-permute-start.4) | collective-permute-done | bytes 786464 | tf_op jit(solution)/shard_map/ppermute | solution.py:21
  73.8 3.4 %collective-permute-start.6 = (bf16[512,384]{1,0:T(8,128)(2,1)}, bf16[512,384]{1,0:T(8,128)(2,1)S(1)}, u32[]{:S(2)}, u32[]{:S(2)}) collective-permute-start(bf16[512,384]{1,0:T(8,128)(2,1)} %slice.18), channel_id=1, source_target_pairs={{0,12},{4,0},{8,4},{12,8},{1,13},{5,1},{9,5},{13,9},{2,14},{6,2},{... | collective-permute-start | bytes 1179656 | tf_op jit(solution)/shard_map/ppermute | solution.py:21
  78.2 1.9 collective-permute-start.7
  83.5 1.4 shard_map.65.refs_0_
  85.0 5.0 %collective-permute-done.7.refs_2_ = bf16[512,384]{1,0:T(8,128)(2,1)} collective-permute-done((bf16[512,384]{1,0:T(8,128)(2,1)}, bf16[512,384]{1,0:T(8,128)(2,1)}, u32[]{:S(2)}, u32[]{:S(2)}) %collective-permute-start.7) | collective-permute-done | bytes 393248 | tf_op jit(solution)/shard_map/ppermute | solution.py:21
  90.0 2.5 %shard_map.66 = bf16[384,1024]{1,0:T(8,128)(2,1)} custom-call(bf16[8,4,48,384]{3,2,1,0:T(8,128)(2,1)S(1)} %all-to-all-done.1.rows_ref, f32[384,1024]{1,0:T(8,128)S(1)} %shard_map.65.refs_0_, bf16[512,384]{1,0:T(8,128)(2,1)S(1)} %collective-permute-done.6.refs_1_, bf16[512,384]{1,0:T(8,128)(2,1)} %collective-permute-done.7.refs_2_), custom_call_target="tpu_custom_call" | custom-call | flops 603979776 | bytes 3538944 | tf_op jit(solution)/shard_map/pallas_call | solution.py:69
  92.5 9.1 %all-to-all-start.3 = ((bf16[4,96,1024]{2,1,0:T(8,128)(2,1)}), bf16[4,96,1024]{2,1,0:T(8,128)(2,1)}, u32[]{:S(2)}, u32[]{:S(2)}) async-start(bf16[4,96,1024]{2,1,0:T(8,128)(2,1)} %bitcast.15), calls=%async_computation.3 | async-start | bytes 1572864 | tf_op jit(solution)/shard_map/all_to_all | solution.py:195
  101.7 1.9 collective-permute-start.2
  103.6 3.4 %collective-permute-start.3 = (bf16[512,384]{1,0:T(8,128)(2,1)S(1)}, bf16[512,384]{1,0:T(8,128)(2,1)S(1)}, u32[]{:S(2)}, u32[]{:S(2)}) collective-permute-start(bf16[512,384]{1,0:T(8,128)(2,1)S(1)} %slice.17), channel_id=1, source_target_pairs={{0,4},{4,8},{8,12},{12,0},{1,5},{5,9},{9,13},{13,1},{2,6},{6,10},{... | collective-permute-start | bytes 1179656 | tf_op jit(solution)/shard_map/ppermute | solution.py:21
  107.0 3.9 %collective-permute-done.2.low_ref = bf16[512,384]{1,0:T(8,128)(2,1)S(1)} collective-permute-done((bf16[512,384]{1,0:T(8,128)(2,1)S(1)}, bf16[512,384]{1,0:T(8,128)(2,1)S(1)}, u32[]{:S(2)}, u32[]{:S(2)}) %collective-permute-start.2) | collective-permute-done | bytes 393248 | tf_op jit(solution)/shard_map/ppermute | solution.py:21
  110.9 3.2 %collective-permute-done.3.high_ref = bf16[512,384]{1,0:T(8,128)(2,1)S(1)} collective-permute-done((bf16[512,384]{1,0:T(8,128)(2,1)S(1)}, bf16[512,384]{1,0:T(8,128)(2,1)S(1)}, u32[]{:S(2)}, u32[]{:S(2)}) %collective-permute-start.3) | collective-permute-done | bytes 393248 | tf_op jit(solution)/shard_map/ppermute | solution.py:21
  114.9 3.5 %shard_map.64 = bf16[384,1024]{1,0:T(8,128)(2,1)} custom-call(bf16[8,4,48,384]{3,2,1,0:T(8,128)(2,1)S(1)} %all-to-all-done.1.rows_ref, bf16[1024,384]{1,0:T(8,128)(2,1)S(1)} %collective-permute-done.after_ref, bf16[1024,384]{1,0:T(8,128)(2,1)S(1)} %collective-permute-done.1.before_ref, bf16[1024,384]{1,0:T(8,128)(2,1)} %bitcast.11.own_ref, ...), custom_call_target="tpu_custom_call" | custom-call | flops 1207959552 | bytes 5111808 | tf_op jit(solution)/shard_map/pallas_call | solution.py:106
  119.5 5.4 %all-to-all-start.2 = ((bf16[4,96,1024]{2,1,0:T(8,128)(2,1)}), bf16[4,96,1024]{2,1,0:T(8,128)(2,1)}, u32[]{:S(2)}, u32[]{:S(2)}) async-start(bf16[4,96,1024]{2,1,0:T(8,128)(2,1)} %bitcast.12), calls=%async_computation.2 | async-start | bytes 1572864 | tf_op jit(solution)/shard_map/all_to_all | solution.py:195
  125.0 1.9 collective-permute-start.8
  126.9 3.4 %collective-permute-start.9 = (bf16[1024,384]{1,0:T(8,128)(2,1)S(1)}, bf16[1024,384]{1,0:T(8,128)(2,1)S(1)}, u32[]{:S(2)}, u32[]{:S(2)}) collective-permute-start(bf16[1024,384]{1,0:T(8,128)(2,1)S(1)} %bitcast.34), channel_id=1, source_target_pairs={{0,4},{4,8},{8,12},{12,0},{1,5},{5,9},{9,13},{13,1},{2,6},{6,10},{... | collective-permute-start | bytes 2359304 | tf_op jit(solution)/shard_map/ppermute | solution.py:21
  130.3 2.5 %collective-permute-start.10 = (bf16[1024,384]{1,0:T(8,128)(2,1)S(1)}, bf16[1024,384]{1,0:T(8,128)(2,1)S(1)}, u32[]{:S(2)}, u32[]{:S(2)}) collective-permute-start(bf16[1024,384]{1,0:T(8,128)(2,1)S(1)} %bitcast.35), channel_id=1, source_target_pairs={{0,8},{4,12},{8,0},{12,4},{1,9},{5,13},{9,1},{13,5},{2,10},{6,14},... | collective-permute-start | bytes 2359304 | tf_op jit(solution)/shard_map/ppermute | solution.py:21
  132.8 2.0 convert_reduce_fusion
  134.8 8.5 %all-to-all-done.2 = bf16[4,96,1024]{2,1,0:T(8,128)(2,1)} async-done(((bf16[4,96,1024]{2,1,0:T(8,128)(2,1)}), bf16[4,96,1024]{2,1,0:T(8,128)(2,1)}, u32[]{:S(2)}, u32[]{:S(2)}) %all-to-all-start.2) | async-done | bytes 786464 | tf_op jit(solution)/shard_map/all_to_all | solution.py:195
  144.8 14.6 %all_gather.3.hidden_ref = bf16[384,1024]{1,0:T(8,128)(2,1)S(1)} all-gather(bf16[96,1024]{1,0:T(8,128)(2,1)S(1)} %multiply_convert_fusion), channel_id=1, replica_groups=mesh['y'=8,'zl'=2,'core'=2,'x'=4,'zh'=4] {'zh'}, dimensions={0}, use_global_device_ids=true | all-gather | bytes 983040 | tf_op jit(solution)/shard_map/all_gather | solution.py:208
  160.4 2.3 %shard_map.67 = bf16[8,4,48,384]{3,2,1,0:T(8,128)(2,1)S(1)} custom-call(s32[4]{0:T(128)S(1)} %pad_add_fusion.order_ref, bf16[384,1024]{1,0:T(8,128)(2,1)S(1)} %all_gather.3.hidden_ref, bf16[1024,384]{1,0:T(8,128)(2,1)S(1)} %bitcast.36, bf16[1024,384]{1,0:T(8,128)(2,1)S(1)} %collective-permute-done.8.after_ref, ...), custom_call_target="tpu_custom_call" | custom-call | flops 1207959552 | bytes 5111808 | tf_op jit(solution)/shard_map/pallas_call | solution.py:139
  162.7 33.3 %all_to_all.38 = bf16[32,48,384]{2,1,0:T(8,128)(2,1)S(1)} all-to-all(bf16[32,48,384]{2,1,0:T(8,128)(2,1)S(1)} %bitcast.29), channel_id=1, replica_groups=mesh['y'=8,'zl'=2,'core'=2,'x'=4,'zh'=4] {'y','x'}, dimensions={0} | all-to-all | bytes 2359296 | tf_op jit(solution)/shard_map/all_to_all | solution.py:210
  196.8 11.3 %all-to-all-start.5 = ((bf16[4,48,384]{2,1,0:T(8,128)(2,1)}), bf16[4,48,384]{2,1,0:T(8,128)(2,1)S(1)}, u32[]{:S(2)}, u32[]{:S(2)}) async-start(bf16[4,48,384]{2,1,0:T(8,128)(2,1)} %reduce_sum.52), calls=%async_computation.5 | async-start | bytes 294912 | tf_op jit(solution)/shard_map/all_to_all | solution.py:218
  208.2 3.7 %all-to-all-done.5 = bf16[4,48,384]{2,1,0:T(8,128)(2,1)S(1)} async-done(((bf16[4,48,384]{2,1,0:T(8,128)(2,1)}), bf16[4,48,384]{2,1,0:T(8,128)(2,1)S(1)}, u32[]{:S(2)}, u32[]{:S(2)}) %all-to-all-start.5) | async-done | bytes 147488 | tf_op jit(solution)/shard_map/all_to_all | solution.py:218
  (48 shorter events, 14.9 us)
Async XLA Ops:
  0.0 1.1 copy-start
  2.2 21.1 %all-to-all-start = ((bf16[16,48,384]{2,1,0:T(8,128)(2,1)}), bf16[16,48,384]{2,1,0:T(8,128)(2,1)S(1)}, u32[]{:S(2)}, u32[]{:S(2)}) async-start(bf16[16,48,384]{2,1,0:T(8,128)(2,1)} %bitcast.5), calls=%async_computation | async-start | bytes 1179648 | tf_op jit(solution)/shard_map/all_to_all | solution.py:172
  24.5 55.6 %all-to-all-start.1 = ((bf16[8,4,48,384]{3,2,1,0:T(8,128)(2,1)}), bf16[8,4,48,384]{3,2,1,0:T(8,128)(2,1)S(1)}, u32[]{:S(2)}, u32[]{:S(2)}) async-start(bf16[8,4,48,384]{3,2,1,0:T(8,128)(2,1)} %broadcast_in_dim.19), calls=%async_computation.1 | async-start | bytes 2359296 | tf_op jit(solution)/shard_map/all_to_all | solution.py:183
  28.7 20.4 %collective-permute-start = (bf16[1024,384]{1,0:T(8,128)(2,1)}, bf16[1024,384]{1,0:T(8,128)(2,1)S(1)}, u32[]{:S(2)}, u32[]{:S(2)}) collective-permute-start(bf16[1024,384]{1,0:T(8,128)(2,1)} %bitcast.11.own_ref), channel_id=1, source_target_pairs={{0,12},{4,0},{8,4},{12,8},{1,13},{5,1},{9,5},{13,9},{2,14},{6,2},{... | collective-permute-start | bytes 2359304 | tf_op jit(solution)/shard_map/ppermute | solution.py:21
  31.3 21.9 %collective-permute-start.1 = (bf16[1024,384]{1,0:T(8,128)(2,1)}, bf16[1024,384]{1,0:T(8,128)(2,1)S(1)}, u32[]{:S(2)}, u32[]{:S(2)}) collective-permute-start(bf16[1024,384]{1,0:T(8,128)(2,1)} %bitcast.11.own_ref), channel_id=1, source_target_pairs={{0,4},{4,8},{8,12},{12,0},{1,5},{5,9},{9,13},{13,1},{2,6},{6,10},{... | collective-permute-start | bytes 2359304 | tf_op jit(solution)/shard_map/ppermute | solution.py:21
  53.1 19.8 %collective-permute-start.4 = (bf16[1024,384]{1,0:T(8,128)(2,1)}, bf16[1024,384]{1,0:T(8,128)(2,1)S(1)}, u32[]{:S(2)}, u32[]{:S(2)}) collective-permute-start(bf16[1024,384]{1,0:T(8,128)(2,1)} %bitcast.30), channel_id=1, source_target_pairs={{0,12},{4,0},{8,4},{12,8},{1,13},{5,1},{9,5},{13,9},{2,14},{6,2},{... | collective-permute-start | bytes 2359304 | tf_op jit(solution)/shard_map/ppermute | solution.py:21
  55.0 22.1 %collective-permute-start.5 = (bf16[1024,384]{1,0:T(8,128)(2,1)}, bf16[1024,384]{1,0:T(8,128)(2,1)S(1)}, u32[]{:S(2)}, u32[]{:S(2)}) collective-permute-start(bf16[1024,384]{1,0:T(8,128)(2,1)} %bitcast.31), channel_id=1, source_target_pairs={{0,4},{4,8},{8,12},{12,0},{1,5},{5,9},{9,13},{13,1},{2,6},{6,10},{... | collective-permute-start | bytes 2359304 | tf_op jit(solution)/shard_map/ppermute | solution.py:21
  72.9 5.2 %copy-start.1 = (bf16[1024,384]{1,0:T(8,128)(2,1)}, bf16[1024,384]{1,0:T(8,128)(2,1)S(1)}, u32[]{:S(2)}) copy-start(bf16[1024,384]{1,0:T(8,128)(2,1)S(1)} %collective-permute-done.4.refs_1_) | copy-start | bytes 2359300
  73.8 11.2 %collective-permute-start.6 = (bf16[512,384]{1,0:T(8,128)(2,1)}, bf16[512,384]{1,0:T(8,128)(2,1)S(1)}, u32[]{:S(2)}, u32[]{:S(2)}) collective-permute-start(bf16[512,384]{1,0:T(8,128)(2,1)} %slice.18), channel_id=1, source_target_pairs={{0,12},{4,0},{8,4},{12,8},{1,13},{5,1},{9,5},{13,9},{2,14},{6,2},{... | collective-permute-start | bytes 1179656 | tf_op jit(solution)/shard_map/ppermute | solution.py:21
  77.2 1.0 copy-start.3
  78.2 11.8 %collective-permute-start.7 = (bf16[512,384]{1,0:T(8,128)(2,1)}, bf16[512,384]{1,0:T(8,128)(2,1)}, u32[]{:S(2)}, u32[]{:S(2)}) collective-permute-start(bf16[512,384]{1,0:T(8,128)(2,1)} %slice.19), channel_id=1, source_target_pairs={{0,4},{4,8},{8,12},{12,0},{1,5},{5,9},{9,13},{13,1},{2,6},{6,10},{... | collective-permute-start | bytes 1179656 | tf_op jit(solution)/shard_map/ppermute | solution.py:21
  80.1 1.1 copy-start.2
  81.3 1.1 copy-start.4
  82.4 1.1 copy-start.5
  92.5 27.0 %all-to-all-start.3 = ((bf16[4,96,1024]{2,1,0:T(8,128)(2,1)}), bf16[4,96,1024]{2,1,0:T(8,128)(2,1)}, u32[]{:S(2)}, u32[]{:S(2)}) async-start(bf16[4,96,1024]{2,1,0:T(8,128)(2,1)} %bitcast.15), calls=%async_computation.3 | async-start | bytes 1572864 | tf_op jit(solution)/shard_map/all_to_all | solution.py:195
  101.7 9.3 %collective-permute-start.2 = (bf16[512,384]{1,0:T(8,128)(2,1)S(1)}, bf16[512,384]{1,0:T(8,128)(2,1)S(1)}, u32[]{:S(2)}, u32[]{:S(2)}) collective-permute-start(bf16[512,384]{1,0:T(8,128)(2,1)S(1)} %slice.16), channel_id=1, source_target_pairs={{0,12},{4,0},{8,4},{12,8},{1,13},{5,1},{9,5},{13,9},{2,14},{6,2},{... | collective-permute-start | bytes 1179656 | tf_op jit(solution)/shard_map/ppermute | solution.py:21
  103.6 10.5 %collective-permute-start.3 = (bf16[512,384]{1,0:T(8,128)(2,1)S(1)}, bf16[512,384]{1,0:T(8,128)(2,1)S(1)}, u32[]{:S(2)}, u32[]{:S(2)}) collective-permute-start(bf16[512,384]{1,0:T(8,128)(2,1)S(1)} %slice.17), channel_id=1, source_target_pairs={{0,4},{4,8},{8,12},{12,0},{1,5},{5,9},{9,13},{13,1},{2,6},{6,10},{... | collective-permute-start | bytes 1179656 | tf_op jit(solution)/shard_map/ppermute | solution.py:21
  110.9 3.2 %copy-start.8 = (bf16[512,384]{1,0:T(8,128)(2,1)}, bf16[512,384]{1,0:T(8,128)(2,1)S(1)}, u32[]{:S(2)}) copy-start(bf16[512,384]{1,0:T(8,128)(2,1)S(1)} %collective-permute-done.2.low_ref) | copy-start | bytes 1179652
  114.1 0.8 copy-start.9
  118.4 6.6 %copy-start.6 = (bf16[1,1024,384]{2,1,0:T(8,128)(2,1)S(1)}, bf16[1,1024,384]{2,1,0:T(8,128)(2,1)}, u32[]{:S(2)}) copy-start(bf16[1,1024,384]{2,1,0:T(8,128)(2,1)} %param.11) | copy-start | bytes 2359300
  119.5 23.8 %all-to-all-start.2 = ((bf16[4,96,1024]{2,1,0:T(8,128)(2,1)}), bf16[4,96,1024]{2,1,0:T(8,128)(2,1)}, u32[]{:S(2)}, u32[]{:S(2)}) async-start(bf16[4,96,1024]{2,1,0:T(8,128)(2,1)} %bitcast.12), calls=%async_computation.2 | async-start | bytes 1572864 | tf_op jit(solution)/shard_map/all_to_all | solution.py:195
  125.0 34.5 %collective-permute-start.8 = (bf16[1024,384]{1,0:T(8,128)(2,1)S(1)}, bf16[1024,384]{1,0:T(8,128)(2,1)S(1)}, u32[]{:S(2)}, u32[]{:S(2)}) collective-permute-start(bf16[1024,384]{1,0:T(8,128)(2,1)S(1)} %bitcast.33), channel_id=1, source_target_pairs={{0,12},{4,0},{8,4},{12,8},{1,13},{5,1},{9,5},{13,9},{2,14},{6,2},{... | collective-permute-start | bytes 2359304 | tf_op jit(solution)/shard_map/ppermute | solution.py:21
  126.9 32.6 %collective-permute-start.9 = (bf16[1024,384]{1,0:T(8,128)(2,1)S(1)}, bf16[1024,384]{1,0:T(8,128)(2,1)S(1)}, u32[]{:S(2)}, u32[]{:S(2)}) collective-permute-start(bf16[1024,384]{1,0:T(8,128)(2,1)S(1)} %bitcast.34), channel_id=1, source_target_pairs={{0,4},{4,8},{8,12},{12,0},{1,5},{5,9},{9,13},{13,1},{2,6},{6,10},{... | collective-permute-start | bytes 2359304 | tf_op jit(solution)/shard_map/ppermute | solution.py:21
  130.3 30.1 %collective-permute-start.10 = (bf16[1024,384]{1,0:T(8,128)(2,1)S(1)}, bf16[1024,384]{1,0:T(8,128)(2,1)S(1)}, u32[]{:S(2)}, u32[]{:S(2)}) collective-permute-start(bf16[1024,384]{1,0:T(8,128)(2,1)S(1)} %bitcast.35), channel_id=1, source_target_pairs={{0,8},{4,12},{8,0},{12,4},{1,9},{5,13},{9,1},{13,5},{2,10},{6,14},... | collective-permute-start | bytes 2359304 | tf_op jit(solution)/shard_map/ppermute | solution.py:21
  143.4 1.4 copy-start.7
  196.8 15.0 %all-to-all-start.5 = ((bf16[4,48,384]{2,1,0:T(8,128)(2,1)}), bf16[4,48,384]{2,1,0:T(8,128)(2,1)S(1)}, u32[]{:S(2)}, u32[]{:S(2)}) async-start(bf16[4,48,384]{2,1,0:T(8,128)(2,1)} %reduce_sum.52), calls=%async_computation.5 | async-start | bytes 294912 | tf_op jit(solution)/shard_map/all_to_all | solution.py:218

commit v9 on v8

--- a/solution.py
+++ b/solution.py
@@ -21,14 +21,21 @@
     return lax.ppermute(array, axis, [(i, (i + step) % size) for i in range(size)])
 
 
+def turn(array, back):
+    size = lax.axis_size("x")
+    pairs = []
+    for core in range(2):
+        step = 1 if (core == 0) == back else -1
+        pairs += [(core * size + i, core * size + (i + step) % size) for i in range(size)]
+    return lax.ppermute(array, ("core", "x"), pairs)
+
+
 def beside(weight):
-    return shift(weight, "x", -1), shift(weight, "x", 1)
+    return turn(weight, False), turn(weight, True)
 
 
 def across(pair):
-    after, before = pair
-    half = after.shape[0] // 2
-    return shift(after[:half], "x", -1), shift(before[half:], "x", 1)
+    return (turn(pair[0], False),)
 
 
 def block_term(rows_ref, step, block):
@@ -49,14 +56,8 @@
     for start in range(0, width, TILE):
         tile = pl.ds(start, TILE)
         total = None if opened is None else opened[:, tile]
-        pieces = list(block_refs)
-        for step in steps:
-            block = pieces.pop(0)
-            if block.shape[0] == width:
-                block = block[tile, :]
-            else:
-                other, part = pieces.pop(0), block.shape[0]
-                block = (block if start < part else other)[pl.ds(start % part, TILE), :]
+        for step, block in zip(steps, block_refs):
+            block = block[tile, :]
             term = block_term(rows_ref, step, block)
             total = term if total is None else total + term
         out_ref[:, tile] = total.astype(out_ref.dtype)
@@ -80,12 +81,10 @@
     )(rows, *operands)
 
 
-def gate_kernel(rows_ref, after_ref, before_ref, own_ref, low_ref, high_ref, out_ref, own, opposite, sems):
-    half = low_ref.shape[0]
+def gate_kernel(rows_ref, after_ref, before_ref, own_ref, across_ref, out_ref, own, opposite, sems):
     copies = (
         pltpu.make_async_copy(own_ref, own, sems.at[0]),
-        pltpu.make_async_copy(low_ref, opposite.at[pl.ds(0, half), :], sems.at[1]),
-        pltpu.make_async_copy(high_ref, opposite.at[pl.ds(half, half), :], sems.at[2]),
+        pltpu.make_async_copy(across_ref, opposite, sems.at[1]),
     )
     for copy in copies:
         copy.start()
@@ -93,12 +92,11 @@
     copies[0].wait()
     total += block_term(rows_ref, 0, own[...])
     copies[1].wait()
-    copies[2].wait()
     total += block_term(rows_ref, 2, opposite[...])
     out_ref[...] = total.astype(out_ref.dtype)
 
 
-def project_gate(rows, own, pair, halves):
+def project_gate(rows, own, pair, opposite):
     sources, blocks, cap, depth = rows.shape
     width = own.shape[0]
     vmem = pl.BlockSpec(memory_space=pltpu.VMEM)
@@ -106,12 +104,12 @@
     return pl.pallas_call(
         gate_kernel,
         out_shape=jax.ShapeDtypeStruct((sources * cap, width), jnp.bfloat16),
-        in_specs=[vmem] * 3 + [anywhere] * 3,
+        in_specs=[vmem] * 3 + [anywhere] * 2,
         out_specs=vmem,
         scratch_shapes=[
             pltpu.VMEM((width, depth), jnp.bfloat16),
             pltpu.VMEM((width, depth), jnp.bfloat16),
-            pltpu.SemaphoreType.DMA((3,)),
+            pltpu.SemaphoreType.DMA((2,)),
         ],
         compiler_params=pltpu.CompilerParams(vmem_limit_bytes=GRANT),
         cost_estimate=pl.CostEstimate(
@@ -119,7 +117,7 @@
             bytes_accessed=2 * (rows.size + blocks * own.size + sources * cap * width),
             transcendentals=0,
         ),
-    )(rows, *pair, own, *[pltpu.with_memory_space_constraint(half, pltpu.HBM) for half in halves])
+    )(rows, *pair, own, pltpu.with_memory_space_constraint(opposite[0], pltpu.HBM))
 
 
 def expand_kernel(order_ref, hidden_ref, own_ref, after_ref, before_ref, across_ref, out_ref):
@@ -176,7 +174,8 @@
         concat_axis=0,
         tiled=True,
     ).reshape(EXPERTS, x_size, CAP, width_part)
-    order = [(x_own + step) % x_size for step in range(x_size)]
+    sign = 1 - 2 * lax.axis_index("core")
+    order = [(x_own + x_size + sign * step) % x_size for step in range(x_size)]
     mine = lax.dynamic_index_in_dim(local, x_own, 0, keepdims=False)
     mine = jnp.stack([lax.dynamic_index_in_dim(mine, place, 0, keepdims=False) for place in order])
     sent_y = jnp.broadcast_to(mine[None], (y_size, x_size, CAP, width_part))
@@ -186,7 +185,7 @@
     gate_own = w_gate[0]
     width = gate_own.shape[0]
     gate_pair = beside(gate_own)
-    gate_halves = across(gate_pair)
+    gate_across = across(gate_pair)
     up_own, _ = lax.optimization_barrier((w_up[0], gate_pair))
     up_pair = beside(up_own)
     up_across = across(up_pair)
@@ -196,7 +195,7 @@
         parts = parts.reshape(zh_size, total_rows // zh_size, -1)
         return jnp.sum(parts.astype(jnp.float32), axis=0)
 
-    gate_term = project_gate(rows, gate_own, gate_pair, gate_halves)
+    gate_term = project_gate(rows, gate_own, gate_pair, gate_across)
     gate_share = share(gate_term)
     up_open = project((0, 1, 3), rows, width, jnp.float32, up_own, *up_pair)
     up_term = project((2,), rows, width, jnp.bfloat16, up_open, *up_across)

time: 214 us -> 199 us (0.930)
  waiting for transfers between devices: 71 us -> 51.4 us
  blocking collectives: 47.9 us -> 57.5 us
  starting transfers between devices: 69.1 us -> 65.1 us
  local copies, waits for them, and re-layouts: 8.35 us -> 5.14 us
  Pallas kernels: 9.7 us -> 12.1 us
    ppermute x11 -> x1, waiting for transfers between devices: 46.7 us -> 0.01 us  [shift(): lax.ppermute(array, axis, [(i, (i + step) % size) for i in range(size)])]
    ppermute x0 -> x8, waiting for transfers between devices: none -> 41.4 us  [turn(): return lax.ppermute(array, ('core', 'x'), pairs)]
    ppermute x11 -> x1, starting transfers between devices: 28.9 us -> 1.92 us  [shift(): lax.ppermute(array, axis, [(i, (i + step) % size) for i in range(size)])]
    ppermute x0 -> x8, starting transfers between devices: none -> 23.3 us  [turn(): return lax.ppermute(array, ('core', 'x'), pairs)]
    all_to_all x1, blocking collectives: 33.3 us -> 42.4 us  [on_device(): lax.all_to_all(back.reshape(y_size * x_size, CAP, width_part), ('y', 'x')...]
    all_to_all x2, waiting for transfers between devices: 9.67 us -> 1.91 us  [share(): parts = lax.all_to_all(term, 'zh', split_axis=0, concat_axis=0, tiled=True)]
    all_to_all x1, waiting for transfers between devices: 10.9 us -> 4.32 us  [on_device(): lax.all_to_all(sent.reshape(EXPERTS * x_size, CAP, width_part), LOCAL + (...]
    unnamed x20 -> x18, local copies, waits for them, and re-layouts: 4.34 us -> 2.93 us
  transfers between devices with their start and end apart: 16 -> 14, of which waited for: 11 -> 8; matrix products, arithmetic and copies ran while one was open for 3% -> 2% of each run, Pallas kernels for 2% -> 4%
where the time goes in v9:
time: 199 us; the launch traced here: 198 us
  starting transfers between devices  65.1 us (33%)
  blocking collectives  57.5 us (29%)
  waiting for transfers between devices  51.4 us (26%)
  Pallas kernels  12.1 us (6%)
  other arithmetic  5.38 us (3%)
  local copies, waits for them, and re-layouts  5.14 us (3%)
    all_to_all x1, blocking collectives, on_device(): lax.all_to_all(back.reshape(y_size * x_size, CAP, width_part), ('y', 'x')...  42.4 us
    ppermute x8, waiting for transfers between devices, turn(): return lax.ppermute(array, ('core', 'x'), pairs)  41.4 us
    ppermute x8, starting transfers between devices, turn(): return lax.ppermute(array, ('core', 'x'), pairs)  23.3 us
    all_gather x1, blocking collectives, on_device(): hidden_rows = lax.all_gather(hidden, 'zh', axis=0, tiled=True)  15 us
    all_to_all x2, starting transfers between devices, share(): parts = lax.all_to_all(term, 'zh', split_axis=0, concat_axis=0, tiled=True)  13.3 us
    all_to_all x1, starting transfers between devices, on_device(): lax.all_to_all(back, LOCAL, split_axis=0, concat_axis=0, tiled=True)  12.2 us
    all_to_all x1, starting transfers between devices, on_device(): lax.all_to_all(sent.reshape(EXPERTS * x_size, CAP, width_part), LOCAL + (...  10.2 us
    pallas_call x2, Pallas kernels, project(): pl.pallas_call(functools.partial(project_kernel, steps), out_shape=jax.Sh...  5.17 us
  transfers between devices with their start and end apart: 14, of which 8 were waited for; matrix products, arithmetic and copies ran while one was open for 2% of the time, Pallas kernels for 4%

profile of v9, /device:TPU:1, one launch (start us, length us, event | category | flops | bytes accessed | tf_op | source)
XLA Modules:
  0.0 198.0 jit_solution(12957005526785607647)
XLA Ops:
  2.2 10.2 %all-to-all-start = ((bf16[16,48,384]{2,1,0:T(8,128)(2,1)}), bf16[16,48,384]{2,1,0:T(8,128)(2,1)S(1)}, u32[]{:S(2)}, u32[]{:S(2)}) async-start(bf16[16,48,384]{2,1,0:T(8,128)(2,1)} %bitcast.5), calls=%async_computation | async-start | bytes 1179648 | tf_op jit(solution)/shard_map/all_to_all | solution.py:170
  12.4 3.3 %collective-permute-start = (bf16[1024,384]{1,0:T(8,128)(2,1)S(1)}, bf16[1024,384]{1,0:T(8,128)(2,1)}, u32[]{:S(2)}, u32[]{:S(2)}) collective-permute-start(bf16[1024,384]{1,0:T(8,128)(2,1)S(1)} %bitcast.33), channel_id=1, source_target_pairs={{0,12},{4,0},{8,4},{12,8},{16,20},{20,24},{24,28},{28,16},{1,13},{... | collective-permute-start | bytes 2359304 | tf_op jit(solution)/shard_map/ppermute | solution.py:30
  15.7 3.2 %collective-permute-start.1 = (bf16[1024,384]{1,0:T(8,128)(2,1)S(1)}, bf16[1024,384]{1,0:T(8,128)(2,1)}, u32[]{:S(2)}, u32[]{:S(2)}) collective-permute-start(bf16[1024,384]{1,0:T(8,128)(2,1)S(1)} %bitcast.34), channel_id=1, source_target_pairs={{0,4},{4,8},{8,12},{12,0},{16,28},{20,16},{24,20},{28,24},{1,5},{5... | collective-permute-start | bytes 2359304 | tf_op jit(solution)/shard_map/ppermute | solution.py:30
  19.0 4.3 %all-to-all-done = bf16[16,48,384]{2,1,0:T(8,128)(2,1)S(1)} async-done(((bf16[16,48,384]{2,1,0:T(8,128)(2,1)}), bf16[16,48,384]{2,1,0:T(8,128)(2,1)S(1)}, u32[]{:S(2)}, u32[]{:S(2)}) %all-to-all-start) | async-done | bytes 589856 | tf_op jit(solution)/shard_map/all_to_all | solution.py:170
  23.4 1.1 broadcast_in_dim.19
  24.6 4.3 %all-to-all-start.1 = ((bf16[8,4,48,384]{3,2,1,0:T(8,128)(2,1)}), bf16[8,4,48,384]{3,2,1,0:T(8,128)(2,1)S(1)}, u32[]{:S(2)}, u32[]{:S(2)}) async-start(bf16[8,4,48,384]{3,2,1,0:T(8,128)(2,1)} %broadcast_in_dim.19), calls=%async_computation.1 | async-start | bytes 2359296 | tf_op jit(solution)/shard_map/all_to_all | solution.py:182
  28.8 9.9 %collective-permute-done.after_ref = bf16[1024,384]{1,0:T(8,128)(2,1)} collective-permute-done((bf16[1024,384]{1,0:T(8,128)(2,1)S(1)}, bf16[1024,384]{1,0:T(8,128)(2,1)}, u32[]{:S(2)}, u32[]{:S(2)}) %collective-permute-start) | collective-permute-done | bytes 786464 | tf_op jit(solution)/shard_map/ppermute | solution.py:30
  38.7 2.8 %collective-permute-start.3 = (bf16[1024,384]{1,0:T(8,128)(2,1)S(1)}, bf16[1024,384]{1,0:T(8,128)(2,1)}, u32[]{:S(2)}, u32[]{:S(2)}) collective-permute-start(bf16[1024,384]{1,0:T(8,128)(2,1)S(1)} %bitcast.30), channel_id=1, source_target_pairs={{0,12},{4,0},{8,4},{12,8},{16,20},{20,24},{24,28},{28,16},{1,13},{... | collective-permute-start | bytes 2359304 | tf_op jit(solution)/shard_map/ppermute | solution.py:30
  41.5 3.7 %collective-permute-start.4 = (bf16[1024,384]{1,0:T(8,128)(2,1)S(1)}, bf16[1024,384]{1,0:T(8,128)(2,1)S(1)}, u32[]{:S(2)}, u32[]{:S(2)}) collective-permute-start(bf16[1024,384]{1,0:T(8,128)(2,1)S(1)} %bitcast.31), channel_id=1, source_target_pairs={{0,4},{4,8},{8,12},{12,0},{16,28},{20,16},{24,20},{28,24},{1,5},{5... | collective-permute-start | bytes 2359304 | tf_op jit(solution)/shard_map/ppermute | solution.py:30
  45.2 11.3 %collective-permute-done.3.refs_1_ = bf16[1024,384]{1,0:T(8,128)(2,1)} collective-permute-done((bf16[1024,384]{1,0:T(8,128)(2,1)S(1)}, bf16[1024,384]{1,0:T(8,128)(2,1)}, u32[]{:S(2)}, u32[]{:S(2)}) %collective-permute-start.3) | collective-permute-done | bytes 786464 | tf_op jit(solution)/shard_map/ppermute | solution.py:30
  56.5 1.9 collective-permute-start.5
  58.4 3.3 %collective-permute-done.4.refs_2_ = bf16[1024,384]{1,0:T(8,128)(2,1)S(1)} collective-permute-done((bf16[1024,384]{1,0:T(8,128)(2,1)S(1)}, bf16[1024,384]{1,0:T(8,128)(2,1)S(1)}, u32[]{:S(2)}, u32[]{:S(2)}) %collective-permute-start.4) | collective-permute-done | bytes 786464 | tf_op jit(solution)/shard_map/ppermute | solution.py:30
  62.7 1.1 copy-done.4
  63.8 2.5 %shard_map.65.refs_0_ = f32[384,1024]{1,0:T(8,128)S(1)} custom-call(bf16[8,4,48,384]{3,2,1,0:T(8,128)(2,1)S(1)} %all-to-all-done.1.rows_ref, bf16[1024,384]{1,0:T(8,128)(2,1)S(1)} %bitcast.32, bf16[1024,384]{1,0:T(8,128)(2,1)} %collective-permute-done.3.refs_1_, bf16[1024,384]{1,0:T(8,128)(2,1)S(1)} %copy-done.4), custom_call_target="tpu_custom_call" | custom-call | flops 905969664 | bytes 4325376 | tf_op jit(solution)/shard_map/pallas_call | solution.py:70
  66.3 4.4 %collective-permute-done.5.refs_1_ = bf16[1024,384]{1,0:T(8,128)(2,1)} collective-permute-done((bf16[1024,384]{1,0:T(8,128)(2,1)}, bf16[1024,384]{1,0:T(8,128)(2,1)}, u32[]{:S(2)}, u32[]{:S(2)}) %collective-permute-start.5) | collective-permute-done | bytes 786464 | tf_op jit(solution)/shard_map/ppermute | solution.py:30
  70.7 2.6 %shard_map.66 = bf16[384,1024]{1,0:T(8,128)(2,1)} custom-call(bf16[8,4,48,384]{3,2,1,0:T(8,128)(2,1)S(1)} %all-to-all-done.1.rows_ref, f32[384,1024]{1,0:T(8,128)S(1)} %shard_map.65.refs_0_, bf16[1024,384]{1,0:T(8,128)(2,1)} %collective-permute-done.5.refs_1_), custom_call_target="tpu_custom_call" | custom-call | flops 603979776 | bytes 3538944 | tf_op jit(solution)/shard_map/pallas_call | solution.py:70
  73.4 6.5 %all-to-all-start.3 = ((bf16[4,96,1024]{2,1,0:T(8,128)(2,1)}), bf16[4,96,1024]{2,1,0:T(8,128)(2,1)S(1)}, u32[]{:S(2)}, u32[]{:S(2)}) async-start(bf16[4,96,1024]{2,1,0:T(8,128)(2,1)} %bitcast.15), calls=%async_computation.3 | async-start | bytes 1572864 | tf_op jit(solution)/shard_map/all_to_all | solution.py:194
  79.8 1.9 collective-permute-start.2
  81.8 12.5 %collective-permute-done.2.across_ref = bf16[1024,384]{1,0:T(8,128)(2,1)S(1)} collective-permute-done((bf16[1024,384]{1,0:T(8,128)(2,1)}, bf16[1024,384]{1,0:T(8,128)(2,1)S(1)}, u32[]{:S(2)}, u32[]{:S(2)}) %collective-permute-start.2) | collective-permute-done | bytes 786464 | tf_op jit(solution)/shard_map/ppermute | solution.py:30
  95.2 4.5 %shard_map.64 = bf16[384,1024]{1,0:T(8,128)(2,1)} custom-call(bf16[8,4,48,384]{3,2,1,0:T(8,128)(2,1)S(1)} %all-to-all-done.1.rows_ref, bf16[1024,384]{1,0:T(8,128)(2,1)} %collective-permute-done.after_ref, bf16[1024,384]{1,0:T(8,128)(2,1)} %collective-permute-done.1.before_ref, bf16[1024,384]{1,0:T(8,128)(2,1)S(1)} %bitcast.35, bf16[1024,384]{1,0:T(8,128)(2,1)} %copy-done.8), custom_call_target="tpu_custom_call" | custom-call | flops 1207959552 | bytes 5111808 | tf_op jit(solution)/shard_map/pallas_call | solution.py:104
  99.8 6.8 %all-to-all-start.2 = ((bf16[4,96,1024]{2,1,0:T(8,128)(2,1)}), bf16[4,96,1024]{2,1,0:T(8,128)(2,1)}, u32[]{:S(2)}, u32[]{:S(2)}) async-start(bf16[4,96,1024]{2,1,0:T(8,128)(2,1)} %bitcast.12), calls=%async_computation.2 | async-start | bytes 1572864 | tf_op jit(solution)/shard_map/all_to_all | solution.py:194
  106.6 1.9 collective-permute-start.6
  108.5 4.6 %collective-permute-start.7 = (bf16[1024,384]{1,0:T(8,128)(2,1)S(1)}, bf16[1024,384]{1,0:T(8,128)(2,1)S(1)}, u32[]{:S(2)}, u32[]{:S(2)}) collective-permute-start(bf16[1024,384]{1,0:T(8,128)(2,1)S(1)} %bitcast.37), channel_id=1, source_target_pairs={{0,4},{4,8},{8,12},{12,0},{16,28},{20,16},{24,20},{28,24},{1,5},{5... | collective-permute-start | bytes 2359304 | tf_op jit(solution)/shard_map/ppermute | solution.py:30
  113.1 1.9 collective-permute-start.8
  115.0 2.0 %convert_reduce_fusion = f32[96,1024]{1,0:T(8,128)} fusion(bf16[4,96,1024]{2,1,0:T(8,128)(2,1)} %copy-done.6), kind=kLoop, calls=%fused_computation | loop fusion | flops 688128 | bytes 1179648 | tf_op jit(solution)/shard_map/reduce_sum | solution.py:196
  117.1 1.9 all-to-all-done.2
  119.0 1.3 convert_reduce_fusion.1
  120.5 15.0 %all_gather.3.hidden_ref = bf16[384,1024]{1,0:T(8,128)(2,1)S(1)} all-gather(bf16[96,1024]{1,0:T(8,128)(2,1)S(1)} %multiply_convert_fusion), channel_id=1, replica_groups=mesh['y'=8,'zl'=2,'core'=2,'x'=4,'zh'=4] {'zh'}, dimensions={0}, use_global_device_ids=true | all-gather | bytes 983040 | tf_op jit(solution)/shard_map/all_gather | solution.py:207
  135.5 2.3 %shard_map.67 = bf16[8,4,48,384]{3,2,1,0:T(8,128)(2,1)S(1)} custom-call(s32[4]{0:T(128)S(1)} %pad_add_fusion.order_ref, bf16[384,1024]{1,0:T(8,128)(2,1)S(1)} %all_gather.3.hidden_ref, bf16[1024,384]{1,0:T(8,128)(2,1)S(1)} %bitcast.39, bf16[1024,384]{1,0:T(8,128)(2,1)S(1)} %collective-permute-done.6.after_ref, ...), custom_call_target="tpu_custom_call" | custom-call | flops 1207959552 | bytes 5111808 | tf_op jit(solution)/shard_map/pallas_call | solution.py:137
  137.9 42.4 %all_to_all.38 = bf16[32,48,384]{2,1,0:T(8,128)(2,1)S(1)} all-to-all(bf16[32,48,384]{2,1,0:T(8,128)(2,1)S(1)} %bitcast.29), channel_id=1, replica_groups=mesh['y'=8,'zl'=2,'core'=2,'x'=4,'zh'=4] {'y','x'}, dimensions={0} | all-to-all | bytes 2359296 | tf_op jit(solution)/shard_map/all_to_all | solution.py:209
  181.1 12.2 %all-to-all-start.5 = ((bf16[4,48,384]{2,1,0:T(8,128)(2,1)}), bf16[4,48,384]{2,1,0:T(8,128)(2,1)S(1)}, u32[]{:S(2)}, u32[]{:S(2)}) async-start(bf16[4,48,384]{2,1,0:T(8,128)(2,1)} %reduce_sum.52), calls=%async_computation.5 | async-start | bytes 294912 | tf_op jit(solution)/shard_map/all_to_all | solution.py:217
  193.3 3.7 %all-to-all-done.5 = bf16[4,48,384]{2,1,0:T(8,128)(2,1)S(1)} async-done(((bf16[4,48,384]{2,1,0:T(8,128)(2,1)}), bf16[4,48,384]{2,1,0:T(8,128)(2,1)S(1)}, u32[]{:S(2)}, u32[]{:S(2)}) %all-to-all-start.5) | async-done | bytes 147488 | tf_op jit(solution)/shard_map/all_to_all | solution.py:217
  (38 shorter events, 6.1 us)
Async XLA Ops:
  0.0 1.1 copy-start
  1.0 11.4 %copy-start.2 = (bf16[1,1024,384]{2,1,0:T(8,128)(2,1)S(1)}, bf16[1,1024,384]{2,1,0:T(8,128)(2,1)}, u32[]{:S(2)}) copy-start(bf16[1,1024,384]{2,1,0:T(8,128)(2,1)} %param.9) | copy-start | bytes 2359300
  2.2 21.1 %all-to-all-start = ((bf16[16,48,384]{2,1,0:T(8,128)(2,1)}), bf16[16,48,384]{2,1,0:T(8,128)(2,1)S(1)}, u32[]{:S(2)}, u32[]{:S(2)}) async-start(bf16[16,48,384]{2,1,0:T(8,128)(2,1)} %bitcast.5), calls=%async_computation | async-start | bytes 1179648 | tf_op jit(solution)/shard_map/all_to_all | solution.py:170
  12.4 26.2 %collective-permute-start = (bf16[1024,384]{1,0:T(8,128)(2,1)S(1)}, bf16[1024,384]{1,0:T(8,128)(2,1)}, u32[]{:S(2)}, u32[]{:S(2)}) collective-permute-start(bf16[1024,384]{1,0:T(8,128)(2,1)S(1)} %bitcast.33), channel_id=1, source_target_pairs={{0,12},{4,0},{8,4},{12,8},{16,20},{20,24},{24,28},{28,16},{1,13},{... | collective-permute-start | bytes 2359304 | tf_op jit(solution)/shard_map/ppermute | solution.py:30
  15.7 23.0 %collective-permute-start.1 = (bf16[1024,384]{1,0:T(8,128)(2,1)S(1)}, bf16[1024,384]{1,0:T(8,128)(2,1)}, u32[]{:S(2)}, u32[]{:S(2)}) collective-permute-start(bf16[1024,384]{1,0:T(8,128)(2,1)S(1)} %bitcast.34), channel_id=1, source_target_pairs={{0,4},{4,8},{8,12},{12,0},{16,28},{20,16},{24,20},{28,24},{1,5},{5... | collective-permute-start | bytes 2359304 | tf_op jit(solution)/shard_map/ppermute | solution.py:30
  24.6 14.1 %copy-start.1 = (bf16[1,1024,384]{2,1,0:T(8,128)(2,1)S(1)}, bf16[1,1024,384]{2,1,0:T(8,128)(2,1)}, u32[]{:S(2)}) copy-start(bf16[1,1024,384]{2,1,0:T(8,128)(2,1)} %param.10) | copy-start | bytes 2359300
  24.6 38.1 %all-to-all-start.1 = ((bf16[8,4,48,384]{3,2,1,0:T(8,128)(2,1)}), bf16[8,4,48,384]{3,2,1,0:T(8,128)(2,1)S(1)}, u32[]{:S(2)}, u32[]{:S(2)}) async-start(bf16[8,4,48,384]{3,2,1,0:T(8,128)(2,1)} %broadcast_in_dim.19), calls=%async_computation.1 | async-start | bytes 2359296 | tf_op jit(solution)/shard_map/all_to_all | solution.py:182
  38.7 17.8 %collective-permute-start.3 = (bf16[1024,384]{1,0:T(8,128)(2,1)S(1)}, bf16[1024,384]{1,0:T(8,128)(2,1)}, u32[]{:S(2)}, u32[]{:S(2)}) collective-permute-start(bf16[1024,384]{1,0:T(8,128)(2,1)S(1)} %bitcast.30), channel_id=1, source_target_pairs={{0,12},{4,0},{8,4},{12,8},{16,20},{20,24},{24,28},{28,16},{1,13},{... | collective-permute-start | bytes 2359304 | tf_op jit(solution)/shard_map/ppermute | solution.py:30
  41.5 20.2 %collective-permute-start.4 = (bf16[1024,384]{1,0:T(8,128)(2,1)S(1)}, bf16[1024,384]{1,0:T(8,128)(2,1)S(1)}, u32[]{:S(2)}, u32[]{:S(2)}) collective-permute-start(bf16[1024,384]{1,0:T(8,128)(2,1)S(1)} %bitcast.31), channel_id=1, source_target_pairs={{0,4},{4,8},{8,12},{12,0},{16,28},{20,16},{24,20},{28,24},{1,5},{5... | collective-permute-start | bytes 2359304 | tf_op jit(solution)/shard_map/ppermute | solution.py:30
  56.5 14.2 %collective-permute-start.5 = (bf16[1024,384]{1,0:T(8,128)(2,1)}, bf16[1024,384]{1,0:T(8,128)(2,1)}, u32[]{:S(2)}, u32[]{:S(2)}) collective-permute-start(bf16[1024,384]{1,0:T(8,128)(2,1)} %collective-permute-done.3.refs_1_), channel_id=1, source_target_pairs={{0,12},{4,0},{8,4},{12,8},{16,20},{20,24},{24,28},{28,16},{1,13},{... | collective-permute-start | bytes 2359304 | tf_op jit(solution)/shard_map/ppermute | solution.py:30
  61.8 0.9 copy-start.3
  62.7 1.1 copy-start.4
  73.4 26.4 %all-to-all-start.3 = ((bf16[4,96,1024]{2,1,0:T(8,128)(2,1)}), bf16[4,96,1024]{2,1,0:T(8,128)(2,1)S(1)}, u32[]{:S(2)}, u32[]{:S(2)}) async-start(bf16[4,96,1024]{2,1,0:T(8,128)(2,1)} %bitcast.15), calls=%async_computation.3 | async-start | bytes 1572864 | tf_op jit(solution)/shard_map/all_to_all | solution.py:194
  79.8 14.4 %collective-permute-start.2 = (bf16[1024,384]{1,0:T(8,128)(2,1)}, bf16[1024,384]{1,0:T(8,128)(2,1)S(1)}, u32[]{:S(2)}, u32[]{:S(2)}) collective-permute-start(bf16[1024,384]{1,0:T(8,128)(2,1)} %collective-permute-done.after_ref), channel_id=1, source_target_pairs={{0,12},{4,0},{8,4},{12,8},{16,20},{20,24},{24,28},{28,16},{1,13},{... | collective-permute-start | bytes 2359304 | tf_op jit(solution)/shard_map/ppermute | solution.py:30
  94.3 0.9 copy-start.8
  99.7 6.9 %copy-start.5 = (bf16[1,1024,384]{2,1,0:T(8,128)(2,1)S(1)}, bf16[1,1024,384]{2,1,0:T(8,128)(2,1)}, u32[]{:S(2)}) copy-start(bf16[1,1024,384]{2,1,0:T(8,128)(2,1)} %param.11) | copy-start | bytes 2359300
  99.7 6.9 %copy-start.6 = (bf16[4,96,1024]{2,1,0:T(8,128)(2,1)}, bf16[4,96,1024]{2,1,0:T(8,128)(2,1)S(1)}, u32[]{:S(2)}) copy-start(bf16[4,96,1024]{2,1,0:T(8,128)(2,1)S(1)} %all-to-all-done.3) | copy-start | bytes 2359300
  99.8 19.2 %all-to-all-start.2 = ((bf16[4,96,1024]{2,1,0:T(8,128)(2,1)}), bf16[4,96,1024]{2,1,0:T(8,128)(2,1)}, u32[]{:S(2)}, u32[]{:S(2)}) async-start(bf16[4,96,1024]{2,1,0:T(8,128)(2,1)} %bitcast.12), calls=%async_computation.2 | async-start | bytes 1572864 | tf_op jit(solution)/shard_map/all_to_all | solution.py:194
  106.6 28.9 %collective-permute-start.6 = (bf16[1024,384]{1,0:T(8,128)(2,1)S(1)}, bf16[1024,384]{1,0:T(8,128)(2,1)S(1)}, u32[]{:S(2)}, u32[]{:S(2)}) collective-permute-start(bf16[1024,384]{1,0:T(8,128)(2,1)S(1)} %bitcast.36), channel_id=1, source_target_pairs={{0,12},{4,0},{8,4},{12,8},{16,20},{20,24},{24,28},{28,16},{1,13},{... | collective-permute-start | bytes 2359304 | tf_op jit(solution)/shard_map/ppermute | solution.py:30
  108.5 27.0 %collective-permute-start.7 = (bf16[1024,384]{1,0:T(8,128)(2,1)S(1)}, bf16[1024,384]{1,0:T(8,128)(2,1)S(1)}, u32[]{:S(2)}, u32[]{:S(2)}) collective-permute-start(bf16[1024,384]{1,0:T(8,128)(2,1)S(1)} %bitcast.37), channel_id=1, source_target_pairs={{0,4},{4,8},{8,12},{12,0},{16,28},{20,16},{24,20},{28,24},{1,5},{5... | collective-permute-start | bytes 2359304 | tf_op jit(solution)/shard_map/ppermute | solution.py:30
  113.1 22.4 %collective-permute-start.8 = (bf16[1024,384]{1,0:T(8,128)(2,1)S(1)}, bf16[1024,384]{1,0:T(8,128)(2,1)S(1)}, u32[]{:S(2)}, u32[]{:S(2)}) collective-permute-start(bf16[1024,384]{1,0:T(8,128)(2,1)S(1)} %bitcast.38), channel_id=1, source_target_pairs={{0,8},{4,12},{8,0},{12,4},{1,9},{5,13},{9,1},{13,5},{2,10},{6,14},... | collective-permute-start | bytes 2359304 | tf_op jit(solution)/shard_map/ppermute | solution.py:21
  119.0 1.4 copy-start.7
  181.1 15.9 %all-to-all-start.5 = ((bf16[4,48,384]{2,1,0:T(8,128)(2,1)}), bf16[4,48,384]{2,1,0:T(8,128)(2,1)S(1)}, u32[]{:S(2)}, u32[]{:S(2)}) async-start(bf16[4,48,384]{2,1,0:T(8,128)(2,1)} %reduce_sum.52), calls=%async_computation.5 | async-start | bytes 294912 | tf_op jit(solution)/shard_map/all_to_all | solution.py:217

commit v10 on v9

--- a/solution.py
+++ b/solution.py
@@ -36,6 +36,11 @@
 
 def across(pair):
     return (turn(pair[0], False),)
+
+
+def across_halves(pair):
+    half = pair[0].shape[0] // 2
+    return turn(pair[0][:half], False), turn(pair[1][half:], True)
 
 
 def block_term(rows_ref, step, block):
@@ -81,10 +86,12 @@
     )(rows, *operands)
 
 
-def gate_kernel(rows_ref, after_ref, before_ref, own_ref, across_ref, out_ref, own, opposite, sems):
+def gate_kernel(rows_ref, after_ref, before_ref, own_ref, low_ref, high_ref, out_ref, own, opposite, sems):
+    half = low_ref.shape[0]
     copies = (
         pltpu.make_async_copy(own_ref, own, sems.at[0]),
-        pltpu.make_async_copy(across_ref, opposite, sems.at[1]),
+        pltpu.make_async_copy(low_ref, opposite.at[pl.ds(0, half), :], sems.at[1]),
+        pltpu.make_async_copy(high_ref, opposite.at[pl.ds(half, half), :], sems.at[2]),
     )
     for copy in copies:
         copy.start()
@@ -92,11 +99,12 @@
     copies[0].wait()
     total += block_term(rows_ref, 0, own[...])
     copies[1].wait()
+    copies[2].wait()
     total += block_term(rows_ref, 2, opposite[...])
     out_ref[...] = total.astype(out_ref.dtype)
 
 
-def project_gate(rows, own, pair, opposite):
+def project_gate(rows, own, pair, halves):
     sources, blocks, cap, depth = rows.shape
     width = own.shape[0]
     vmem = pl.BlockSpec(memory_space=pltpu.VMEM)
@@ -104,12 +112,12 @@
     return pl.pallas_call(
         gate_kernel,
         out_shape=jax.ShapeDtypeStruct((sources * cap, width), jnp.bfloat16),
-        in_specs=[vmem] * 3 + [anywhere] * 2,
+        in_specs=[vmem] * 3 + [anywhere] * 3,
         out_specs=vmem,
         scratch_shapes=[
             pltpu.VMEM((width, depth), jnp.bfloat16),
             pltpu.VMEM((width, depth), jnp.bfloat16),
-            pltpu.SemaphoreType.DMA((2,)),
+            pltpu.SemaphoreType.DMA((3,)),
         ],
         compiler_params=pltpu.CompilerParams(vmem_limit_bytes=GRANT),
         cost_estimate=pl.CostEstimate(
@@ -117,7 +125,7 @@
             bytes_accessed=2 * (rows.size + blocks * own.size + sources * cap * width),
             transcendentals=0,
         ),
-    )(rows, *pair, own, pltpu.with_memory_space_constraint(opposite[0], pltpu.HBM))
+    )(rows, *pair, own, *[pltpu.with_memory_space_constraint(half, pltpu.HBM) for half in halves])
 
 
 def expand_kernel(order_ref, hidden_ref, own_ref, after_ref, before_ref, across_ref, out_ref):
@@ -185,7 +193,7 @@
     gate_own = w_gate[0]
     width = gate_own.shape[0]
     gate_pair = beside(gate_own)
-    gate_across = across(gate_pair)
+    gate_across = across_halves(gate_pair)
     up_own, _ = lax.optimization_barrier((w_up[0], gate_pair))
     up_pair = beside(up_own)
     up_across = across(up_pair)

time: 199 us -> 199 us (level)
  waiting for transfers between devices: 51.4 us -> 42.6 us
  starting transfers between devices: 65.1 us -> 70 us
  blocking collectives: 57.5 us -> 61 us
    ppermute x8 -> x9, waiting for transfers between devices: 41.4 us -> 32.4 us  [turn(): return lax.ppermute(array, ('core', 'x'), pairs)]
    ppermute x8 -> x9, starting transfers between devices: 23.3 us -> 29.7 us  [turn(): return lax.ppermute(array, ('core', 'x'), pairs)]
    all_to_all x1, starting transfers between devices: 12.2 us -> 9.56 us  [on_device(): lax.all_to_all(back, LOCAL, split_axis=0, concat_axis=0, tiled=True)]
    all_gather x1, blocking collectives: 15 us -> 17.6 us  [on_device(): hidden_rows = lax.all_gather(hidden, 'zh', axis=0, tiled=True)]
    ppermute x1, waiting for transfers between devices: 0.01 us -> 2.1 us  [shift(): lax.ppermute(array, axis, [(i, (i + step) % size) for i in range(size)])]
  transfers between devices with their start and end apart: 14 -> 15, of which waited for: 8 -> 9; matrix products, arithmetic and copies ran while one was open for 2% -> 2% of each run, Pallas kernels for 4% -> 3%
where the time goes in v10:
time: 199 us; the launch traced here: 197 us
  starting transfers between devices  70 us (35%)
  blocking collectives  61 us (31%)
  waiting for transfers between devices  42.6 us (21%)
  Pallas kernels  11.6 us (6%)
  local copies, waits for them, and re-layouts  6.21 us (3%)
  other arithmetic  4.6 us (2%)
    all_to_all x1, blocking collectives, on_device(): lax.all_to_all(back.reshape(y_size * x_size, CAP, width_part), ('y', 'x')...  43.4 us
    ppermute x9, waiting for transfers between devices, turn(): return lax.ppermute(array, ('core', 'x'), pairs)  32.4 us
    ppermute x9, starting transfers between devices, turn(): return lax.ppermute(array, ('core', 'x'), pairs)  29.7 us
    all_gather x1, blocking collectives, on_device(): hidden_rows = lax.all_gather(hidden, 'zh', axis=0, tiled=True)  17.6 us
    all_to_all x2, starting transfers between devices, share(): parts = lax.all_to_all(term, 'zh', split_axis=0, concat_axis=0, tiled=True)  12.8 us
    all_to_all x1, starting transfers between devices, on_device(): lax.all_to_all(sent.reshape(EXPERTS * x_size, CAP, width_part), LOCAL + (...  10.2 us
    all_to_all x1, starting transfers between devices, on_device(): lax.all_to_all(back, LOCAL, split_axis=0, concat_axis=0, tiled=True)  9.56 us
    pallas_call x2, Pallas kernels, project(): pl.pallas_call(functools.partial(project_kernel, steps), out_shape=jax.Sh...  5.16 us
  transfers between devices with their start and end apart: 15, of which 9 were waited for; matrix products, arithmetic and copies ran while one was open for 2% of the time, Pallas kernels for 3%

profile of v10, /device:TPU:1, one launch (start us, length us, event | category | flops | bytes accessed | tf_op | source)
XLA Modules:
  0.0 197.4 jit_solution(13446202887040146673)
XLA Ops:
  2.2 10.2 %all-to-all-start = ((bf16[16,48,384]{2,1,0:T(8,128)(2,1)}), bf16[16,48,384]{2,1,0:T(8,128)(2,1)S(1)}, u32[]{:S(2)}, u32[]{:S(2)}) async-start(bf16[16,48,384]{2,1,0:T(8,128)(2,1)} %bitcast.5), calls=%async_computation | async-start | bytes 1179648 | tf_op jit(solution)/shard_map/all_to_all | solution.py:178
  12.4 3.3 %collective-permute-start = (bf16[1024,384]{1,0:T(8,128)(2,1)}, bf16[1024,384]{1,0:T(8,128)(2,1)S(1)}, u32[]{:S(2)}, u32[]{:S(2)}) collective-permute-start(bf16[1024,384]{1,0:T(8,128)(2,1)} %bitcast.11.own_ref), channel_id=1, source_target_pairs={{0,12},{4,0},{8,4},{12,8},{16,20},{20,24},{24,28},{28,16},{1,13},{... | collective-permute-start | bytes 2359304 | tf_op jit(solution)/shard_map/ppermute | solution.py:30
  15.7 3.2 %collective-permute-start.1 = (bf16[1024,384]{1,0:T(8,128)(2,1)}, bf16[1024,384]{1,0:T(8,128)(2,1)S(1)}, u32[]{:S(2)}, u32[]{:S(2)}) collective-permute-start(bf16[1024,384]{1,0:T(8,128)(2,1)} %bitcast.11.own_ref), channel_id=1, source_target_pairs={{0,4},{4,8},{8,12},{12,0},{16,28},{20,16},{24,20},{28,24},{1,5},{5... | collective-permute-start | bytes 2359304 | tf_op jit(solution)/shard_map/ppermute | solution.py:30
  19.0 4.3 %all-to-all-done = bf16[16,48,384]{2,1,0:T(8,128)(2,1)S(1)} async-done(((bf16[16,48,384]{2,1,0:T(8,128)(2,1)}), bf16[16,48,384]{2,1,0:T(8,128)(2,1)S(1)}, u32[]{:S(2)}, u32[]{:S(2)}) %all-to-all-start) | async-done | bytes 589856 | tf_op jit(solution)/shard_map/all_to_all | solution.py:178
  24.5 4.1 %all-to-all-start.1 = ((bf16[8,4,48,384]{3,2,1,0:T(8,128)(2,1)}), bf16[8,4,48,384]{3,2,1,0:T(8,128)(2,1)S(1)}, u32[]{:S(2)}, u32[]{:S(2)}) async-start(bf16[8,4,48,384]{3,2,1,0:T(8,128)(2,1)} %broadcast_in_dim.19), calls=%async_computation.1 | async-start | bytes 2359296 | tf_op jit(solution)/shard_map/all_to_all | solution.py:190
  28.7 9.7 %collective-permute-done.after_ref = bf16[1024,384]{1,0:T(8,128)(2,1)S(1)} collective-permute-done((bf16[1024,384]{1,0:T(8,128)(2,1)}, bf16[1024,384]{1,0:T(8,128)(2,1)S(1)}, u32[]{:S(2)}, u32[]{:S(2)}) %collective-permute-start) | collective-permute-done | bytes 786464 | tf_op jit(solution)/shard_map/ppermute | solution.py:30
  38.4 3.1 %collective-permute-start.4 = (bf16[1024,384]{1,0:T(8,128)(2,1)}, bf16[1024,384]{1,0:T(8,128)(2,1)}, u32[]{:S(2)}, u32[]{:S(2)}) collective-permute-start(bf16[1024,384]{1,0:T(8,128)(2,1)} %bitcast.30), channel_id=1, source_target_pairs={{0,12},{4,0},{8,4},{12,8},{16,20},{20,24},{24,28},{28,16},{1,13},{... | collective-permute-start | bytes 2359304 | tf_op jit(solution)/shard_map/ppermute | solution.py:30
  41.5 3.4 %collective-permute-start.5 = (bf16[1024,384]{1,0:T(8,128)(2,1)}, bf16[1024,384]{1,0:T(8,128)(2,1)S(1)}, u32[]{:S(2)}, u32[]{:S(2)}) collective-permute-start(bf16[1024,384]{1,0:T(8,128)(2,1)} %bitcast.31), channel_id=1, source_target_pairs={{0,4},{4,8},{8,12},{12,0},{16,28},{20,16},{24,20},{28,24},{1,5},{5... | collective-permute-start | bytes 2359304 | tf_op jit(solution)/shard_map/ppermute | solution.py:30
  44.9 11.3 %collective-permute-done.4.refs_1_ = bf16[1024,384]{1,0:T(8,128)(2,1)} collective-permute-done((bf16[1024,384]{1,0:T(8,128)(2,1)}, bf16[1024,384]{1,0:T(8,128)(2,1)}, u32[]{:S(2)}, u32[]{:S(2)}) %collective-permute-start.4) | collective-permute-done | bytes 786464 | tf_op jit(solution)/shard_map/ppermute | solution.py:30
  56.2 2.5 %collective-permute-start.6 = (bf16[1024,384]{1,0:T(8,128)(2,1)}, bf16[1024,384]{1,0:T(8,128)(2,1)}, u32[]{:S(2)}, u32[]{:S(2)}) collective-permute-start(bf16[1024,384]{1,0:T(8,128)(2,1)} %collective-permute-done.4.refs_1_), channel_id=1, source_target_pairs={{0,12},{4,0},{8,4},{12,8},{16,20},{20,24},{24,28},{28,16},{1,13},{... | collective-permute-start | bytes 2359304 | tf_op jit(solution)/shard_map/ppermute | solution.py:30
  58.7 3.1 %collective-permute-done.5.refs_2_ = bf16[1024,384]{1,0:T(8,128)(2,1)S(1)} collective-permute-done((bf16[1024,384]{1,0:T(8,128)(2,1)}, bf16[1024,384]{1,0:T(8,128)(2,1)S(1)}, u32[]{:S(2)}, u32[]{:S(2)}) %collective-permute-start.5) | collective-permute-done | bytes 786464 | tf_op jit(solution)/shard_map/ppermute | solution.py:30
  65.0 2.5 %shard_map.65.refs_0_ = f32[384,1024]{1,0:T(8,128)S(1)} custom-call(bf16[8,4,48,384]{3,2,1,0:T(8,128)(2,1)S(1)} %all-to-all-done.1.rows_ref, bf16[1024,384]{1,0:T(8,128)(2,1)S(1)} %bitcast.32, bf16[1024,384]{1,0:T(8,128)(2,1)} %collective-permute-done.4.refs_1_, bf16[1024,384]{1,0:T(8,128)(2,1)S(1)} %copy-done.3), custom_call_target="tpu_custom_call" | custom-call | flops 905969664 | bytes 4325376 | tf_op jit(solution)/shard_map/pallas_call | solution.py:75
  67.6 3.1 %collective-permute-done.6.refs_1_ = bf16[1024,384]{1,0:T(8,128)(2,1)} collective-permute-done((bf16[1024,384]{1,0:T(8,128)(2,1)}, bf16[1024,384]{1,0:T(8,128)(2,1)}, u32[]{:S(2)}, u32[]{:S(2)}) %collective-permute-start.6) | collective-permute-done | bytes 786464 | tf_op jit(solution)/shard_map/ppermute | solution.py:30
  70.7 2.6 %shard_map.66 = bf16[384,1024]{1,0:T(8,128)(2,1)} custom-call(bf16[8,4,48,384]{3,2,1,0:T(8,128)(2,1)S(1)} %all-to-all-done.1.rows_ref, f32[384,1024]{1,0:T(8,128)S(1)} %shard_map.65.refs_0_, bf16[1024,384]{1,0:T(8,128)(2,1)} %collective-permute-done.6.refs_1_), custom_call_target="tpu_custom_call" | custom-call | flops 603979776 | bytes 3538944 | tf_op jit(solution)/shard_map/pallas_call | solution.py:75
  73.3 6.5 %all-to-all-start.3 = ((bf16[4,96,1024]{2,1,0:T(8,128)(2,1)}), bf16[4,96,1024]{2,1,0:T(8,128)(2,1)}, u32[]{:S(2)}, u32[]{:S(2)}) async-start(bf16[4,96,1024]{2,1,0:T(8,128)(2,1)} %bitcast.15), calls=%async_computation.3 | async-start | bytes 1572864 | tf_op jit(solution)/shard_map/all_to_all | solution.py:202
  79.8 1.9 collective-permute-start.2
  81.8 4.6 %collective-permute-start.3 = (bf16[512,384]{1,0:T(8,128)(2,1)S(1)}, bf16[512,384]{1,0:T(8,128)(2,1)S(1)}, u32[]{:S(2)}, u32[]{:S(2)}) collective-permute-start(bf16[512,384]{1,0:T(8,128)(2,1)S(1)} %slice.9), channel_id=1, source_target_pairs={{0,4},{4,8},{8,12},{12,0},{16,28},{20,16},{24,20},{28,24},{1,5},{5... | collective-permute-start | bytes 1179656 | tf_op jit(solution)/shard_map/ppermute | solution.py:30
  86.4 3.4 %collective-permute-done.2.low_ref = bf16[512,384]{1,0:T(8,128)(2,1)S(1)} collective-permute-done((bf16[512,384]{1,0:T(8,128)(2,1)S(1)}, bf16[512,384]{1,0:T(8,128)(2,1)S(1)}, u32[]{:S(2)}, u32[]{:S(2)}) %collective-permute-start.2) | collective-permute-done | bytes 393248 | tf_op jit(solution)/shard_map/ppermute | solution.py:30
  89.8 1.8 collective-permute-done.3.high_ref
  92.3 3.5 %shard_map.64 = bf16[384,1024]{1,0:T(8,128)(2,1)} custom-call(bf16[8,4,48,384]{3,2,1,0:T(8,128)(2,1)S(1)} %all-to-all-done.1.rows_ref, bf16[1024,384]{1,0:T(8,128)(2,1)S(1)} %collective-permute-done.after_ref, bf16[1024,384]{1,0:T(8,128)(2,1)S(1)} %collective-permute-done.1.before_ref, bf16[1024,384]{1,0:T(8,128)(2,1)} %bitcast.11.own_ref, ...), custom_call_target="tpu_custom_call" | custom-call | flops 1207959552 | bytes 5111808 | tf_op jit(solution)/shard_map/pallas_call | solution.py:112
  95.9 6.3 %all-to-all-start.2 = ((bf16[4,96,1024]{2,1,0:T(8,128)(2,1)}), bf16[4,96,1024]{2,1,0:T(8,128)(2,1)}, u32[]{:S(2)}, u32[]{:S(2)}) async-start(bf16[4,96,1024]{2,1,0:T(8,128)(2,1)} %bitcast.12), calls=%async_computation.2 | async-start | bytes 1572864 | tf_op jit(solution)/shard_map/all_to_all | solution.py:202
  102.2 5.3 %collective-permute-start.7 = (bf16[1024,384]{1,0:T(8,128)(2,1)S(1)}, bf16[1024,384]{1,0:T(8,128)(2,1)S(1)}, u32[]{:S(2)}, u32[]{:S(2)}) collective-permute-start(bf16[1024,384]{1,0:T(8,128)(2,1)S(1)} %bitcast.33), channel_id=1, source_target_pairs={{0,12},{4,0},{8,4},{12,8},{16,20},{20,24},{24,28},{28,16},{1,13},{... | collective-permute-start | bytes 2359304 | tf_op jit(solution)/shard_map/ppermute | solution.py:30
  107.5 2.4 %collective-permute-start.8 = (bf16[1024,384]{1,0:T(8,128)(2,1)S(1)}, bf16[1024,384]{1,0:T(8,128)(2,1)S(1)}, u32[]{:S(2)}, u32[]{:S(2)}) collective-permute-start(bf16[1024,384]{1,0:T(8,128)(2,1)S(1)} %bitcast.34), channel_id=1, source_target_pairs={{0,4},{4,8},{8,12},{12,0},{16,28},{20,16},{24,20},{28,24},{1,5},{5... | collective-permute-start | bytes 2359304 | tf_op jit(solution)/shard_map/ppermute | solution.py:30
  109.9 3.7 %collective-permute-start.9 = (bf16[1024,384]{1,0:T(8,128)(2,1)S(1)}, bf16[1024,384]{1,0:T(8,128)(2,1)}, u32[]{:S(2)}, u32[]{:S(2)}) collective-permute-start(bf16[1024,384]{1,0:T(8,128)(2,1)S(1)} %bitcast.35), channel_id=1, source_target_pairs={{0,8},{4,12},{8,0},{12,4},{1,9},{5,13},{9,1},{13,5},{2,10},{6,14},... | collective-permute-start | bytes 2359304 | tf_op jit(solution)/shard_map/ppermute | solution.py:21
  113.6 1.3 convert_reduce_fusion
  114.9 1.3 convert_reduce_fusion.1
  116.3 17.6 %all_gather.3.hidden_ref = bf16[384,1024]{1,0:T(8,128)(2,1)S(1)} all-gather(bf16[96,1024]{1,0:T(8,128)(2,1)S(1)} %multiply_convert_fusion), channel_id=1, replica_groups=mesh['y'=8,'zl'=2,'core'=2,'x'=4,'zh'=4] {'zh'}, dimensions={0}, use_global_device_ids=true | all-gather | bytes 983040 | tf_op jit(solution)/shard_map/all_gather | solution.py:215
  134.0 2.1 %collective-permute-done.9.across_ref = bf16[1024,384]{1,0:T(8,128)(2,1)} collective-permute-done((bf16[1024,384]{1,0:T(8,128)(2,1)S(1)}, bf16[1024,384]{1,0:T(8,128)(2,1)}, u32[]{:S(2)}, u32[]{:S(2)}) %collective-permute-start.9) | collective-permute-done | bytes 786464 | tf_op jit(solution)/shard_map/ppermute | solution.py:21
  136.1 2.9 %shard_map.67 = bf16[8,4,48,384]{3,2,1,0:T(8,128)(2,1)S(1)} custom-call(s32[4]{0:T(128)S(1)} %pad_add_fusion.order_ref, bf16[384,1024]{1,0:T(8,128)(2,1)S(1)} %all_gather.3.hidden_ref, bf16[1024,384]{1,0:T(8,128)(2,1)S(1)} %bitcast.36, bf16[1024,384]{1,0:T(8,128)(2,1)S(1)} %collective-permute-done.7.after_ref, ...), custom_call_target="tpu_custom_call" | custom-call | flops 1207959552 | bytes 5111808 | tf_op jit(solution)/shard_map/pallas_call | solution.py:145
  139.0 43.4 %all_to_all.38 = bf16[32,48,384]{2,1,0:T(8,128)(2,1)S(1)} all-to-all(bf16[32,48,384]{2,1,0:T(8,128)(2,1)S(1)} %bitcast.29), channel_id=1, replica_groups=mesh['y'=8,'zl'=2,'core'=2,'x'=4,'zh'=4] {'y','x'}, dimensions={0} | all-to-all | bytes 2359296 | tf_op jit(solution)/shard_map/all_to_all | solution.py:217
  183.2 9.6 %all-to-all-start.5 = ((bf16[4,48,384]{2,1,0:T(8,128)(2,1)}), bf16[4,48,384]{2,1,0:T(8,128)(2,1)S(1)}, u32[]{:S(2)}, u32[]{:S(2)}) async-start(bf16[4,48,384]{2,1,0:T(8,128)(2,1)} %reduce_sum.52), calls=%async_computation.5 | async-start | bytes 294912 | tf_op jit(solution)/shard_map/all_to_all | solution.py:225
  192.8 3.7 %all-to-all-done.5 = bf16[4,48,384]{2,1,0:T(8,128)(2,1)S(1)} async-done(((bf16[4,48,384]{2,1,0:T(8,128)(2,1)}), bf16[4,48,384]{2,1,0:T(8,128)(2,1)S(1)}, u32[]{:S(2)}, u32[]{:S(2)}) %all-to-all-start.5) | async-done | bytes 147488 | tf_op jit(solution)/shard_map/all_to_all | solution.py:225
  (38 shorter events, 9.4 us)
Async XLA Ops:
  0.0 1.1 copy-start
  2.2 21.1 %all-to-all-start = ((bf16[16,48,384]{2,1,0:T(8,128)(2,1)}), bf16[16,48,384]{2,1,0:T(8,128)(2,1)S(1)}, u32[]{:S(2)}, u32[]{:S(2)}) async-start(bf16[16,48,384]{2,1,0:T(8,128)(2,1)} %bitcast.5), calls=%async_computation | async-start | bytes 1179648 | tf_op jit(solution)/shard_map/all_to_all | solution.py:178
  12.4 25.9 %collective-permute-start = (bf16[1024,384]{1,0:T(8,128)(2,1)}, bf16[1024,384]{1,0:T(8,128)(2,1)S(1)}, u32[]{:S(2)}, u32[]{:S(2)}) collective-permute-start(bf16[1024,384]{1,0:T(8,128)(2,1)} %bitcast.11.own_ref), channel_id=1, source_target_pairs={{0,12},{4,0},{8,4},{12,8},{16,20},{20,24},{24,28},{28,16},{1,13},{... | collective-permute-start | bytes 2359304 | tf_op jit(solution)/shard_map/ppermute | solution.py:30
  15.7 22.7 %collective-permute-start.1 = (bf16[1024,384]{1,0:T(8,128)(2,1)}, bf16[1024,384]{1,0:T(8,128)(2,1)S(1)}, u32[]{:S(2)}, u32[]{:S(2)}) collective-permute-start(bf16[1024,384]{1,0:T(8,128)(2,1)} %bitcast.11.own_ref), channel_id=1, source_target_pairs={{0,4},{4,8},{8,12},{12,0},{16,28},{20,16},{24,20},{28,24},{1,5},{5... | collective-permute-start | bytes 2359304 | tf_op jit(solution)/shard_map/ppermute | solution.py:30
  24.5 38.2 %all-to-all-start.1 = ((bf16[8,4,48,384]{3,2,1,0:T(8,128)(2,1)}), bf16[8,4,48,384]{3,2,1,0:T(8,128)(2,1)S(1)}, u32[]{:S(2)}, u32[]{:S(2)}) async-start(bf16[8,4,48,384]{3,2,1,0:T(8,128)(2,1)} %broadcast_in_dim.19), calls=%async_computation.1 | async-start | bytes 2359296 | tf_op jit(solution)/shard_map/all_to_all | solution.py:190
  38.4 17.8 %collective-permute-start.4 = (bf16[1024,384]{1,0:T(8,128)(2,1)}, bf16[1024,384]{1,0:T(8,128)(2,1)}, u32[]{:S(2)}, u32[]{:S(2)}) collective-permute-start(bf16[1024,384]{1,0:T(8,128)(2,1)} %bitcast.30), channel_id=1, source_target_pairs={{0,12},{4,0},{8,4},{12,8},{16,20},{20,24},{24,28},{28,16},{1,13},{... | collective-permute-start | bytes 2359304 | tf_op jit(solution)/shard_map/ppermute | solution.py:30
  41.5 20.3 %collective-permute-start.5 = (bf16[1024,384]{1,0:T(8,128)(2,1)}, bf16[1024,384]{1,0:T(8,128)(2,1)S(1)}, u32[]{:S(2)}, u32[]{:S(2)}) collective-permute-start(bf16[1024,384]{1,0:T(8,128)(2,1)} %bitcast.31), channel_id=1, source_target_pairs={{0,4},{4,8},{8,12},{12,0},{16,28},{20,16},{24,20},{28,24},{1,5},{5... | collective-permute-start | bytes 2359304 | tf_op jit(solution)/shard_map/ppermute | solution.py:30
  56.2 14.5 %collective-permute-start.6 = (bf16[1024,384]{1,0:T(8,128)(2,1)}, bf16[1024,384]{1,0:T(8,128)(2,1)}, u32[]{:S(2)}, u32[]{:S(2)}) collective-permute-start(bf16[1024,384]{1,0:T(8,128)(2,1)} %collective-permute-done.4.refs_1_), channel_id=1, source_target_pairs={{0,12},{4,0},{8,4},{12,8},{16,20},{20,24},{24,28},{28,16},{1,13},{... | collective-permute-start | bytes 2359304 | tf_op jit(solution)/shard_map/ppermute | solution.py:30
  61.9 0.9 copy-start.2
  62.8 1.1 copy-start.1
  63.9 1.1 copy-start.3
  73.3 22.5 %all-to-all-start.3 = ((bf16[4,96,1024]{2,1,0:T(8,128)(2,1)}), bf16[4,96,1024]{2,1,0:T(8,128)(2,1)}, u32[]{:S(2)}, u32[]{:S(2)}) async-start(bf16[4,96,1024]{2,1,0:T(8,128)(2,1)} %bitcast.15), calls=%async_computation.3 | async-start | bytes 1572864 | tf_op jit(solution)/shard_map/all_to_all | solution.py:202
  79.8 10.0 %collective-permute-start.2 = (bf16[512,384]{1,0:T(8,128)(2,1)S(1)}, bf16[512,384]{1,0:T(8,128)(2,1)S(1)}, u32[]{:S(2)}, u32[]{:S(2)}) collective-permute-start(bf16[512,384]{1,0:T(8,128)(2,1)S(1)} %slice.8), channel_id=1, source_target_pairs={{0,12},{4,0},{8,4},{12,8},{16,20},{20,24},{24,28},{28,16},{1,13},{... | collective-permute-start | bytes 1179656 | tf_op jit(solution)/shard_map/ppermute | solution.py:30
  81.8 9.8 %collective-permute-start.3 = (bf16[512,384]{1,0:T(8,128)(2,1)S(1)}, bf16[512,384]{1,0:T(8,128)(2,1)S(1)}, u32[]{:S(2)}, u32[]{:S(2)}) collective-permute-start(bf16[512,384]{1,0:T(8,128)(2,1)S(1)} %slice.9), channel_id=1, source_target_pairs={{0,4},{4,8},{8,12},{12,0},{16,28},{20,16},{24,20},{28,24},{1,5},{5... | collective-permute-start | bytes 1179656 | tf_op jit(solution)/shard_map/ppermute | solution.py:30
  89.8 1.8 copy-start.5
  91.6 0.8 copy-start.6
  95.8 6.4 %copy-start.4 = (bf16[1,1024,384]{2,1,0:T(8,128)(2,1)S(1)}, bf16[1,1024,384]{2,1,0:T(8,128)(2,1)}, u32[]{:S(2)}) copy-start(bf16[1,1024,384]{2,1,0:T(8,128)(2,1)} %param.11) | copy-start | bytes 2359300
  95.9 19.1 %all-to-all-start.2 = ((bf16[4,96,1024]{2,1,0:T(8,128)(2,1)}), bf16[4,96,1024]{2,1,0:T(8,128)(2,1)}, u32[]{:S(2)}, u32[]{:S(2)}) async-start(bf16[4,96,1024]{2,1,0:T(8,128)(2,1)} %bitcast.12), calls=%async_computation.2 | async-start | bytes 1572864 | tf_op jit(solution)/shard_map/all_to_all | solution.py:202
  102.2 31.8 %collective-permute-start.7 = (bf16[1024,384]{1,0:T(8,128)(2,1)S(1)}, bf16[1024,384]{1,0:T(8,128)(2,1)S(1)}, u32[]{:S(2)}, u32[]{:S(2)}) collective-permute-start(bf16[1024,384]{1,0:T(8,128)(2,1)S(1)} %bitcast.33), channel_id=1, source_target_pairs={{0,12},{4,0},{8,4},{12,8},{16,20},{20,24},{24,28},{28,16},{1,13},{... | collective-permute-start | bytes 2359304 | tf_op jit(solution)/shard_map/ppermute | solution.py:30
  107.5 26.5 %collective-permute-start.8 = (bf16[1024,384]{1,0:T(8,128)(2,1)S(1)}, bf16[1024,384]{1,0:T(8,128)(2,1)S(1)}, u32[]{:S(2)}, u32[]{:S(2)}) collective-permute-start(bf16[1024,384]{1,0:T(8,128)(2,1)S(1)} %bitcast.34), channel_id=1, source_target_pairs={{0,4},{4,8},{8,12},{12,0},{16,28},{20,16},{24,20},{28,24},{1,5},{5... | collective-permute-start | bytes 2359304 | tf_op jit(solution)/shard_map/ppermute | solution.py:30
  109.9 26.2 %collective-permute-start.9 = (bf16[1024,384]{1,0:T(8,128)(2,1)S(1)}, bf16[1024,384]{1,0:T(8,128)(2,1)}, u32[]{:S(2)}, u32[]{:S(2)}) collective-permute-start(bf16[1024,384]{1,0:T(8,128)(2,1)S(1)} %bitcast.35), channel_id=1, source_target_pairs={{0,8},{4,12},{8,0},{12,4},{1,9},{5,13},{9,1},{13,5},{2,10},{6,14},... | collective-permute-start | bytes 2359304 | tf_op jit(solution)/shard_map/ppermute | solution.py:21
  183.2 13.3 %all-to-all-start.5 = ((bf16[4,48,384]{2,1,0:T(8,128)(2,1)}), bf16[4,48,384]{2,1,0:T(8,128)(2,1)S(1)}, u32[]{:S(2)}, u32[]{:S(2)}) async-start(bf16[4,48,384]{2,1,0:T(8,128)(2,1)} %reduce_sum.52), calls=%async_computation.5 | async-start | bytes 294912 | tf_op jit(solution)/shard_map/all_to_all | solution.py:225
